TPU v7x, 512 devices: a whole 4x4x16 slice. The times are simulated.
512 devices in a mesh: arm: 4 (over z_lo), gx: 8 (over x, core), gy: 16 (over y, z_hi).
Axes of the slice: x: 4, y: 4, z: 16 (z_hi: 4, z_lo: 4; z = z_hi * 4 + z_lo), core: 2. Of those that a mesh axis runs over, the one named last changes fastest.
Arguments:
- fields: float32 [4, 256, 256, 256], P('arm', 'gx', 'gy'), may hold values from -1.2 to 2
- flory_chi: float32 [4, 4], replicated, may hold values from 0 to 2
Outputs:
- field_out: float32 [4, 256, 256, 256], P('arm', 'gx', 'gy')
- volume_frac: float32 [4, 256, 256, 256], P('arm', 'gx', 'gy')
All inputs are finite; a program needn't handle non-finite values.
Results may differ from a plain program's by a relative error of at most 0.0001.
Values sent between devices are 32-bit elements; how exact they have to be, the bound alone decides.
No kernel may reach another device: no remote copies, remote signals or barrier semaphores. Data moves between devices by JAX's collectives and lax.ppermute only.
A program may use at most 64 MiB of HBM per device.

v0:
```python
import jax
import jax.numpy as jnp
from jax import lax
from jax.sharding import PartitionSpec as P

SPECIES = 4
STEPS = 8


diffusion = 0.14
contour_step = 0.05
mixing = 0.5
compress = 1.0


def padded_2(array, sides, width):
    for axis, dim in sides:
        size, length = (lax.axis_size(axis), array.shape[dim])
        up = [(i, (i + 1) % size) for i in range(size)]
        down = [(j, i) for i, j in up]
        last = lax.slice_in_dim(array, length - width, length, axis=dim)
        initial = lax.slice_in_dim(array, 0, width, axis=dim)
        before = lax.ppermute(last, axis, up)
        after = lax.ppermute(initial, axis, down)
        array = jnp.concatenate([before, array, after], axis=dim)
    return array


def update(padded, field):
    centre = padded[1:-1, 1:-1]
    spread = padded[2:, 1:-1] + padded[:-2, 1:-1]
    spread = spread + padded[1:-1, 2:] + padded[1:-1, :-2]
    spread = spread + jnp.roll(centre, 1, 2) + jnp.roll(centre, -1, 2)
    return centre + diffusion * (spread - 6.0 * centre) - contour_step * field * centre


def local(fields, flory_chi):
    field_here = fields[0]
    arm_index = lax.axis_index("arm")
    size_x = field_here.shape[0]
    size_y = field_here.shape[1]
    cell_count = size_x * size_y * field_here.shape[2] * lax.axis_size("gx") * lax.axis_size("gy")

    def single(state):
        padded = padded_2(state, (("gx", 0), ("gy", 1)), 1)
        return update(padded, field_here)

    def march_all(state):
        states = [state]
        for step_id in range(STEPS):
            state = single(state)
            states.append(state)
        return states

    inner = march_all(jnp.ones(field_here.shape, jnp.float32))
    finish = inner[STEPS]
    gathered = lax.all_gather(finish[None], "arm", axis=0, tiled=True)
    junction = jnp.ones(field_here.shape, jnp.float32)
    for member in range(SPECIES):
        junction = junction * jnp.where(arm_index == member, 1.0, gathered[member])
    whole_sum = jnp.sum(junction * finish)
    outer = march_all(junction)
    density = 0.5 * inner[STEPS] * outer[0]
    for step_id in range(1, STEPS + 1):
        weight = 0.5 if step_id == STEPS else 1.0
        density = density + weight * inner[STEPS - step_id] * outer[step_id]
    chi_row = jnp.sum(
        jnp.where((jnp.arange(SPECIES) == arm_index)[:, None], flory_chi, 0.0), axis=0
    )
    contour_total = SPECIES * STEPS
    partition = lax.psum(whole_sum, ("gx", "gy"))
    mean_part = partition / cell_count
    volume = density / (contour_total * mean_part)
    all_phi = lax.all_gather(volume[None], "arm", axis=0, tiled=True)
    mixture = chi_row[0] * all_phi[0]
    for member in range(1, SPECIES):
        mixture = mixture + chi_row[member] * all_phi[member]
    pressure = compress * (jnp.sum(all_phi, axis=0) - 1.0)
    field_new = field_here + mixing * (mixture + pressure - field_here)
    field_total = lax.psum(jnp.sum(field_new), ("gx", "gy"))
    field_out = field_new - field_total / cell_count
    return (field_out[None], volume[None])


def solution(mesh):
    placed = (P("arm", "gx", "gy", None), P())
    return jax.shard_map(
        local,
        mesh=mesh,
        in_specs=placed,
        out_specs=(P("arm", "gx", "gy", None), P("arm", "gx", "gy", None)),
        check_vma=False,
    )
```

profile of v0, /device:TPU:32, one launch (start us, length us, event | category | flops | bytes accessed | tf_op | source)
XLA Modules:
  0.0 1278.3 jit_solution(7828308266407531379)
XLA Ops:
  13.9 9.1 collective-permute-start.3
  23.0 7.1 collective-permute-start.2
  30.2 3.1 collective-permute-done.2
  36.1 2.9 collective-permute-done.5
  39.1 7.7 collective-permute-start.7
  46.8 4.1 collective-permute-start.6
  52.0 4.5 collective-permute-done.6
  58.5 2.9 collective-permute-done.9
  61.5 4.8 collective-permute-start.11
  66.3 7.0 collective-permute-start.10
  83.7 9.4 collective-permute-start.14
  100.0 4.8 collective-permute-start.19
  104.8 7.7 collective-permute-start.18
  116.6 2.9 collective-permute-done.21
  119.6 7.3 collective-permute-start.23
  126.9 5.0 collective-permute-start.22
  132.1 4.7 collective-permute-done.22
  138.7 2.9 collective-permute-done.25
  141.7 6.5 collective-permute-start.27
  148.2 5.3 collective-permute-start.26
  153.7 4.4 collective-permute-done.26
  160.0 2.9 collective-permute-done.29
  163.0 3.4 collective-permute-start.31
  166.5 8.4 collective-permute-start.30
  178.2 50.6 %all-gather.5.cloned.1.call-done = f32[128,16,256]{2,1,0:T(8,128)} async-done(((f32[32,16,256]{2,1,0:T(8,128)}), f32[128,16,256]{2,1,0:T(8,128)}) %all-gather.5.cloned.1.call-update) | async-done | bytes 2097168 | tf_op jit(solution)/shard_map/all_gather | solution.py:57
  238.4 7.6 collective-permute-start.35
  246.0 4.2 collective-permute-start.34
  251.1 404.9 %psum.14 = f32[]{:T(128)} all-reduce(f32[]{:T(128)} %get-tuple-element.4), channel_id=1, replica_groups=mesh['arm'=4,'gx'=8,'gy'=16] {'gx','gy'}, use_global_device_ids=true, to_apply=%region_2.3 | all-reduce | flops 1 | bytes 8 | tf_op jit(solution)/shard_map/psum | solution.py:71
  656.7 3.0 fusion.85
  661.2 2.9 collective-permute-done.37
  664.2 4.4 collective-permute-start.39
  668.5 7.5 collective-permute-start.38
  680.5 2.9 collective-permute-done.41
  685.5 9.9 collective-permute-start.42
  699.0 2.9 collective-permute-done.45
  704.4 10.0 collective-permute-start.46
  717.8 2.9 collective-permute-done.49
  723.0 9.9 collective-permute-start.50
  736.5 2.9 collective-permute-done.53
  742.4 9.3 collective-permute-start.54
  755.2 2.9 collective-permute-done.57
  760.2 10.2 collective-permute-start.58
  774.0 2.9 collective-permute-done.61
  779.0 10.2 collective-permute-start.62
  790.8 2.9 fusion.22
  794.6 58.4 %all-gather.7.cloned.1.call-done = f32[128,16,256]{2,1,0:T(8,128)} async-done(((f32[32,16,256]{2,1,0:T(8,128)}), f32[128,16,256]{2,1,0:T(8,128)}) %all-gather.7.cloned.1.call-update) | async-done | bytes 2097168 | tf_op jit(solution)/shard_map/all_gather | solution.py:74
  855.7 4.4 fusion.158
  860.2 409.7 %psum.15 = f32[]{:T(128)} all-reduce(f32[]{:T(128)} %get-tuple-element.2), channel_id=1, replica_groups=mesh['arm'=4,'gx'=8,'gy'=16] {'gx','gy'}, use_global_device_ids=true, to_apply=%region_5.6 | all-reduce | flops 1 | bytes 8 | tf_op jit(solution)/shard_map/psum | solution.py:80
  (196 shorter events, 95.0 us)
Async XLA Ops:
  7.2 221.6 %all-gather.5.cloned.1.call-start = ((), (), s32[]{:S(2)}) async-start(), calls=%async_computation | async-start | bytes 2621440 | tf_op jit(solution)/shard_map/all_gather | solution.py:57
  9.4 4.4 collective-permute-start.1
  13.9 16.2 %collective-permute-start.3 = (f32[34,1,256]{2,1,0:T(1,128)S(1)}, f32[34,1,256]{2,1,0:T(1,128)S(1)}, u32[]{:S(2)}, u32[]{:S(2)}) collective-permute-start(f32[34,1,256]{2,1,0:T(1,128)S(1)} %get-tuple-element.37), channel_id=1, source_target_pairs={{0,1},{1,2},{2,3},{3,4},{4,5},{5,6},{6,7},{7,8},{8,9},{9,10},{10,1... | collective-permute-start | bytes 104456 | tf_op jit(solution)/shard_map/ppermute | solution.py:23
  23.0 10.2 collective-permute-start.2
  34.6 4.4 collective-permute-start.5
  39.1 13.0 %collective-permute-start.7 = (f32[34,1,256]{2,1,0:T(1,128)S(1)}, f32[34,1,256]{2,1,0:T(1,128)S(1)}, u32[]{:S(2)}, u32[]{:S(2)}) collective-permute-start(f32[34,1,256]{2,1,0:T(1,128)S(1)} %get-tuple-element.35), channel_id=1, source_target_pairs={{0,1},{1,2},{2,3},{3,4},{4,5},{5,6},{6,7},{7,8},{8,9},{9,10},{10,1... | collective-permute-start | bytes 104456 | tf_op jit(solution)/shard_map/ppermute | solution.py:23
  46.8 9.7 collective-permute-start.6
  57.0 4.4 collective-permute-start.9
  61.5 12.0 collective-permute-start.11
  66.3 9.7 collective-permute-start.10
  76.8 4.4 collective-permute-start.13
  81.2 12.3 collective-permute-start.15
  83.7 11.0 collective-permute-start.14
  100.0 12.6 collective-permute-start.19
  104.8 9.9 collective-permute-start.18
  115.2 4.4 collective-permute-start.21
  119.6 12.4 collective-permute-start.23
  126.9 9.8 collective-permute-start.22
  137.2 4.4 collective-permute-start.25
  141.7 12.0 collective-permute-start.27
  148.2 9.9 collective-permute-start.26
  158.6 4.4 collective-permute-start.29
  163.0 12.0 collective-permute-start.31
  166.5 10.3 collective-permute-start.30
  178.1 674.8 %all-gather.7.cloned.1.call-start = ((), (), s32[]{:S(2)}) async-start(), calls=%async_computation.1 | async-start | bytes 2621440 | tf_op jit(solution)/shard_map/all_gather | solution.py:74
  238.4 418.3 %collective-permute-start.35 = (f32[34,1,256]{2,1,0:T(1,128)}, f32[34,1,256]{2,1,0:T(1,128)}, u32[]{:S(2)}, u32[]{:S(2)}) collective-permute-start(f32[34,1,256]{2,1,0:T(1,128)} %get-tuple-element.21), channel_id=1, source_target_pairs={{0,1},{1,2},{2,3},{3,4},{4,5},{5,6},{6,7},{7,8},{8,9},{9,10},{10,1... | collective-permute-start | bytes 104456 | tf_op jit(solution)/shard_map/ppermute | solution.py:23
  246.0 410.6 %collective-permute-start.34 = (f32[34,1,256]{2,1,0:T(1,128)}, f32[34,1,256]{2,1,0:T(1,128)}, u32[]{:S(2)}, u32[]{:S(2)}) collective-permute-start(f32[34,1,256]{2,1,0:T(1,128)} %get-tuple-element.20), channel_id=1, source_target_pairs={{1,0},{2,1},{3,2},{4,3},{5,4},{6,5},{7,6},{8,7},{9,8},{10,9},{11,1... | collective-permute-start | bytes 104456 | tf_op jit(solution)/shard_map/ppermute | solution.py:24
  659.7 4.4 collective-permute-start.37
  664.2 12.0 collective-permute-start.39
  668.5 10.0 collective-permute-start.38
  679.1 4.4 collective-permute-start.41
  683.6 12.0 collective-permute-start.43
  685.5 11.5 collective-permute-start.42
  697.5 4.4 collective-permute-start.45
  702.0 12.5 collective-permute-start.47
  704.4 11.4 collective-permute-start.46
  716.3 4.4 collective-permute-start.49
  720.8 12.3 collective-permute-start.51
  723.0 11.5 collective-permute-start.50
  735.1 4.4 collective-permute-start.53
  739.5 12.3 collective-permute-start.55
  742.4 10.9 collective-permute-start.54
  753.8 4.4 collective-permute-start.57
  758.2 12.3 collective-permute-start.59
  760.2 11.8 collective-permute-start.58
  772.6 4.4 collective-permute-start.61
  777.0 12.3 collective-permute-start.63
  779.0 11.8 collective-permute-start.62
  (28 other events, 194.3 us)
Sparse Core Ops, SparseCore 0:
  178.2 50.4 all-gather.4
  793.9 58.9 all-gather.6
where the time goes:
time: 1280 us
  blocking collectives  815 us (64%)
  starting transfers between devices  208 us (16%)
  waiting for transfers between devices  205 us (16%)
  other arithmetic  26.6 us (2%)
  between operations  16.2 us (1%)
    psum x1, blocking collectives, local(): field_total = lax.psum(jnp.sum(field_new), ('gx', 'gy'))  410 us
    psum x1, blocking collectives, local(): partition = lax.psum(whole_sum, ('gx', 'gy'))  405 us
    ppermute x32, starting transfers between devices, padded_2(): after = lax.ppermute(initial, axis, down)  130 us
    ppermute x32, starting transfers between devices, padded_2(): before = lax.ppermute(last, axis, up)  77.9 us
    all_gather x1, waiting for transfers between devices, local(): all_phi = lax.all_gather(volume[None], 'arm', axis=0, tiled=True)  58.4 us
    all_gather x1, waiting for transfers between devices, local(): gathered = lax.all_gather(finish[None], 'arm', axis=0, tiled=True)  50.6 us
    ppermute x32, waiting for transfers between devices, padded_2(): before = lax.ppermute(last, axis, up)  48.4 us
    ppermute x32, waiting for transfers between devices, padded_2(): after = lax.ppermute(initial, axis, down)  47.6 us
  transfers between devices with their start and end apart: 66, of which 51 were waited for; matrix products, arithmetic and copies ran while one was open for 1% of the time, Pallas kernels for 0%

commit v1 on v0

v1 whole, which is shorter than its diff:
```python
import functools

import jax
import jax.numpy as jnp
from jax import lax
from jax.experimental import pallas as pl
from jax.experimental.pallas import tpu as pltpu
from jax.sharding import PartitionSpec as P

SPECIES = 4
STEPS = 8


diffusion = 0.14
contour_step = 0.05
mixing = 0.5
compress = 1.0

LANES = 128
COEF_ONE = (1.0 - 6.0 * diffusion) / diffusion
COEF_FIELD = contour_step / diffusion
SCALE = diffusion**STEPS

BX, BY = 32, 4
COEF_REACH = (6, 5, 4)
MID_REACH = (3, 2, 1, 0)
JUNC_REACH = (7, 6, 5, 4)


def packed_size(reach):
    return sum(BX + 2 * r for r in reach)


def lane_masks():
    lane = lax.broadcasted_iota(jnp.int32, (8, LANES), 1)
    return lane == LANES - 1, lane == 0


def step(src, dst, coef, xs, ys, coef_shift):
    y0, y1 = ys
    dx, dy = coef_shift
    last, first = lane_masks()

    @pl.loop(xs[0], xs[1])
    def _(x):
        v = src[x, y0:y1]
        other = pltpu.roll(v, 4, 1)
        up = pltpu.roll(jnp.where(last, other, v), 1, 2)
        down = pltpu.roll(jnp.where(first, other, v), LANES - 1, 2)
        total = (src[x - 1, y0:y1] + src[x + 1, y0:y1]) + (
            src[x, y0 - 1 : y1 - 1] + src[x, y0 + 1 : y1 + 1]
        )
        total = total + (up + down)
        dst[x, y0:y1] = total + coef[x + dx, y0 + dy : y1 + dy] * v


def interleave_kernel(recv, coef, sums):
    for s in range(SPECIES):
        part = recv[s]
        coef[pl.ds(s, 2 * BX * BY, stride=4), :] = COEF_ONE - COEF_FIELD * part
        sums[s : s + 1, :] = jnp.sum(part, axis=0, keepdims=True)
    sums[4:8, :] = jnp.zeros((4, LANES), jnp.float32)


def pack_kernel(reach, own, low, high, up, down):
    edge = low.shape[0]
    offset = 0
    for j, r in enumerate(reach):
        for dst, y in ((up, j), (down, BY - 1 - j)):
            dst[offset : offset + r] = low[edge - r : edge, y]
            dst[offset + r : offset + r + BX] = own[:, y]
            dst[offset + r + BX : offset + 2 * r + BX] = high[0:r, y]
        offset += BX + 2 * r


def unpack(dst, reach, low, high, shift):
    ox, oy = shift
    offset = 0
    for j, r in enumerate(reach):
        n = BX + 2 * r
        dst[ox - r : ox + BX + r, oy - 1 - j] = low[offset : offset + n]
        dst[ox - r : ox + BX + r, oy + BY + j] = high[offset : offset + n]
        offset += n


def emit(src, shift, reach, wide, up, down):
    ox, oy = shift
    wide[...] = src[ox - 4 : ox + BX + 4, oy : oy + BY]
    offset = 0
    for j, r in enumerate(reach):
        n = BX + 2 * r
        up[offset : offset + n] = src[ox - r : ox + BX + r, oy + j]
        down[offset : offset + n] = src[ox - r : ox + BX + r, oy + BY - 1 - j]
        offset += n


def inner_first(own, xlow, xhigh, ylow, yhigh, coef, s2, s3, wide, up, down, a, b):
    coef[7 : 7 + BX, 3:7] = own[...]
    coef[0:7, 3:7] = xlow[...]
    coef[7 + BX :, 3:7] = xhigh[...]
    unpack(coef, COEF_REACH, ylow, yhigh, (7, 3))
    here = (slice(7, 7 + BX), slice(3, 7))

    @pl.loop(0, 14 + BX)
    def _(x):
        a[x] = 6.0 + coef[x]

    step(a, b, coef, (1, 45), (1, 9), (0, 0))
    s2[...] = b[here]
    step(b, a, coef, (2, 44), (2, 8), (0, 0))
    s3[...] = a[here]
    step(a, b, coef, (3, 43), (3, 7), (0, 0))
    emit(b, (7, 3), MID_REACH, wide, up, down)


def others(v, shift):
    row = lax.broadcasted_iota(jnp.int32, (8, LANES), 0) % 4
    return jnp.where(
        row + shift < 4, pltpu.roll(v, 8 - shift, 1), pltpu.roll(v, 4 - shift, 1)
    )


def inner_second(wide, ylow, yhigh, coef, s5, s6, s7, s8, junction, part, a, b):
    a[0 : BX + 8, 4:8] = wide[...]
    unpack(a, MID_REACH, ylow, yhigh, (4, 4))
    here = (slice(4, 4 + BX), slice(4, 8))
    step(a, b, coef, (1, 39), (1, 11), (3, -1))
    s5[...] = b[here]
    step(b, a, coef, (2, 38), (2, 10), (3, -1))
    s6[...] = a[here]
    step(a, b, coef, (3, 37), (3, 9), (3, -1))
    s7[...] = b[here]
    step(b, a, coef, (4, 36), (4, 8), (3, -1))
    part[...] = jnp.zeros_like(part)

    @pl.loop(0, BX)
    def _(x):
        q = a[x + 4, 4:8]
        s8[x] = q
        true = q * SCALE
        product = others(true, 1) * others(true, 2) * others(true, 3)
        junction[x] = product
        part[...] += jnp.sum(q * product, axis=0)


def outer_first(
    own, xlow, xhigh, ylow, yhigh, coef, s4, s5, s6, s7, s8, dens, wide, up, down, a, b
):
    a[8 : 8 + BX, 4:8] = own[...]
    a[0:8, 4:8] = xlow[...]
    a[8 + BX :, 4:8] = xhigh[...]
    unpack(a, JUNC_REACH, ylow, yhigh, (8, 4))
    here = (slice(8, 8 + BX), slice(4, 8))
    shift = (-1, -1)
    dens[...] = 0.5 * s8[...] * own[...]
    step(a, b, coef, (1, 47), (1, 11), shift)
    dens[...] += s7[...] * b[here]
    step(b, a, coef, (2, 46), (2, 10), shift)
    dens[...] += s6[...] * a[here]
    step(a, b, coef, (3, 45), (3, 9), shift)
    dens[...] += s5[...] * b[here]
    step(b, a, coef, (4, 44), (4, 8), shift)
    dens[...] += s4[4 : 4 + BX] * a[here]
    emit(a, (8, 4), MID_REACH, wide, up, down)


def outer_second(wide, ylow, yhigh, coef, s2, s3, dens, mix, out, a, b, flat):
    a[0 : BX + 8, 4:8] = wide[...]
    unpack(a, MID_REACH, ylow, yhigh, (4, 4))
    here = (slice(4, 4 + BX), slice(4, 8))
    step(a, b, coef, (1, 39), (1, 11), (3, -1))
    d5 = (here, b)
    dens_now = dens[...] + s3[...] * b[here]
    a_prev = dens_now
    flat[0] = a_prev.reshape(8 * BX * BY, LANES)
    step(b, a, coef, (2, 38), (2, 10), (3, -1))
    flat[0] = flat[0] + (s2[...] * a[here]).reshape(8 * BX * BY, LANES)
    step(a, b, coef, (3, 37), (3, 9), (3, -1))
    s1 = 6.0 + coef[7 : 7 + BX, 3:7]
    flat[0] = flat[0] + (s1 * b[here]).reshape(8 * BX * BY, LANES)
    step(b, a, coef, (4, 36), (4, 8), (3, -1))
    flat[0] = flat[0] + (0.5 * a[here]).reshape(8 * BX * BY, LANES)

    @pl.loop(0, BX)
    def _(x):
        rows = pl.ds(pl.multiple_of(x * 8 * BY, 8 * BY), 8 * BY)
        d = flat[0, rows].reshape(BY, 8, LANES)
        mixed = mix[0] * d
        for k in range(1, SPECIES):
            mixed = mixed + mix[k] * others(d, k)
        flat[1, rows] = mixed.reshape(8 * BY, LANES)

    n = 2 * BX * BY
    for s in range(SPECIES):
        for i in range(2):
            out[s, i * n : (i + 1) * n, :] = flat[i, pl.ds(s, n, stride=4), :]


def tiles(*lead):
    return jax.ShapeDtypeStruct(lead + (8, LANES), jnp.float32)


def scratch(*lead):
    return pltpu.VMEM(lead + (8, LANES), jnp.float32)


def call(kernel, outs, scratches=()):
    return pl.pallas_call(
        kernel,
        out_shape=outs,
        scratch_shapes=list(scratches),
        compiler_params=pltpu.CompilerParams(vmem_limit_bytes=40 * 1024 * 1024),
    )


def local(fields, flory_chi):
    field_here = fields[0]
    arm_index = lax.axis_index("arm")
    arms, size_gx, size_gy = (lax.axis_size(a) for a in ("arm", "gx", "gy"))
    size_z = field_here.shape[2]
    cell_count = BX * 16 * size_z * size_gx * size_gy

    def ring(shift):
        size = arms * size_gy
        at = lambda r: (r % arms) * size_gy + (r % size) // arms
        return [(at(r), at(r + shift)) for r in range(size)]

    def along_y(up, down):
        low = lax.ppermute(down, ("arm", "gy"), ring(1))
        high = lax.ppermute(up, ("arm", "gy"), ring(-1 + arms * size_gy))
        return low, high

    def along_x(array, width):
        n = size_gx
        low = lax.ppermute(array[BX - width :], "gx", [(i, (i + 1) % n) for i in range(n)])
        high = lax.ppermute(array[:width], "gx", [(i, (i - 1) % n) for i in range(n)])
        return low, high

    def pack(reach, own, low, high):
        size = packed_size(reach)
        return call(functools.partial(pack_kernel, reach), (tiles(size),) * 2)(own, low, high)

    payload = field_here.reshape(BX, arms, BY, 2, LANES).transpose(1, 0, 2, 3, 4)
    payload = payload.reshape(arms, 2 * BX * BY, LANES)
    recv = lax.all_to_all(payload, "arm", 0, 0)
    coef_flat, field_sums = call(
        interleave_kernel,
        (jax.ShapeDtypeStruct((8 * BX * BY, LANES), jnp.float32), tiles()),
    )(recv)
    coef_own = coef_flat.reshape(BX, BY, 8, LANES)
    xlow, xhigh = along_x(coef_own, 7)
    ylow, yhigh = along_y(*pack(COEF_REACH, coef_own, xlow[:], xhigh[:]))

    own = tiles(BX, BY)
    mid = packed_size(MID_REACH)
    coef, s2, s3, s4, up, down = call(
        inner_first,
        (tiles(14 + BX, 6 + BY), own, own, tiles(BX + 8, BY), tiles(mid), tiles(mid)),
        [scratch(14 + BX, 6 + BY)] * 2,
    )(coef_own, xlow, xhigh, ylow, yhigh)
    ylow, yhigh = along_y(up, down)
    s5, s6, s7, s8, junction, part = call(
        inner_second, (own,) * 5 + (tiles(),), [scratch(BX + 8, BY + 8)] * 2
    )(s4, ylow, yhigh, coef)

    sums = jnp.stack([part, field_sums])
    sums = jnp.sum(
        lax.all_to_all(jnp.broadcast_to(sums, (size_gx,) + sums.shape), "gx", 0, 0), axis=0
    )
    sums = jnp.sum(
        lax.all_to_all(jnp.broadcast_to(sums, (size_gy,) + sums.shape), "gy", 0, 0), axis=0
    )

    xlow, xhigh = along_x(junction, 8)
    ylow, yhigh = along_y(*pack(JUNC_REACH, junction, xlow, xhigh))
    dens, wide, up, down = call(
        outer_first,
        (own, tiles(BX + 8, BY), tiles(mid), tiles(mid)),
        [scratch(16 + BX, 8 + BY)] * 2,
    )(junction, xlow, xhigh, ylow, yhigh, coef, s4, s5, s6, s7, s8)
    ylow, yhigh = along_y(up, down)

    weights = flory_chi + compress
    mix = jnp.stack(
        [
            jnp.tile(jnp.stack([weights[a, (a + k) % SPECIES] for a in range(SPECIES)]), 2)
            for k in range(SPECIES)
        ]
    )
    mix = jnp.broadcast_to(mix[:, :, None], (SPECIES, 8, LANES))
    out = call(
        outer_second,
        jax.ShapeDtypeStruct((arms, 4 * BX * BY, LANES), jnp.float32),
        [scratch(BX + 8, BY + 8)] * 2 + [pltpu.VMEM((2, 8 * BX * BY, LANES), jnp.float32)],
    )(wide, ylow, yhigh, coef, s2, s3, dens, mix)

    tail = jnp.broadcast_to(sums.reshape(1, 16, LANES), (arms, 16, LANES))
    back = lax.all_to_all(jnp.concatenate([out, tail], axis=1), "arm", 0, 0)
    totals = jnp.sum(back[:, 4 * BX * BY :], axis=0)
    chain = jnp.sum(totals[:8]) / SPECIES
    field_sum = jnp.sum(
        jnp.where((jnp.arange(8) == arm_index)[:, None], totals[8:], 0.0)
    )
    scale = cell_count / (SPECIES * STEPS * chain)

    def unfold(flat):
        flat = flat.reshape(arms, BX, BY, 2, LANES).transpose(1, 0, 2, 3, 4)
        return flat.reshape(field_here.shape)

    n = 2 * BX * BY
    volume = unfold(back[:, :n]) * scale
    mixture = unfold(back[:, n : 2 * n]) * scale
    chi_sum = jnp.sum(
        jnp.where((jnp.arange(SPECIES) == arm_index)[:, None], flory_chi, 0.0)
    )
    mean_new = (1.0 - mixing) * field_sum / cell_count + mixing * chi_sum / SPECIES
    field_new = field_here + mixing * (mixture - compress - field_here)
    field_out = field_new - mean_new
    return (field_out[None], volume[None])


def solution(mesh):
    placed = (P("arm", "gx", "gy", None), P())
    return jax.shard_map(
        local,
        mesh=mesh,
        in_specs=placed,
        out_specs=(P("arm", "gx", "gy", None), P("arm", "gx", "gy", None)),
        check_vma=False,
    )
```

time: 1280 us -> 244 us (0.19)
  the two profiles are of different devices: /device:TPU:32 before, /device:TPU:6 now
where the time goes in v1:
time: 244 us; the launch traced here: 243 us
  waiting for transfers between devices  69.2 us (28%)
  starting transfers between devices  59.2 us (24%)
  Pallas kernels  57.8 us (24%)
  blocking collectives  20.2 us (8%)
  local copies, waits for them, and re-layouts  19.3 us (8%)
  other arithmetic  14.1 us (6%)
  between operations  2.92 us (1%)
    ppermute x4, starting transfers between devices, along_y(): high = lax.ppermute(up, ('arm', 'gy'), ring(-1 + arms * size_gy))  33.6 us
    ppermute x4, waiting for transfers between devices, along_y(): low = lax.ppermute(down, ('arm', 'gy'), ring(1))  27.6 us
    all_to_all x1, waiting for transfers between devices, local(): back = lax.all_to_all(jnp.concatenate([out, tail], axis=1), 'arm', 0, 0)  25.3 us
    all_to_all x1, blocking collectives, local(): recv = lax.all_to_all(payload, 'arm', 0, 0)  20.2 us
    pallas_call x1, Pallas kernels, local(): call(outer_first, (own, tiles(BX + 8, BY), tiles(mid), tiles(mid)), [scra...  17.9 us
    pallas_call x1, Pallas kernels, local(): call(outer_second, jax.ShapeDtypeStruct((arms, 4 * BX * BY, LANES), jnp.f...  14.2 us
    unnamed x36, local copies, waits for them, and re-layouts  13.7 us
    pallas_call x1, Pallas kernels, local(): call(inner_second, (own,) * 5 + (tiles(),), [scratch(BX + 8, BY + 8)] * 2)  13 us
  transfers between devices with their start and end apart: 15, of which 10 were waited for; matrix products, arithmetic and copies ran while one was open for 6% of the time, Pallas kernels for 7%

profile of v1, /device:TPU:6, one launch (start us, length us, event | category | flops | bytes accessed | tf_op | source)
XLA Modules:
  0.0 242.7 jit_solution(553252985055636074)
XLA Ops:
  0.6 1.3 reshape_squeeze.3
  2.0 20.2 %all_to_all.20.recv = f32[4,256,128]{2,1,0:T(8,128)S(1)} all-to-all(f32[4,256,128]{2,1,0:T(8,128)S(1)} %bitcast.39), channel_id=1, replica_groups=mesh['arm'=4,'gx'=8,'gy'=16] {'arm'}, dimensions={0} | all-to-all | bytes 1048576 | tf_op jit(solution)/shard_map/all_to_all | solution.py:245
  22.3 1.7 collective-permute-start.1
  24.0 2.5 %collective-permute-done.low.xlow = f32[7,4,8,128]{3,2,1,0:T(8,128)S(1)} collective-permute-done((f32[7,4,8,128]{3,2,1,0:T(8,128)S(1)}, f32[7,4,8,128]{3,2,1,0:T(8,128)S(1)}, u32[]{:S(2)}, u32[]{:S(2)}) %collective-permute-start) | collective-permute-done | bytes 114720 | tf_op jit(solution)/shard_map/ppermute | solution.py:235
  26.6 2.1 collective-permute-start.2
  28.7 10.5 %collective-permute-start.3 = (f32[126,8,128]{2,1,0:T(8,128)S(1)}, f32[126,8,128]{2,1,0:T(8,128)S(1)}, u32[]{:S(2)}, u32[]{:S(2)}) collective-permute-start(f32[126,8,128]{2,1,0:T(8,128)S(1)} %get-tuple-element.26), channel_id=1, source_target_pairs={{0,399},{128,0},{256,128},{384,256},{1,384},{129,1},{257,129},{385... | collective-permute-start | bytes 1548296 | tf_op jit(solution)/shard_map/ppermute | solution.py:230
  39.2 9.5 %collective-permute-done.2.ylow = f32[126,8,128]{2,1,0:T(8,128)S(1)} collective-permute-done((f32[126,8,128]{2,1,0:T(8,128)S(1)}, f32[126,8,128]{2,1,0:T(8,128)S(1)}, u32[]{:S(2)}, u32[]{:S(2)}) %collective-permute-start.2) | collective-permute-done | bytes 516128 | tf_op jit(solution)/shard_map/ppermute | solution.py:229
  48.8 1.7 collective-permute-done.3.yhigh
  50.5 11.2 %shard_map.43 = (f32[46,10,8,128]{3,2,1,0:T(8,128)S(1)}, f32[32,4,8,128]{3,2,1,0:T(8,128)S(1)}, f32[32,4,8,128]{3,2,1,0:T(8,128)S(1)}, f32[40,4,8,128]{3,2,1,0:T...) custom-call(f32[32,4,8,128]{3,2,1,0:T(8,128)S(1)} %bitcast.34, ...), custom_call_target="tpu_custom_call" | custom-call | tf_op jit(solution)/shard_map/pallas_call | solution.py:256
  61.8 0.8 copy-done.2
  63.4 1.9 collective-permute-start.4
  65.3 7.7 %collective-permute-start.5 = (f32[140,8,128]{2,1,0:T(8,128)S(1)}, f32[140,8,128]{2,1,0:T(8,128)S(1)}, u32[]{:S(2)}, u32[]{:S(2)}) collective-permute-start(f32[140,8,128]{2,1,0:T(8,128)S(1)} %get-tuple-element.29), channel_id=1, source_target_pairs={{0,399},{128,0},{256,128},{384,256},{1,384},{129,1},{257,129},{385... | collective-permute-start | bytes 1720328 | tf_op jit(solution)/shard_map/ppermute | solution.py:230
  73.0 11.9 %collective-permute-done.4.ylow = f32[140,8,128]{2,1,0:T(8,128)S(1)} collective-permute-done((f32[140,8,128]{2,1,0:T(8,128)S(1)}, f32[140,8,128]{2,1,0:T(8,128)S(1)}, u32[]{:S(2)}, u32[]{:S(2)}) %collective-permute-start.4) | collective-permute-done | bytes 573472 | tf_op jit(solution)/shard_map/ppermute | solution.py:229
  84.8 1.2 collective-permute-done.5.yhigh
  86.0 13.0 %shard_map.44 = (f32[32,4,8,128]{3,2,1,0:T(8,128)S(1)}, f32[32,4,8,128]{3,2,1,0:T(8,128)S(1)}, f32[32,4,8,128]{3,2,1,0:T(8,128)S(1)}, f32[32,4,8,128]{3,2,1,0:T(...) custom-call(f32[40,4,8,128]{3,2,1,0:T(8,128)S(1)} %get-tuple-element.27.wide.s4, ...), custom_call_target="tpu_custom_call" | custom-call | tf_op jit(solution)/shard_map/pallas_call | solution.py:262
  100.6 0.8 copy-done.12
  101.4 0.8 copy-done.14
  102.3 1.7 collective-permute-start.7
  104.0 2.6 %collective-permute-done.6.low.xlow = f32[8,4,8,128]{3,2,1,0:T(8,128)S(1)} collective-permute-done((f32[8,4,8,128]{3,2,1,0:T(8,128)S(1)}, f32[8,4,8,128]{3,2,1,0:T(8,128)S(1)}, u32[]{:S(2)}, u32[]{:S(2)}) %collective-permute-start.6) | collective-permute-done | bytes 131104 | tf_op jit(solution)/shard_map/ppermute | solution.py:235
  106.7 1.2 shard_map.45
  107.9 1.9 collective-permute-start.8
  109.8 7.7 %collective-permute-start.9 = (f32[172,8,128]{2,1,0:T(8,128)}, f32[172,8,128]{2,1,0:T(8,128)}, u32[]{:S(2)}, u32[]{:S(2)}) collective-permute-start(f32[172,8,128]{2,1,0:T(8,128)} %get-tuple-element.33), channel_id=1, source_target_pairs={{0,399},{128,0},{256,128},{384,256},{1,384},{129,1},{257,129},{385... | collective-permute-start | bytes 2113544 | tf_op jit(solution)/shard_map/ppermute | solution.py:230
  118.9 6.0 %all-to-all-start.1 = ((f32[8,2,8,128]{3,2,1,0:T(8,128)}), f32[8,2,8,128]{3,2,1,0:T(8,128)S(1)}, u32[]{:S(2)}, u32[]{:S(2)}) async-start(f32[8,2,8,128]{3,2,1,0:T(8,128)} %broadcast_in_dim.48), calls=%async_computation.1 | async-start | bytes 131072 | tf_op jit(solution)/shard_map/all_to_all | solution.py:268
  124.8 6.2 %collective-permute-done.8.ylow = f32[172,8,128]{2,1,0:T(8,128)} collective-permute-done((f32[172,8,128]{2,1,0:T(8,128)}, f32[172,8,128]{2,1,0:T(8,128)}, u32[]{:S(2)}, u32[]{:S(2)}) %collective-permute-start.8) | collective-permute-done | bytes 704544 | tf_op jit(solution)/shard_map/ppermute | solution.py:229
  131.0 1.7 collective-permute-done.9.yhigh
  132.8 1.0 copy-done.9
  133.8 1.0 copy-done.11
  134.9 1.0 copy-done.13
  135.9 1.0 copy-done.15
  137.0 17.9 %shard_map.46 = (f32[32,4,8,128]{3,2,1,0:T(8,128)S(1)}, f32[40,4,8,128]{3,2,1,0:T(8,128)S(1)}, f32[140,8,128]{2,1,0:T(8,128)}, f32[140,8,128]{2,1,0:T(8,128)}) custom-call(f32[32,4,8,128]{3,2,1,0:T(8,128)S(1)} %get-tuple-element.31.own, f32[8,4,8,128]{3,2,1,0:T(8,128)S(1)} %collective-permute-done.6.low.xlow, ...), custom_call_target="tpu_custom_call" | custom-call | tf_op jit(solution)/shard_map/pallas_call | solution.py:276
  154.9 0.8 copy-done
  156.5 2.0 collective-permute-start.10
  158.6 7.7 %collective-permute-start.11 = (f32[140,8,128]{2,1,0:T(8,128)}, f32[140,8,128]{2,1,0:T(8,128)}, u32[]{:S(2)}, u32[]{:S(2)}) collective-permute-start(f32[140,8,128]{2,1,0:T(8,128)} %get-tuple-element.40), channel_id=1, source_target_pairs={{0,399},{128,0},{256,128},{384,256},{1,384},{129,1},{257,129},{385... | collective-permute-start | bytes 1720328 | tf_op jit(solution)/shard_map/ppermute | solution.py:230
  167.7 3.8 %all-to-all-start.2 = ((f32[16,2,8,128]{3,2,1,0:T(8,128)}), f32[16,2,8,128]{3,2,1,0:T(8,128)S(1)}, u32[]{:S(2)}, u32[]{:S(2)}) async-start(f32[16,2,8,128]{3,2,1,0:T(8,128)} %broadcast_in_dim.49), calls=%async_computation.2 | async-start | bytes 262144 | tf_op jit(solution)/shard_map/all_to_all | solution.py:271
  171.5 2.8 %pad_maximum_fusion.3 = f32[4]{0:T(128)S(1)} fusion(f32[1]{0:T(128)} %bitcast.8, f32[1]{0:T(128)} %bitcast.7, f32[1]{0:T(128)} %bitcast.6, f32[1]{0:T(128)} %bitcast.5), kind=kLoop, calls=%fused_computation.13 | loop fusion | flops 12 | bytes 32 | tf_op jit(solution)/shard_map/stack | solution.py:286
  174.4 2.6 %pad_maximum_fusion.4 = f32[4]{0:T(128)S(1)} fusion(f32[1]{0:T(128)} %bitcast.12, f32[1]{0:T(128)} %bitcast.11, f32[1]{0:T(128)} %bitcast.10, f32[1]{0:T(128)} %bitcast.9), kind=kLoop, calls=%fused_computation.14 | loop fusion | flops 12 | bytes 32 | tf_op jit(solution)/shard_map/stack | solution.py:286
  177.1 2.6 %pad_maximum_fusion.5 = f32[4]{0:T(128)S(1)} fusion(f32[1]{0:T(128)} %bitcast.16, f32[1]{0:T(128)} %bitcast.15, f32[1]{0:T(128)} %bitcast.14, f32[1]{0:T(128)} %bitcast.13), kind=kLoop, calls=%fused_computation.15 | loop fusion | flops 12 | bytes 32 | tf_op jit(solution)/shard_map/stack | solution.py:286
  179.8 2.6 %pad_maximum_fusion.6 = f32[4]{0:T(128)S(1)} fusion(f32[1]{0:T(128)} %bitcast.20, f32[1]{0:T(128)} %bitcast.19, f32[1]{0:T(128)} %bitcast.18, f32[1]{0:T(128)} %bitcast.17), kind=kLoop, calls=%fused_computation.16 | loop fusion | flops 12 | bytes 32 | tf_op jit(solution)/shard_map/stack | solution.py:286
  182.5 6.5 %all-to-all-done.2 = f32[16,2,8,128]{3,2,1,0:T(8,128)S(1)} async-done(((f32[16,2,8,128]{3,2,1,0:T(8,128)}), f32[16,2,8,128]{3,2,1,0:T(8,128)S(1)}, u32[]{:S(2)}, u32[]{:S(2)}) %all-to-all-start.2) | async-done | bytes 131104 | tf_op jit(solution)/shard_map/all_to_all | solution.py:271
  189.1 1.0 copy-done.3
  190.2 1.0 copy-done.5
  191.2 1.0 copy-done.7
  192.3 14.2 %shard_map.47 = f32[4,512,128]{2,1,0:T(8,128)S(1)} custom-call(f32[40,4,8,128]{3,2,1,0:T(8,128)S(1)} %copy-done.1, f32[140,8,128]{2,1,0:T(8,128)S(1)} %collective-permute-done.10.ylow, f32[140,8,128]{2,1,0:T(8,128)} %collective-permute-done.11.yhigh, f32[46,10,8,128]{3,2,1,0:T(8,128)S(1)} %get-tuple-element.30.coef, f32[32,4,8,128]{3,2,1,0:T(8,128)S(1)} %copy-done.3, ...), custom_call_target="tpu_custom_call" | custom-call | tf_op jit(solution)/shard_map/pallas_call | solution.py:291
  206.5 1.1 pad_maximum_fusion
  207.6 4.3 %all-to-all-start.3 = ((f32[4,528,128]{2,1,0:T(8,128)}), f32[4,528,128]{2,1,0:T(8,128)S(1)}, u32[]{:S(2)}, u32[]{:S(2)}) async-start(f32[4,528,128]{2,1,0:T(8,128)} %pad_maximum_fusion), calls=%async_computation.3 | async-start | bytes 2162688 | tf_op jit(solution)/shard_map/all_to_all | solution.py:298
  212.6 25.3 %all-to-all-done.3 = f32[4,528,128]{2,1,0:T(8,128)S(1)} async-done(((f32[4,528,128]{2,1,0:T(8,128)}), f32[4,528,128]{2,1,0:T(8,128)S(1)}, u32[]{:S(2)}, u32[]{:S(2)}) %all-to-all-start.3) | async-done | bytes 1081376 | tf_op jit(solution)/shard_map/all_to_all | solution.py:298
  239.9 1.2 mul.52
  241.8 0.9 add_subtract_fusion
  (63 shorter events, 8.0 us)
Async XLA Ops:
  22.3 4.2 %collective-permute-start = (f32[7,4,8,128]{3,2,1,0:T(8,128)S(1)}, f32[7,4,8,128]{3,2,1,0:T(8,128)S(1)}, u32[]{:S(2)}, u32[]{:S(2)}) collective-permute-start(f32[7,4,8,128]{3,2,1,0:T(8,128)S(1)} %bitcast.41), channel_id=1, source_target_pairs={{0,16},{16,32},{32,48},{48,64},{64,80},{80,96},{96,112},{112,0},{1... | collective-permute-start | bytes 344072 | tf_op jit(solution)/shard_map/ppermute | solution.py:235
  22.3 4.2 %collective-permute-start.1 = (f32[7,4,8,128]{3,2,1,0:T(8,128)S(1)}, f32[7,4,8,128]{3,2,1,0:T(8,128)S(1)}, u32[]{:S(2)}, u32[]{:S(2)}) collective-permute-start(f32[7,4,8,128]{3,2,1,0:T(8,128)S(1)} %bitcast.40), channel_id=1, source_target_pairs={{0,112},{16,0},{32,16},{48,32},{64,48},{80,64},{96,80},{112,96},{1... | collective-permute-start | bytes 344072 | tf_op jit(solution)/shard_map/ppermute | solution.py:236
  26.6 22.2 %collective-permute-start.2 = (f32[126,8,128]{2,1,0:T(8,128)S(1)}, f32[126,8,128]{2,1,0:T(8,128)S(1)}, u32[]{:S(2)}, u32[]{:S(2)}) collective-permute-start(f32[126,8,128]{2,1,0:T(8,128)S(1)} %get-tuple-element.25), channel_id=1, source_target_pairs={{0,128},{128,256},{256,384},{384,1},{1,129},{129,257},{257,385},{3... | collective-permute-start | bytes 1548296 | tf_op jit(solution)/shard_map/ppermute | solution.py:229
  28.7 21.8 %collective-permute-start.3 = (f32[126,8,128]{2,1,0:T(8,128)S(1)}, f32[126,8,128]{2,1,0:T(8,128)S(1)}, u32[]{:S(2)}, u32[]{:S(2)}) collective-permute-start(f32[126,8,128]{2,1,0:T(8,128)S(1)} %get-tuple-element.26), channel_id=1, source_target_pairs={{0,399},{128,0},{256,128},{384,256},{1,384},{129,1},{257,129},{385... | collective-permute-start | bytes 1548296 | tf_op jit(solution)/shard_map/ppermute | solution.py:230
  61.8 0.8 copy-start.2
  62.6 0.8 copy-start.4
  63.4 21.5 %collective-permute-start.4 = (f32[140,8,128]{2,1,0:T(8,128)S(1)}, f32[140,8,128]{2,1,0:T(8,128)S(1)}, u32[]{:S(2)}, u32[]{:S(2)}) collective-permute-start(f32[140,8,128]{2,1,0:T(8,128)S(1)} %get-tuple-element.28), channel_id=1, source_target_pairs={{0,128},{128,256},{256,384},{384,1},{1,129},{129,257},{257,385},{3... | collective-permute-start | bytes 1720328 | tf_op jit(solution)/shard_map/ppermute | solution.py:229
  65.3 20.8 %collective-permute-start.5 = (f32[140,8,128]{2,1,0:T(8,128)S(1)}, f32[140,8,128]{2,1,0:T(8,128)S(1)}, u32[]{:S(2)}, u32[]{:S(2)}) collective-permute-start(f32[140,8,128]{2,1,0:T(8,128)S(1)} %get-tuple-element.29), channel_id=1, source_target_pairs={{0,399},{128,0},{256,128},{384,256},{1,384},{129,1},{257,129},{385... | collective-permute-start | bytes 1720328 | tf_op jit(solution)/shard_map/ppermute | solution.py:230
  99.0 0.8 copy-start.8
  99.8 0.8 copy-start.10
  100.6 0.8 copy-start.12
  101.4 0.8 copy-start.14
  102.2 15.3 %copy-start.17 = (f32[4,4]{1,0:T(4,128)S(1)}, f32[4,4]{1,0:T(4,128)}, u32[]{:S(2)}) copy-start(f32[4,4]{1,0:T(4,128)} %param.3) | copy-start | bytes 196
  102.2 4.4 %collective-permute-start.6 = (f32[8,4,8,128]{3,2,1,0:T(8,128)S(1)}, f32[8,4,8,128]{3,2,1,0:T(8,128)S(1)}, u32[]{:S(2)}, u32[]{:S(2)}) collective-permute-start(f32[8,4,8,128]{3,2,1,0:T(8,128)S(1)} %get-tuple-element.51), channel_id=1, source_target_pairs={{0,16},{16,32},{32,48},{48,64},{64,80},{80,96},{96,112},{112,0},{1... | collective-permute-start | bytes 393224 | tf_op jit(solution)/shard_map/ppermute | solution.py:235
  102.3 4.4 %collective-permute-start.7 = (f32[8,4,8,128]{3,2,1,0:T(8,128)S(1)}, f32[8,4,8,128]{3,2,1,0:T(8,128)S(1)}, u32[]{:S(2)}, u32[]{:S(2)}) collective-permute-start(f32[8,4,8,128]{3,2,1,0:T(8,128)S(1)} %get-tuple-element.50), channel_id=1, source_target_pairs={{0,112},{16,0},{32,16},{48,32},{64,48},{80,64},{96,80},{112,96},{1... | collective-permute-start | bytes 393224 | tf_op jit(solution)/shard_map/ppermute | solution.py:236
  107.9 23.2 %collective-permute-start.8 = (f32[172,8,128]{2,1,0:T(8,128)}, f32[172,8,128]{2,1,0:T(8,128)}, u32[]{:S(2)}, u32[]{:S(2)}) collective-permute-start(f32[172,8,128]{2,1,0:T(8,128)} %get-tuple-element.32), channel_id=1, source_target_pairs={{0,128},{128,256},{256,384},{384,1},{1,129},{129,257},{257,385},{3... | collective-permute-start | bytes 2113544 | tf_op jit(solution)/shard_map/ppermute | solution.py:229
  109.8 23.0 %collective-permute-start.9 = (f32[172,8,128]{2,1,0:T(8,128)}, f32[172,8,128]{2,1,0:T(8,128)}, u32[]{:S(2)}, u32[]{:S(2)}) collective-permute-start(f32[172,8,128]{2,1,0:T(8,128)} %get-tuple-element.33), channel_id=1, source_target_pairs={{0,399},{128,0},{256,128},{384,256},{1,384},{129,1},{257,129},{385... | collective-permute-start | bytes 2113544 | tf_op jit(solution)/shard_map/ppermute | solution.py:230
  118.9 48.2 %all-to-all-start.1 = ((f32[8,2,8,128]{3,2,1,0:T(8,128)}), f32[8,2,8,128]{3,2,1,0:T(8,128)S(1)}, u32[]{:S(2)}, u32[]{:S(2)}) async-start(f32[8,2,8,128]{3,2,1,0:T(8,128)} %broadcast_in_dim.48), calls=%async_computation.1 | async-start | bytes 131072 | tf_op jit(solution)/shard_map/all_to_all | solution.py:268
  132.8 1.0 copy-start.9
  133.8 1.0 copy-start.11
  134.9 1.0 copy-start.13
  135.9 1.0 copy-start.15
  154.9 0.8 copy-start
  155.7 0.8 copy-start.6
  156.5 32.6 %copy-start.1 = (f32[40,4,8,128]{3,2,1,0:T(8,128)S(1)}, f32[40,4,8,128]{3,2,1,0:T(8,128)}, u32[]{:S(2)}) copy-start(f32[40,4,8,128]{3,2,1,0:T(8,128)} %copy-done) | copy-start | bytes 1966084
  156.5 32.5 %collective-permute-start.10 = (f32[140,8,128]{2,1,0:T(8,128)}, f32[140,8,128]{2,1,0:T(8,128)S(1)}, u32[]{:S(2)}, u32[]{:S(2)}) collective-permute-start(f32[140,8,128]{2,1,0:T(8,128)} %get-tuple-element.39), channel_id=1, source_target_pairs={{0,128},{128,256},{256,384},{384,1},{1,129},{129,257},{257,385},{3... | collective-permute-start | bytes 1720328 | tf_op jit(solution)/shard_map/ppermute | solution.py:229
  158.6 30.5 %collective-permute-start.11 = (f32[140,8,128]{2,1,0:T(8,128)}, f32[140,8,128]{2,1,0:T(8,128)}, u32[]{:S(2)}, u32[]{:S(2)}) collective-permute-start(f32[140,8,128]{2,1,0:T(8,128)} %get-tuple-element.40), channel_id=1, source_target_pairs={{0,399},{128,0},{256,128},{384,256},{1,384},{129,1},{257,129},{385... | collective-permute-start | bytes 1720328 | tf_op jit(solution)/shard_map/ppermute | solution.py:230
  167.7 21.3 %all-to-all-start.2 = ((f32[16,2,8,128]{3,2,1,0:T(8,128)}), f32[16,2,8,128]{3,2,1,0:T(8,128)S(1)}, u32[]{:S(2)}, u32[]{:S(2)}) async-start(f32[16,2,8,128]{3,2,1,0:T(8,128)} %broadcast_in_dim.49), calls=%async_computation.2 | async-start | bytes 262144 | tf_op jit(solution)/shard_map/all_to_all | solution.py:271
  189.1 1.0 copy-start.3
  190.2 1.0 copy-start.5
  191.2 1.0 copy-start.7
  207.6 30.3 %all-to-all-start.3 = ((f32[4,528,128]{2,1,0:T(8,128)}), f32[4,528,128]{2,1,0:T(8,128)S(1)}, u32[]{:S(2)}, u32[]{:S(2)}) async-start(f32[4,528,128]{2,1,0:T(8,128)} %pad_maximum_fusion), calls=%async_computation.3 | async-start | bytes 2162688 | tf_op jit(solution)/shard_map/all_to_all | solution.py:298
  239.8 2.0 copy-start.16

commit v2 on v0

v2 whole, which is shorter than its diff:
```python
import functools

import jax
import jax.numpy as jnp
from jax import lax
from jax.experimental import pallas as pl
from jax.experimental.pallas import tpu as pltpu
from jax.sharding import PartitionSpec as P

SPECIES = 4
STEPS = 8


diffusion = 0.14
contour_step = 0.05
mixing = 0.5
compress = 1.0

LANES = 128
COEF_ONE = (1.0 - 6.0 * diffusion) / diffusion
COEF_FIELD = contour_step / diffusion
SCALE = diffusion**STEPS

BX, BY = 32, 4
VMEM_LIMIT = 16 * 1024 * 1024
COEF_REACH = (6, 5, 4)
MID_REACH = (3, 2, 1, 0)
JUNC_REACH = (7, 6, 5, 4)


def packed_size(reach):
    return sum(BX + 2 * r for r in reach)


def lane_masks():
    lane = lax.broadcasted_iota(jnp.int32, (8, LANES), 1)
    return lane == LANES - 1, lane == 0


def step(src, dst, coef, xs, ys, coef_shift):
    (x0, x1), (y0, y1) = xs, ys
    dx, dy = coef_shift
    last, first = lane_masks()
    v = src[x0:x1, y0:y1]
    other = pltpu.roll(v, 4, 2)
    up = pltpu.roll(jnp.where(last, other, v), 1, 3)
    down = pltpu.roll(jnp.where(first, other, v), LANES - 1, 3)
    total = (src[x0 - 1 : x1 - 1, y0:y1] + src[x0 + 1 : x1 + 1, y0:y1]) + (
        src[x0:x1, y0 - 1 : y1 - 1] + src[x0:x1, y0 + 1 : y1 + 1]
    )
    dst[x0:x1, y0:y1] = total + (up + down) + coef[x0 + dx : x1 + dx, y0 + dy : y1 + dy] * v


def interleave_kernel(recv, coef, sums):
    n = BX * BY
    for s in range(SPECIES):
        for half in range(2):
            coef[pl.ds(half * 4 + s, n, stride=8), :] = (
                COEF_ONE - COEF_FIELD * recv[s, half * n : (half + 1) * n]
            )
        sums[s : s + 1, :] = jnp.sum(recv[s], axis=0, keepdims=True)
    sums[4:8, :] = jnp.zeros((4, LANES), jnp.float32)


def by_side(arm, first, second, body):
    odd = arm[0] % 2

    @pl.when(odd == 0)
    def _():
        body(second, first)

    @pl.when(odd == 1)
    def _():
        body(first, second)


def pack_kernel(reach, arm, own, low, high, first, second):
    edge = low.shape[0]

    def body(up, down):
        offset = 0
        for j, r in enumerate(reach):
            for dst, y in ((up, j), (down, BY - 1 - j)):
                dst[offset : offset + r] = low[edge - r : edge, y]
                dst[offset + r : offset + r + BX] = own[:, y]
                dst[offset + r + BX : offset + 2 * r + BX] = high[0:r, y]
            offset += BX + 2 * r

    by_side(arm, first, second, body)


def unpack(arm, dst, reach, first, second, shift):
    ox, oy = shift

    def body(low, high):
        offset = 0
        for j, r in enumerate(reach):
            n = BX + 2 * r
            dst[ox - r : ox + BX + r, oy - 1 - j] = low[offset : offset + n]
            dst[ox - r : ox + BX + r, oy + BY + j] = high[offset : offset + n]
            offset += n

    by_side(arm, first, second, body)


def emit(arm, src, shift, reach, wide, first, second):
    ox, oy = shift
    wide[...] = src[ox - 4 : ox + BX + 4, oy : oy + BY]

    def body(up, down):
        offset = 0
        for j, r in enumerate(reach):
            n = BX + 2 * r
            up[offset : offset + n] = src[ox - r : ox + BX + r, oy + j]
            down[offset : offset + n] = src[ox - r : ox + BX + r, oy + BY - 1 - j]
            offset += n

    by_side(arm, first, second, body)


def inner_first(arm, own, xlow, xhigh, y1, y2, coef, s2, s3, wide, e1, e2, a, b):
    coef[7 : 7 + BX, 3:7] = own[...]
    coef[0:7, 3:7] = xlow[...]
    coef[7 + BX :, 3:7] = xhigh[...]
    unpack(arm, coef, COEF_REACH, y1, y2, (7, 3))
    here = (slice(7, 7 + BX), slice(3, 7))
    a[...] = 6.0 + coef[...]
    step(a, b, coef, (1, 45), (1, 9), (0, 0))
    s2[...] = b[here]
    step(b, a, coef, (2, 44), (2, 8), (0, 0))
    s3[...] = a[here]
    step(a, b, coef, (3, 43), (3, 7), (0, 0))
    emit(arm, b, (7, 3), MID_REACH, wide, e1, e2)


def others(v, shift):
    axis = v.ndim - 2
    row = lax.broadcasted_iota(jnp.int32, (8, LANES), 0) % 4
    return jnp.where(
        row + shift < 4, pltpu.roll(v, 8 - shift, axis), pltpu.roll(v, 4 - shift, axis)
    )


def inner_second(
    arm, wide, y1, y2, coef, sums, s5, s6, s7, s8, junction, spread, a, b
):
    a[0 : BX + 8, 4:8] = wide[...]
    unpack(arm, a, MID_REACH, y1, y2, (4, 4))
    here = (slice(4, 4 + BX), slice(4, 8))
    step(a, b, coef, (1, 39), (1, 11), (3, -1))
    s5[...] = b[here]
    step(b, a, coef, (2, 38), (2, 10), (3, -1))
    s6[...] = a[here]
    step(a, b, coef, (3, 37), (3, 9), (3, -1))
    s7[...] = b[here]
    step(b, a, coef, (4, 36), (4, 8), (3, -1))
    part = jnp.zeros((8, LANES), jnp.float32)
    for x in range(BX):
        q = a[x + 4, 4:8]
        s8[x] = q
        true = q * SCALE
        product = others(true, 1) * others(true, 2) * others(true, 3)
        junction[x] = product
        part = part + jnp.sum(q * product, axis=0)
    row = lax.broadcasted_iota(jnp.int32, (8, LANES), 0)
    chain = jnp.broadcast_to(jnp.sum(part, axis=0, keepdims=True), (8, LANES))
    spread[...] = jnp.broadcast_to(jnp.where(row == 4, chain, sums[...]), spread.shape)


def outer_first(
    arm, own, xlow, xhigh, y1, y2, coef, s4, s5, s6, s7, s8, got,
    dens, wide, e1, e2, spread, a, b
):
    spread[...] = jnp.broadcast_to(jnp.sum(got[...], axis=0), spread.shape)
    a[8 : 8 + BX, 4:8] = own[...]
    a[0:8, 4:8] = xlow[...]
    a[8 + BX :, 4:8] = xhigh[...]
    unpack(arm, a, JUNC_REACH, y1, y2, (8, 4))
    here = (slice(8, 8 + BX), slice(4, 8))
    shift = (-1, -1)
    step(a, b, coef, (1, 47), (1, 11), shift)
    dens[...] = 0.5 * s8[...] * own[...] + s7[...] * b[here]
    step(b, a, coef, (2, 46), (2, 10), shift)
    dens[...] += s6[...] * a[here]
    step(a, b, coef, (3, 45), (3, 9), shift)
    dens[...] += s5[...] * b[here]
    step(b, a, coef, (4, 44), (4, 8), shift)
    dens[...] += s4[4 : 4 + BX] * a[here]
    emit(arm, a, (8, 4), MID_REACH, wide, e1, e2)


def outer_second(
    arm, chi, wide, y1, y2, coef, s2, s3, dens, got, out, a, b, flat, mixed
):
    a[0 : BX + 8, 4:8] = wide[...]
    unpack(arm, a, MID_REACH, y1, y2, (4, 4))
    here = (slice(4, 4 + BX), slice(4, 8))
    rows = (8 * BX * BY, LANES)
    step(a, b, coef, (1, 39), (1, 11), (3, -1))
    flat[...] = (dens[...] + s3[...] * b[here]).reshape(rows)
    step(b, a, coef, (2, 38), (2, 10), (3, -1))
    flat[...] += (s2[...] * a[here]).reshape(rows)
    step(a, b, coef, (3, 37), (3, 9), (3, -1))
    flat[...] += ((6.0 + coef[7 : 7 + BX, 3:7]) * b[here]).reshape(rows)
    step(b, a, coef, (4, 36), (4, 8), (3, -1))
    d = flat[...].reshape(BX, BY, 8, LANES) + 0.5 * a[here]
    flat[...] = d.reshape(rows)
    row = lax.broadcasted_iota(jnp.int32, (8, LANES), 0) % 4
    total = None
    for k in range(SPECIES):
        weight = jnp.zeros((8, LANES), jnp.float32)
        for s in range(SPECIES):
            weight = jnp.where(row == s, chi[s, (s + k) % SPECIES] + compress, weight)
        term = weight * (others(d, k) if k else d)
        total = term if total is None else total + term
    mixed[...] = total.reshape(rows)
    n = BX * BY
    tail = jnp.sum(got[...], axis=0)
    for s in range(SPECIES):
        for i, src in enumerate((flat, mixed)):
            for half in range(2):
                at = (2 * i + half) * n
                out[s, at : at + n, :] = src[pl.ds(half * 4 + s, n, stride=8), :]
        out[s, 4 * n : 4 * n + 8, :] = tail


def finish(cell_count, arm, chi, back, field, new, volume):
    n = BX * BY
    here = arm[0]
    tail = jnp.sum(back[:, 4 * n : 4 * n + 8], axis=0)
    row = lax.broadcasted_iota(jnp.int32, (8, LANES), 0)
    chain = jnp.sum(jnp.where(row == 4, tail, 0.0), keepdims=True) / SPECIES
    field_sum = jnp.sum(jnp.where(row == here, tail, 0.0), keepdims=True)
    scale = cell_count / (SPECIES * STEPS * chain)
    chi_sum = chi[here, 0]
    for s in range(1, SPECIES):
        chi_sum = chi_sum + chi[here, s]
    mean_new = (1.0 - mixing) / cell_count * field_sum + mixing * chi_sum / SPECIES
    for q in range(SPECIES):
        for half in range(2):
            lanes = slice(half * LANES, (half + 1) * LANES)
            for x in range(BX):
                at = half * n + x * BY
                ys = slice(q * BY, (q + 1) * BY)
                volume[x, ys, lanes] = scale * back[q, at : at + BY, :]
                mixture = scale * back[q, 2 * n + at : 2 * n + at + BY, :]
                old = field[x, ys, lanes]
                new[x, ys, lanes] = old + mixing * (mixture - compress - old) - mean_new


def tiles(*lead):
    return jax.ShapeDtypeStruct(lead + (8, LANES), jnp.float32)


def scratch(*lead):
    return pltpu.VMEM(lead + (8, LANES), jnp.float32)


def call(kernel, outs, scratches=(), scalars=0, arrays=0):
    in_specs = [pl.BlockSpec(memory_space=pltpu.SMEM)] * scalars
    in_specs += [pl.BlockSpec(memory_space=pltpu.VMEM)] * arrays
    return pl.pallas_call(
        kernel,
        out_shape=outs,
        in_specs=in_specs,
        scratch_shapes=list(scratches),
        compiler_params=pltpu.CompilerParams(vmem_limit_bytes=VMEM_LIMIT),
    )


def local(fields, flory_chi):
    field_here = fields[0]
    arm = lax.axis_index("arm")[None]
    arms, size_gx, size_gy = (lax.axis_size(a) for a in ("arm", "gx", "gy"))
    cell_count = field_here.size * size_gx * size_gy
    n = BX * BY

    size = arms * size_gy
    at = lambda r: (r % arms) * size_gy + (r % size) // arms
    first_pairs = [(at(r), at(r ^ 1)) for r in range(size)]
    second_pairs = [(at(r), at(((r + 1) ^ 1) - 1)) for r in range(size)]

    def along_y(first, second):
        return (
            lax.ppermute(first, ("arm", "gy"), first_pairs),
            lax.ppermute(second, ("arm", "gy"), second_pairs),
        )

    def along_x(array, width):
        m = size_gx
        low = lax.ppermute(array[BX - width :], "gx", [(i, (i + 1) % m) for i in range(m)])
        high = lax.ppermute(array[:width], "gx", [(i, (i - 1) % m) for i in range(m)])
        return low, high

    def pack(reach, own, low, high):
        kernel = functools.partial(pack_kernel, reach)
        outs = (tiles(packed_size(reach)),) * 2
        return call(kernel, outs, scalars=1, arrays=3)(arm, own, low, high)

    payload = field_here.reshape(BX, arms, BY, 2, LANES).transpose(1, 3, 0, 2, 4)
    recv = lax.all_to_all(payload.reshape(arms, 2 * n, LANES), "arm", 0, 0)
    coef_flat, sums = call(
        interleave_kernel,
        (jax.ShapeDtypeStruct((8 * n, LANES), jnp.float32), tiles()),
        arrays=1,
    )(recv)
    coef_own = coef_flat.reshape(BX, BY, 8, LANES)
    xlow, xhigh = along_x(coef_own, 7)
    y1, y2 = along_y(*pack(COEF_REACH, coef_own, xlow, xhigh))

    own, wide_shape = tiles(BX, BY), tiles(BX + 8, BY)
    mid = tiles(packed_size(MID_REACH))
    coef, s2, s3, s4, e1, e2 = call(
        inner_first,
        (tiles(14 + BX, 6 + BY), own, own, wide_shape, mid, mid),
        [scratch(14 + BX, 6 + BY)] * 2,
        scalars=1,
        arrays=5,
    )(arm, coef_own, xlow, xhigh, y1, y2)
    y1, y2 = along_y(e1, e2)
    s5, s6, s7, s8, junction, spread = call(
        inner_second,
        (own,) * 5 + (tiles(size_gy),),
        [scratch(BX + 8, BY + 8)] * 2,
        scalars=1,
        arrays=5,
    )(arm, s4, y1, y2, coef, sums)

    got = lax.all_to_all(spread, "gy", 0, 0)
    xlow, xhigh = along_x(junction, 8)
    y1, y2 = along_y(*pack(JUNC_REACH, junction, xlow, xhigh))
    dens, wide, e1, e2, spread = call(
        outer_first,
        (own, wide_shape, mid, mid, tiles(size_gx)),
        [scratch(16 + BX, 8 + BY)] * 2,
        scalars=1,
        arrays=12,
    )(arm, junction, xlow, xhigh, y1, y2, coef, s4, s5, s6, s7, s8, got)
    got = lax.all_to_all(spread, "gx", 0, 0)
    y1, y2 = along_y(e1, e2)
    out = call(
        outer_second,
        jax.ShapeDtypeStruct((arms, 4 * n + 8, LANES), jnp.float32),
        [scratch(BX + 8, BY + 8)] * 2 + [pltpu.VMEM((8 * n, LANES), jnp.float32)] * 2,
        scalars=2,
        arrays=8,
    )(arm, flory_chi, wide, y1, y2, coef, s2, s3, dens, got)

    back = lax.all_to_all(out, "arm", 0, 0)
    result = jax.ShapeDtypeStruct(field_here.shape, jnp.float32)
    field_out, volume = call(
        functools.partial(finish, cell_count), (result, result), scalars=2, arrays=2
    )(arm, flory_chi, back, field_here)
    return (field_out[None], volume[None])


def solution(mesh):
    placed = (P("arm", "gx", "gy", None), P())
    return jax.shard_map(
        local,
        mesh=mesh,
        in_specs=placed,
        out_specs=(P("arm", "gx", "gy", None), P("arm", "gx", "gy", None)),
        check_vma=False,
    )
```

time: 1280 us -> 175 us (0.14)
  the two profiles are of different devices: /device:TPU:32 before, /device:TPU:6 now
where the time goes in v2:
time: 175 us; the launch traced here: 174 us
  blocking collectives  73.8 us (42%)
  starting transfers between devices  42.4 us (24%)
  waiting for transfers between devices  40.3 us (23%)
  Pallas kernels  15.7 us (9%)
    ppermute x4, starting transfers between devices, along_y(): lax.ppermute(second, ('arm', 'gy'), second_pairs)  28.2 us
    all_to_all x1, blocking collectives, local(): back = lax.all_to_all(out, 'arm', 0, 0)  27.1 us
    ppermute x4, waiting for transfers between devices, along_y(): lax.ppermute(second, ('arm', 'gy'), second_pairs)  21.4 us
    all_to_all x1, blocking collectives, local(): recv = lax.all_to_all(payload.reshape(arms, 2 * n, LANES), 'arm', 0, 0)  20.2 us
    all_to_all x1, blocking collectives, local(): got = lax.all_to_all(spread, 'gy', 0, 0)  18.8 us
    ppermute x4, waiting for transfers between devices, along_y(): lax.ppermute(first, ('arm', 'gy'), first_pairs)  12.4 us
    ppermute x4, starting transfers between devices, along_y(): lax.ppermute(first, ('arm', 'gy'), first_pairs)  11.9 us
    all_to_all x1, blocking collectives, local(): got = lax.all_to_all(spread, 'gx', 0, 0)  7.69 us
  transfers between devices with their start and end apart: 12, of which 10 were waited for; matrix products, arithmetic and copies ran while one was open for 0% of the time, Pallas kernels for 0%

profile of v2, /device:TPU:6, one launch (start us, length us, event | category | flops | bytes accessed | tf_op | source)
XLA Modules:
  0.0 174.5 jit_solution(14405286460287570782)
XLA Ops:
  0.6 1.3 reshape_squeeze.3
  1.9 0.1 copy.4
  2.1 20.2 %all_to_all.20.recv = f32[4,256,128]{2,1,0:T(8,128)S(1)} all-to-all(f32[4,256,128]{2,1,0:T(8,128)S(1)} %bitcast.15), channel_id=1, replica_groups=mesh['arm'=4,'gx'=8,'gy'=16] {'arm'}, dimensions={0} | all-to-all | bytes 1048576 | tf_op jit(solution)/shard_map/all_to_all | solution.py:301
  22.3 0.2 shard_map.41
  22.5 0.0 collective-permute-start
  22.5 1.7 collective-permute-start.1
  24.2 2.5 %collective-permute-done.low.xlow = f32[7,4,8,128]{3,2,1,0:T(8,128)S(1)} collective-permute-done((f32[7,4,8,128]{3,2,1,0:T(8,128)S(1)}, f32[7,4,8,128]{3,2,1,0:T(8,128)S(1)}, u32[]{:S(2)}, u32[]{:S(2)}) %collective-permute-start) | collective-permute-done | bytes 114720 | tf_op jit(solution)/shard_map/ppermute | solution.py:291
  26.7 0.0 collective-permute-done.1.high.xhigh
  26.7 0.1 shard_map.42
  26.8 2.1 %collective-permute-start.2 = (f32[126,8,128]{2,1,0:T(8,128)S(1)}, f32[126,8,128]{2,1,0:T(8,128)S(1)}, u32[]{:S(2)}, u32[]{:S(2)}) collective-permute-start(f32[126,8,128]{2,1,0:T(8,128)S(1)} %get-tuple-element.28), channel_id=1, source_target_pairs={{0,128},{128,0},{256,384},{384,256},{1,129},{129,1},{257,385},{385... | collective-permute-start | bytes 1548296 | tf_op jit(solution)/shard_map/ppermute | solution.py:285
  28.9 10.7 %collective-permute-start.3 = (f32[126,8,128]{2,1,0:T(8,128)S(1)}, f32[126,8,128]{2,1,0:T(8,128)S(1)}, u32[]{:S(2)}, u32[]{:S(2)}) collective-permute-start(f32[126,8,128]{2,1,0:T(8,128)S(1)} %get-tuple-element.29), channel_id=1, source_target_pairs={{0,399},{128,256},{256,128},{384,1},{1,384},{129,257},{257,129},{3... | collective-permute-start | bytes 1548296 | tf_op jit(solution)/shard_map/ppermute | solution.py:286
  39.6 2.9 %collective-permute-done.2.y1 = f32[126,8,128]{2,1,0:T(8,128)S(1)} collective-permute-done((f32[126,8,128]{2,1,0:T(8,128)S(1)}, f32[126,8,128]{2,1,0:T(8,128)S(1)}, u32[]{:S(2)}, u32[]{:S(2)}) %collective-permute-start.2) | collective-permute-done | bytes 516128 | tf_op jit(solution)/shard_map/ppermute | solution.py:285
  42.4 8.8 %collective-permute-done.3.y2 = f32[126,8,128]{2,1,0:T(8,128)S(1)} collective-permute-done((f32[126,8,128]{2,1,0:T(8,128)S(1)}, f32[126,8,128]{2,1,0:T(8,128)S(1)}, u32[]{:S(2)}, u32[]{:S(2)}) %collective-permute-start.3) | collective-permute-done | bytes 516128 | tf_op jit(solution)/shard_map/ppermute | solution.py:286
  51.3 2.5 %shard_map.43 = (f32[46,10,8,128]{3,2,1,0:T(8,128)S(1)}, f32[32,4,8,128]{3,2,1,0:T(8,128)S(1)}, f32[32,4,8,128]{3,2,1,0:T(8,128)S(1)}, f32[40,4,8,128]{3,2,1,0:T...) custom-call(s32[1]{0:T(128)} %bitcast.arm, f32[32,4,8,128]{3,2,1,0:T(8,128)S(1)} %bitcast.13, ...), custom_call_target="tpu_custom_call" | custom-call | tf_op jit(solution)/shard_map/pallas_call | solution.py:313
  53.7 1.9 %collective-permute-start.4 = (f32[140,8,128]{2,1,0:T(8,128)S(1)}, f32[140,8,128]{2,1,0:T(8,128)S(1)}, u32[]{:S(2)}, u32[]{:S(2)}) collective-permute-start(f32[140,8,128]{2,1,0:T(8,128)S(1)} %get-tuple-element.31), channel_id=1, source_target_pairs={{0,128},{128,0},{256,384},{384,256},{1,129},{129,1},{257,385},{385... | collective-permute-start | bytes 1720328 | tf_op jit(solution)/shard_map/ppermute | solution.py:285
  55.7 7.5 %collective-permute-start.5 = (f32[140,8,128]{2,1,0:T(8,128)S(1)}, f32[140,8,128]{2,1,0:T(8,128)S(1)}, u32[]{:S(2)}, u32[]{:S(2)}) collective-permute-start(f32[140,8,128]{2,1,0:T(8,128)S(1)} %get-tuple-element.32), channel_id=1, source_target_pairs={{0,399},{128,256},{256,128},{384,1},{1,384},{129,257},{257,129},{3... | collective-permute-start | bytes 1720328 | tf_op jit(solution)/shard_map/ppermute | solution.py:286
  63.2 8.0 %collective-permute-done.4.y1 = f32[140,8,128]{2,1,0:T(8,128)S(1)} collective-permute-done((f32[140,8,128]{2,1,0:T(8,128)S(1)}, f32[140,8,128]{2,1,0:T(8,128)S(1)}, u32[]{:S(2)}, u32[]{:S(2)}) %collective-permute-start.4) | collective-permute-done | bytes 573472 | tf_op jit(solution)/shard_map/ppermute | solution.py:285
  71.2 5.5 %collective-permute-done.5.y2 = f32[140,8,128]{2,1,0:T(8,128)S(1)} collective-permute-done((f32[140,8,128]{2,1,0:T(8,128)S(1)}, f32[140,8,128]{2,1,0:T(8,128)S(1)}, u32[]{:S(2)}, u32[]{:S(2)}) %collective-permute-start.5) | collective-permute-done | bytes 573472 | tf_op jit(solution)/shard_map/ppermute | solution.py:286
  76.8 3.1 %shard_map.44 = (f32[32,4,8,128]{3,2,1,0:T(8,128)S(1)}, f32[32,4,8,128]{3,2,1,0:T(8,128)S(1)}, f32[32,4,8,128]{3,2,1,0:T(8,128)S(1)}, f32[32,4,8,128]{3,2,1,0:T(...) custom-call(s32[1]{0:T(128)} %bitcast.arm, f32[40,4,8,128]{3,2,1,0:T(8,128)S(1)} %get-tuple-element.30.wide.s4, ...), custom_call_target="tpu_custom_call" | custom-call | tf_op jit(solution)/shard_map/pallas_call | solution.py:321
  79.9 0.1 collective-permute-start.7
  80.0 0.4 collective-permute-start.6
  80.4 2.1 %collective-permute-done.7.high.xhigh = f32[8,4,8,128]{3,2,1,0:T(8,128)S(1)} collective-permute-done((f32[8,4,8,128]{3,2,1,0:T(8,128)S(1)}, f32[8,4,8,128]{3,2,1,0:T(8,128)S(1)}, u32[]{:S(2)}, u32[]{:S(2)}) %collective-permute-start.7) | collective-permute-done | bytes 131104 | tf_op jit(solution)/shard_map/ppermute | solution.py:292
  82.6 1.9 %collective-permute-done.6.low.xlow = f32[8,4,8,128]{3,2,1,0:T(8,128)S(1)} collective-permute-done((f32[8,4,8,128]{3,2,1,0:T(8,128)S(1)}, f32[8,4,8,128]{3,2,1,0:T(8,128)S(1)}, u32[]{:S(2)}, u32[]{:S(2)}) %collective-permute-start.6) | collective-permute-done | bytes 131104 | tf_op jit(solution)/shard_map/ppermute | solution.py:291
  84.4 0.1 shard_map.45
  84.5 1.9 %collective-permute-start.8 = (f32[172,8,128]{2,1,0:T(8,128)S(1)}, f32[172,8,128]{2,1,0:T(8,128)S(1)}, u32[]{:S(2)}, u32[]{:S(2)}) collective-permute-start(f32[172,8,128]{2,1,0:T(8,128)S(1)} %get-tuple-element.36), channel_id=1, source_target_pairs={{0,128},{128,0},{256,384},{384,256},{1,129},{129,1},{257,385},{385... | collective-permute-start | bytes 2113544 | tf_op jit(solution)/shard_map/ppermute | solution.py:285
  86.5 6.8 %collective-permute-start.9 = (f32[172,8,128]{2,1,0:T(8,128)S(1)}, f32[172,8,128]{2,1,0:T(8,128)S(1)}, u32[]{:S(2)}, u32[]{:S(2)}) collective-permute-start(f32[172,8,128]{2,1,0:T(8,128)S(1)} %get-tuple-element.37), channel_id=1, source_target_pairs={{0,399},{128,256},{256,128},{384,1},{1,384},{129,257},{257,129},{3... | collective-permute-start | bytes 2113544 | tf_op jit(solution)/shard_map/ppermute | solution.py:286
  93.3 18.8 %all_to_all.21.got = f32[16,8,128]{2,1,0:T(8,128)S(1)} all-to-all(f32[16,8,128]{2,1,0:T(8,128)S(1)} %get-tuple-element.42), channel_id=1, replica_groups=mesh['arm'=4,'gx'=8,'gy'=16] {'gy'}, dimensions={0} | all-to-all | bytes 131072 | tf_op jit(solution)/shard_map/all_to_all | solution.py:329
  112.1 0.0 collective-permute-done.8.y1
  112.1 0.4 collective-permute-done.9.y2
  112.5 0.0 copy-start.1
  112.5 3.9 %shard_map.46 = (f32[32,4,8,128]{3,2,1,0:T(8,128)S(1)}, f32[40,4,8,128]{3,2,1,0:T(8,128)S(1)}, f32[140,8,128]{2,1,0:T(8,128)S(1)}, f32[140,8,128]{2,1,0:T(8,128)S(1)}, f32[8,8,128]{2,1,0:T(8,128)S(1)}) custom-call(s32[1]{0:T(128)} %bitcast.arm, f32[32,4,8,128]{3,2,1,0:T(8,128)S(1)} %get-tuple-element.35.own, ...), custom_call_target="tpu_custom_call" | custom-call | tf_op jit(solution)/shard_map/pallas_call | solution.py:332
  116.4 5.9 %collective-permute-start.10 = (f32[140,8,128]{2,1,0:T(8,128)S(1)}, f32[140,8,128]{2,1,0:T(8,128)S(1)}, u32[]{:S(2)}, u32[]{:S(2)}) collective-permute-start(f32[140,8,128]{2,1,0:T(8,128)S(1)} %get-tuple-element.44), channel_id=1, source_target_pairs={{0,128},{128,0},{256,384},{384,256},{1,129},{129,1},{257,385},{385... | collective-permute-start | bytes 1720328 | tf_op jit(solution)/shard_map/ppermute | solution.py:285
  122.4 3.1 %collective-permute-start.11 = (f32[140,8,128]{2,1,0:T(8,128)S(1)}, f32[140,8,128]{2,1,0:T(8,128)S(1)}, u32[]{:S(2)}, u32[]{:S(2)}) collective-permute-start(f32[140,8,128]{2,1,0:T(8,128)S(1)} %get-tuple-element.45), channel_id=1, source_target_pairs={{0,399},{128,256},{256,128},{384,1},{1,384},{129,257},{257,129},{3... | collective-permute-start | bytes 1720328 | tf_op jit(solution)/shard_map/ppermute | solution.py:286
  125.5 7.7 %all_to_all.22.got = f32[8,8,128]{2,1,0:T(8,128)S(1)} all-to-all(f32[8,8,128]{2,1,0:T(8,128)S(1)} %get-tuple-element.49), channel_id=1, replica_groups=mesh['arm'=4,'gx'=8,'gy'=16] {'gx'}, dimensions={0} | all-to-all | bytes 65536 | tf_op jit(solution)/shard_map/all_to_all | solution.py:339
  133.2 1.5 collective-permute-done.10.y1
  134.7 6.7 %collective-permute-done.11.y2 = f32[140,8,128]{2,1,0:T(8,128)S(1)} collective-permute-done((f32[140,8,128]{2,1,0:T(8,128)S(1)}, f32[140,8,128]{2,1,0:T(8,128)S(1)}, u32[]{:S(2)}, u32[]{:S(2)}) %collective-permute-start.11) | collective-permute-done | bytes 573472 | tf_op jit(solution)/shard_map/ppermute | solution.py:286
  141.4 0.0 copy-done.1
  141.4 4.0 %shard_map.47 = f32[4,520,128]{2,1,0:T(8,128)S(1)} custom-call(s32[1]{0:T(128)} %bitcast.arm, f32[4,4]{1,0:T(4,128)S(1)} %copy-done.1, f32[40,4,8,128]{3,2,1,0:T(8,128)S(1)} %get-tuple-element.43.wide, f32[140,8,128]{2,1,0:T(8,128)S(1)} %collective-permute-done.10.y1, f32[140,8,128]{2,1,0:T(8,128)S(1)} %collective-permute-done.11.y2, ...), custom_call_target="tpu_custom_call" | custom-call | tf_op jit(solution)/shard_map/pallas_call | solution.py:341
  145.4 0.0 copy-start
  145.4 27.1 %all_to_all.23.back = f32[4,520,128]{2,1,0:T(8,128)S(1)} all-to-all(f32[4,520,128]{2,1,0:T(8,128)S(1)} %shard_map.47), channel_id=1, replica_groups=mesh['arm'=4,'gx'=8,'gy'=16] {'arm'}, dimensions={0} | all-to-all | bytes 2129920 | tf_op jit(solution)/shard_map/all_to_all | solution.py:349
  172.5 0.0 copy-done
  172.5 2.0 %shard_map.48 = (f32[32,16,256]{2,1,0:T(8,128)}, f32[32,16,256]{2,1,0:T(8,128)}) custom-call(s32[1]{0:T(128)} %bitcast.arm, f32[4,4]{1,0:T(4,128)S(1)} %copy-done.1, f32[4,520,128]{2,1,0:T(8,128)S(1)} %all_to_all.23.back, f32[32,16,256]{2,1,0:T(8,128)S(1)} %bitcast.14), custom_call_target="tpu_custom_call" | custom-call | tf_op jit(solution)/shard_map/pallas_call | solution.py:351
  (2 shorter events, 0.0 us)
Async XLA Ops:
  22.5 4.2 %collective-permute-start = (f32[7,4,8,128]{3,2,1,0:T(8,128)S(1)}, f32[7,4,8,128]{3,2,1,0:T(8,128)S(1)}, u32[]{:S(2)}, u32[]{:S(2)}) collective-permute-start(f32[7,4,8,128]{3,2,1,0:T(8,128)S(1)} %bitcast.17), channel_id=1, source_target_pairs={{0,16},{16,32},{32,48},{48,64},{64,80},{80,96},{96,112},{112,0},{1... | collective-permute-start | bytes 344072 | tf_op jit(solution)/shard_map/ppermute | solution.py:291
  22.5 4.2 %collective-permute-start.1 = (f32[7,4,8,128]{3,2,1,0:T(8,128)S(1)}, f32[7,4,8,128]{3,2,1,0:T(8,128)S(1)}, u32[]{:S(2)}, u32[]{:S(2)}) collective-permute-start(f32[7,4,8,128]{3,2,1,0:T(8,128)S(1)} %bitcast.16), channel_id=1, source_target_pairs={{0,112},{16,0},{32,16},{48,32},{64,48},{80,64},{96,80},{112,96},{1... | collective-permute-start | bytes 344072 | tf_op jit(solution)/shard_map/ppermute | solution.py:292
  26.8 15.7 %collective-permute-start.2 = (f32[126,8,128]{2,1,0:T(8,128)S(1)}, f32[126,8,128]{2,1,0:T(8,128)S(1)}, u32[]{:S(2)}, u32[]{:S(2)}) collective-permute-start(f32[126,8,128]{2,1,0:T(8,128)S(1)} %get-tuple-element.28), channel_id=1, source_target_pairs={{0,128},{128,0},{256,384},{384,256},{1,129},{129,1},{257,385},{385... | collective-permute-start | bytes 1548296 | tf_op jit(solution)/shard_map/ppermute | solution.py:285
  28.9 22.4 %collective-permute-start.3 = (f32[126,8,128]{2,1,0:T(8,128)S(1)}, f32[126,8,128]{2,1,0:T(8,128)S(1)}, u32[]{:S(2)}, u32[]{:S(2)}) collective-permute-start(f32[126,8,128]{2,1,0:T(8,128)S(1)} %get-tuple-element.29), channel_id=1, source_target_pairs={{0,399},{128,256},{256,128},{384,1},{1,384},{129,257},{257,129},{3... | collective-permute-start | bytes 1548296 | tf_op jit(solution)/shard_map/ppermute | solution.py:286
  53.7 17.5 %collective-permute-start.4 = (f32[140,8,128]{2,1,0:T(8,128)S(1)}, f32[140,8,128]{2,1,0:T(8,128)S(1)}, u32[]{:S(2)}, u32[]{:S(2)}) collective-permute-start(f32[140,8,128]{2,1,0:T(8,128)S(1)} %get-tuple-element.31), channel_id=1, source_target_pairs={{0,128},{128,0},{256,384},{384,256},{1,129},{129,1},{257,385},{385... | collective-permute-start | bytes 1720328 | tf_op jit(solution)/shard_map/ppermute | solution.py:285
  55.7 21.1 %collective-permute-start.5 = (f32[140,8,128]{2,1,0:T(8,128)S(1)}, f32[140,8,128]{2,1,0:T(8,128)S(1)}, u32[]{:S(2)}, u32[]{:S(2)}) collective-permute-start(f32[140,8,128]{2,1,0:T(8,128)S(1)} %get-tuple-element.32), channel_id=1, source_target_pairs={{0,399},{128,256},{256,128},{384,1},{1,384},{129,257},{257,129},{3... | collective-permute-start | bytes 1720328 | tf_op jit(solution)/shard_map/ppermute | solution.py:286
  79.9 2.7 %collective-permute-start.7 = (f32[8,4,8,128]{3,2,1,0:T(8,128)S(1)}, f32[8,4,8,128]{3,2,1,0:T(8,128)S(1)}, u32[]{:S(2)}, u32[]{:S(2)}) collective-permute-start(f32[8,4,8,128]{3,2,1,0:T(8,128)S(1)} %get-tuple-element.52), channel_id=1, source_target_pairs={{0,112},{16,0},{32,16},{48,32},{64,48},{80,64},{96,80},{112,96},{1... | collective-permute-start | bytes 393224 | tf_op jit(solution)/shard_map/ppermute | solution.py:292
  80.0 4.4 %collective-permute-start.6 = (f32[8,4,8,128]{3,2,1,0:T(8,128)S(1)}, f32[8,4,8,128]{3,2,1,0:T(8,128)S(1)}, u32[]{:S(2)}, u32[]{:S(2)}) collective-permute-start(f32[8,4,8,128]{3,2,1,0:T(8,128)S(1)} %get-tuple-element.53), channel_id=1, source_target_pairs={{0,16},{16,32},{32,48},{48,64},{64,80},{80,96},{96,112},{112,0},{1... | collective-permute-start | bytes 393224 | tf_op jit(solution)/shard_map/ppermute | solution.py:291
  84.5 27.6 %collective-permute-start.8 = (f32[172,8,128]{2,1,0:T(8,128)S(1)}, f32[172,8,128]{2,1,0:T(8,128)S(1)}, u32[]{:S(2)}, u32[]{:S(2)}) collective-permute-start(f32[172,8,128]{2,1,0:T(8,128)S(1)} %get-tuple-element.36), channel_id=1, source_target_pairs={{0,128},{128,0},{256,384},{384,256},{1,129},{129,1},{257,385},{385... | collective-permute-start | bytes 2113544 | tf_op jit(solution)/shard_map/ppermute | solution.py:285
  86.5 26.0 %collective-permute-start.9 = (f32[172,8,128]{2,1,0:T(8,128)S(1)}, f32[172,8,128]{2,1,0:T(8,128)S(1)}, u32[]{:S(2)}, u32[]{:S(2)}) collective-permute-start(f32[172,8,128]{2,1,0:T(8,128)S(1)} %get-tuple-element.37), channel_id=1, source_target_pairs={{0,399},{128,256},{256,128},{384,1},{1,384},{129,257},{257,129},{3... | collective-permute-start | bytes 2113544 | tf_op jit(solution)/shard_map/ppermute | solution.py:286
  112.5 28.9 %copy-start.1 = (f32[4,4]{1,0:T(4,128)S(1)}, f32[4,4]{1,0:T(4,128)}, u32[]{:S(2)}) copy-start(f32[4,4]{1,0:T(4,128)} %chi.3) | copy-start | bytes 196
  116.4 18.3 %collective-permute-start.10 = (f32[140,8,128]{2,1,0:T(8,128)S(1)}, f32[140,8,128]{2,1,0:T(8,128)S(1)}, u32[]{:S(2)}, u32[]{:S(2)}) collective-permute-start(f32[140,8,128]{2,1,0:T(8,128)S(1)} %get-tuple-element.44), channel_id=1, source_target_pairs={{0,128},{128,0},{256,384},{384,256},{1,129},{129,1},{257,385},{385... | collective-permute-start | bytes 1720328 | tf_op jit(solution)/shard_map/ppermute | solution.py:285
  122.4 19.0 %collective-permute-start.11 = (f32[140,8,128]{2,1,0:T(8,128)S(1)}, f32[140,8,128]{2,1,0:T(8,128)S(1)}, u32[]{:S(2)}, u32[]{:S(2)}) collective-permute-start(f32[140,8,128]{2,1,0:T(8,128)S(1)} %get-tuple-element.45), channel_id=1, source_target_pairs={{0,399},{128,256},{256,128},{384,1},{1,384},{129,257},{257,129},{3... | collective-permute-start | bytes 1720328 | tf_op jit(solution)/shard_map/ppermute | solution.py:286
  145.4 27.1 %copy-start = (f32[1,32,16,256]{3,2,1,0:T(8,128)S(1)}, f32[1,32,16,256]{3,2,1,0:T(8,128)}, u32[]{:S(2)}) copy-start(f32[1,32,16,256]{3,2,1,0:T(8,128)} %param.2) | copy-start | bytes 1572868

commit v3 on v2

--- a/solution.py
+++ b/solution.py
@@ -30,6 +30,10 @@
 
 def packed_size(reach):
     return sum(BX + 2 * r for r in reach)
+
+
+def side_size(reach):
+    return BY * (reach[0] + 1) + 2 * sum(reach)
 
 
 def lane_masks():
@@ -51,7 +55,7 @@
     dst[x0:x1, y0:y1] = total + (up + down) + coef[x0 + dx : x1 + dx, y0 + dy : y1 + dy] * v
 
 
-def interleave_kernel(recv, coef, sums):
+def interleave_kernel(arm, recv, coef, sums, first, second):
     n = BX * BY
     for s in range(SPECIES):
         for half in range(2):
@@ -61,6 +65,14 @@
         sums[s : s + 1, :] = jnp.sum(recv[s], axis=0, keepdims=True)
     sums[4:8, :] = jnp.zeros((4, LANES), jnp.float32)
 
+    def body(up, down):
+        cells = coef[...].reshape(BX, BY, 8, LANES)
+        for j in range(len(COEF_REACH)):
+            up[:, j] = cells[:, j]
+            down[:, BY - 2 - j] = cells[:, BY - 1 - j]
+
+    by_side(arm, first, second, body)
+
 
 def by_side(arm, first, second, body):
     odd = arm[0] % 2
@@ -74,17 +86,50 @@
         body(first, second)
 
 
-def pack_kernel(reach, arm, own, low, high, first, second):
-    edge = low.shape[0]
-
-    def body(up, down):
-        offset = 0
+def pack_sides(reach, arm, own, first, second, *rest):
+    if len(rest) == 4:
+        got, left, right, spread = rest
+        spread[...] = jnp.broadcast_to(jnp.sum(got[...], axis=0), spread.shape)
+    else:
+        left, right = rest
+    width, depth = reach[0] + 1, len(reach)
+
+    def put(at, src, y, r):
+        left[at : at + r] = src[0:r, y]
+        right[at : at + r] = src[BX - r : BX, y]
+        return at + r
+
+    def body(low, high):
+        at = 0
+        for y in range(BY):
+            at = put(at, own, y, width)
         for j, r in enumerate(reach):
-            for dst, y in ((up, j), (down, BY - 1 - j)):
-                dst[offset : offset + r] = low[edge - r : edge, y]
-                dst[offset + r : offset + r + BX] = own[:, y]
-                dst[offset + r + BX : offset + 2 * r + BX] = high[0:r, y]
-            offset += BX + 2 * r
+            at = put(at, low, depth - 1 - j, r)
+            at = put(at, high, j, r)
+
+    by_side(arm, first, second, body)
+
+
+def surround(arm, dst, reach, own, first, second, xlow, xhigh, shift):
+    ox, oy = shift
+    width, depth = reach[0] + 1, len(reach)
+    dst[ox : ox + BX, oy : oy + BY] = own[...]
+
+    def put(at, y, r):
+        dst[ox - r : ox, y] = xlow[at : at + r]
+        dst[ox + BX : ox + BX + r, y] = xhigh[at : at + r]
+        return at + r
+
+    at = 0
+    for y in range(BY):
+        at = put(at, oy + y, width)
+    for j, r in enumerate(reach):
+        at = put(at, oy - 1 - j, r)
+        at = put(at, oy + BY + j, r)
+
+    def body(low, high):
+        dst[ox : ox + BX, oy - depth : oy] = low[...]
+        dst[ox : ox + BX, oy + BY : oy + BY + depth] = high[...]
 
     by_side(arm, first, second, body)
 
@@ -119,10 +164,7 @@
 
 
 def inner_first(arm, own, xlow, xhigh, y1, y2, coef, s2, s3, wide, e1, e2, a, b):
-    coef[7 : 7 + BX, 3:7] = own[...]
-    coef[0:7, 3:7] = xlow[...]
-    coef[7 + BX :, 3:7] = xhigh[...]
-    unpack(arm, coef, COEF_REACH, y1, y2, (7, 3))
+    surround(arm, coef, COEF_REACH, own, y1, y2, xlow, xhigh, (7, 3))
     here = (slice(7, 7 + BX), slice(3, 7))
     a[...] = 6.0 + coef[...]
     step(a, b, coef, (1, 45), (1, 9), (0, 0))
@@ -172,10 +214,7 @@
     dens, wide, e1, e2, spread, a, b
 ):
     spread[...] = jnp.broadcast_to(jnp.sum(got[...], axis=0), spread.shape)
-    a[8 : 8 + BX, 4:8] = own[...]
-    a[0:8, 4:8] = xlow[...]
-    a[8 + BX :, 4:8] = xhigh[...]
-    unpack(arm, a, JUNC_REACH, y1, y2, (8, 4))
+    surround(arm, a, JUNC_REACH, own, y1, y2, xlow, xhigh, (8, 4))
     here = (slice(8, 8 + BX), slice(4, 8))
     shift = (-1, -1)
     step(a, b, coef, (1, 47), (1, 11), shift)
@@ -286,27 +325,35 @@
             lax.ppermute(second, ("arm", "gy"), second_pairs),
         )
 
-    def along_x(array, width):
+    def along_x(left, right):
         m = size_gx
-        low = lax.ppermute(array[BX - width :], "gx", [(i, (i + 1) % m) for i in range(m)])
-        high = lax.ppermute(array[:width], "gx", [(i, (i - 1) % m) for i in range(m)])
+        low = lax.ppermute(right, "gx", [(i, (i + 1) % m) for i in range(m)])
+        high = lax.ppermute(left, "gx", [(i, (i - 1) % m) for i in range(m)])
         return low, high
 
-    def pack(reach, own, low, high):
-        kernel = functools.partial(pack_kernel, reach)
-        outs = (tiles(packed_size(reach)),) * 2
-        return call(kernel, outs, scalars=1, arrays=3)(arm, own, low, high)
+    parts = size_gy // arms
+    z_groups = [[y * parts + z for z in range(parts)] for y in range(size_gy // parts)]
+    y_groups = [list(g) for g in zip(*z_groups)]
+
+    def swap(spread, axis, groups=None):
+        return lax.all_to_all(spread, axis, 0, 0, axis_index_groups=groups)
 
     payload = field_here.reshape(BX, arms, BY, 2, LANES).transpose(1, 3, 0, 2, 4)
     recv = lax.all_to_all(payload.reshape(arms, 2 * n, LANES), "arm", 0, 0)
-    coef_flat, sums = call(
+    rows = tiles(BX, len(COEF_REACH))
+    coef_flat, sums, e1, e2 = call(
         interleave_kernel,
-        (jax.ShapeDtypeStruct((8 * n, LANES), jnp.float32), tiles()),
+        (jax.ShapeDtypeStruct((8 * n, LANES), jnp.float32), tiles(), rows, rows),
+        scalars=1,
         arrays=1,
-    )(recv)
+    )(arm, recv)
     coef_own = coef_flat.reshape(BX, BY, 8, LANES)
-    xlow, xhigh = along_x(coef_own, 7)
-    y1, y2 = along_y(*pack(COEF_REACH, coef_own, xlow, xhigh))
+    y1, y2 = along_y(e1, e2)
+    side = tiles(side_size(COEF_REACH))
+    left, right = call(
+        functools.partial(pack_sides, COEF_REACH), (side, side), scalars=1, arrays=3
+    )(arm, coef_own, y1, y2)
+    xlow, xhigh = along_x(left, right)
 
     own, wide_shape = tiles(BX, BY), tiles(BX + 8, BY)
     mid = tiles(packed_size(MID_REACH))
@@ -320,24 +367,32 @@
     y1, y2 = along_y(e1, e2)
     s5, s6, s7, s8, junction, spread = call(
         inner_second,
-        (own,) * 5 + (tiles(size_gy),),
+        (own,) * 5 + (tiles(size_gx),),
         [scratch(BX + 8, BY + 8)] * 2,
         scalars=1,
         arrays=5,
     )(arm, s4, y1, y2, coef, sums)
 
-    got = lax.all_to_all(spread, "gy", 0, 0)
-    xlow, xhigh = along_x(junction, 8)
-    y1, y2 = along_y(*pack(JUNC_REACH, junction, xlow, xhigh))
+    y1, y2 = along_y(junction, junction)
+    got = swap(spread, "gx")
+    side = tiles(side_size(JUNC_REACH))
+    left, right, spread = call(
+        functools.partial(pack_sides, JUNC_REACH),
+        (side, side, tiles(parts)),
+        scalars=1,
+        arrays=4,
+    )(arm, junction, y1, y2, got)
+    xlow, xhigh = along_x(left, right)
+    got = swap(spread, "gy", z_groups)
     dens, wide, e1, e2, spread = call(
         outer_first,
-        (own, wide_shape, mid, mid, tiles(size_gx)),
+        (own, wide_shape, mid, mid, tiles(len(z_groups))),
         [scratch(16 + BX, 8 + BY)] * 2,
         scalars=1,
         arrays=12,
     )(arm, junction, xlow, xhigh, y1, y2, coef, s4, s5, s6, s7, s8, got)
-    got = lax.all_to_all(spread, "gx", 0, 0)
     y1, y2 = along_y(e1, e2)
+    got = swap(spread, "gy", y_groups)
     out = call(
         outer_second,
         jax.ShapeDtypeStruct((arms, 4 * n + 8, LANES), jnp.float32),

time: 175 us -> 176 us (level)
  blocking collectives: 73.8 us -> 63.2 us
  waiting for transfers between devices: 40.3 us -> 46.9 us
  starting transfers between devices: 42.4 us -> 45.1 us
    all_to_all x0 -> x1, waiting for transfers between devices: none -> 14.5 us  [local(): recv = lax.all_to_all(payload.reshape(arms, 2 * n, LANES), 'arm', 0, 0)]
    all_to_all x3, blocking collectives: 46.7 us -> 37.4 us  [swap(): return lax.all_to_all(spread, axis, 0, 0, axis_index_groups=groups)]
    all_to_all x0 -> x1, starting transfers between devices: none -> 5.89 us  [local(): recv = lax.all_to_all(payload.reshape(arms, 2 * n, LANES), 'arm', 0, 0)]
    ppermute x4, waiting for transfers between devices: 21.4 us -> 17.3 us  [along_y(): lax.ppermute(second, ('arm', 'gy'), second_pairs)]
    ppermute x4, starting transfers between devices: 11.9 us -> 7.96 us  [along_y(): lax.ppermute(first, ('arm', 'gy'), first_pairs)]
    ppermute x4, waiting for transfers between devices: 6.49 us -> 3.8 us  [the longest x2 3.79 us: along_x(): low = lax.ppermute(right, 'gx', [(i, (i + 1) % m) for i in range(m)])]
  transfers between devices with their start and end apart: 12 -> 13, of which waited for: 10 -> 8; matrix products, arithmetic and copies ran while one was open for 0% -> 0% of each run, Pallas kernels for 0% -> 0%
where the time goes in v3:
time: 176 us; the launch traced here: 174 us
  blocking collectives  63.2 us (36%)
  waiting for transfers between devices  46.9 us (27%)
  starting transfers between devices  45.1 us (26%)
  Pallas kernels  15.8 us (9%)
  local copies, waits for them, and re-layouts  2.24 us (1%)
    all_to_all x3, blocking collectives, swap(): return lax.all_to_all(spread, axis, 0, 0, axis_index_groups=groups)  37.4 us
    ppermute x4, starting transfers between devices, along_y(): lax.ppermute(second, ('arm', 'gy'), second_pairs)  27.7 us
    all_to_all x1, blocking collectives, local(): back = lax.all_to_all(out, 'arm', 0, 0)  25.9 us
    ppermute x4, waiting for transfers between devices, along_y(): lax.ppermute(second, ('arm', 'gy'), second_pairs)  17.3 us
    all_to_all x1, waiting for transfers between devices, local(): recv = lax.all_to_all(payload.reshape(arms, 2 * n, LANES), 'arm', 0, 0)  14.5 us
    ppermute x4, waiting for transfers between devices, along_y(): lax.ppermute(first, ('arm', 'gy'), first_pairs)  11.4 us
    ppermute x4, starting transfers between devices, along_y(): lax.ppermute(first, ('arm', 'gy'), first_pairs)  7.96 us
    all_to_all x1, starting transfers between devices, local(): recv = lax.all_to_all(payload.reshape(arms, 2 * n, LANES), 'arm', 0, 0)  5.89 us
  transfers between devices with their start and end apart: 13, of which 8 were waited for; matrix products, arithmetic and copies ran while one was open for 0% of the time, Pallas kernels for 0%

profile of v3, /device:TPU:6, one launch (start us, length us, event | category | flops | bytes accessed | tf_op | source)
XLA Modules:
  0.0 174.1 jit_solution(2713401928606497556)
XLA Ops:
  0.6 1.3 reshape_squeeze.3
  1.9 0.9 copy.4
  2.9 5.9 %all-to-all-start = ((f32[4,256,128]{2,1,0:T(8,128)}), f32[4,256,128]{2,1,0:T(8,128)S(1)}, u32[]{:S(2)}, u32[]{:S(2)}) async-start(f32[4,256,128]{2,1,0:T(8,128)} %bitcast.2), calls=%async_computation | async-start | bytes 1048576 | tf_op jit(solution)/shard_map/all_to_all | solution.py:342
  8.8 14.5 %all-to-all-done.recv = f32[4,256,128]{2,1,0:T(8,128)S(1)} async-done(((f32[4,256,128]{2,1,0:T(8,128)}), f32[4,256,128]{2,1,0:T(8,128)S(1)}, u32[]{:S(2)}, u32[]{:S(2)}) %all-to-all-start) | async-done | bytes 524320 | tf_op jit(solution)/shard_map/all_to_all | solution.py:342
  23.2 0.2 shard_map.41
  23.5 1.9 %collective-permute-start = (f32[32,3,8,128]{3,2,1,0:T(8,128)S(1)}, f32[32,3,8,128]{3,2,1,0:T(8,128)S(1)}, u32[]{:S(2)}, u32[]{:S(2)}) collective-permute-start(f32[32,3,8,128]{3,2,1,0:T(8,128)S(1)} %get-tuple-element.31), channel_id=1, source_target_pairs={{0,128},{128,0},{256,384},{384,256},{1,129},{129,1},{257,385},{385... | collective-permute-start | bytes 1179656 | tf_op jit(solution)/shard_map/ppermute | solution.py:324
  25.4 11.2 %collective-permute-start.1 = (f32[32,3,8,128]{3,2,1,0:T(8,128)S(1)}, f32[32,3,8,128]{3,2,1,0:T(8,128)S(1)}, u32[]{:S(2)}, u32[]{:S(2)}) collective-permute-start(f32[32,3,8,128]{3,2,1,0:T(8,128)S(1)} %get-tuple-element.32), channel_id=1, source_target_pairs={{0,399},{128,256},{256,128},{384,1},{1,384},{129,257},{257,129},{3... | collective-permute-start | bytes 1179656 | tf_op jit(solution)/shard_map/ppermute | solution.py:325
  36.6 0.0 collective-permute-done.first.y1
  36.6 8.2 %collective-permute-done.1.second.y2 = f32[32,3,8,128]{3,2,1,0:T(8,128)S(1)} collective-permute-done((f32[32,3,8,128]{3,2,1,0:T(8,128)S(1)}, f32[32,3,8,128]{3,2,1,0:T(8,128)S(1)}, u32[]{:S(2)}, u32[]{:S(2)}) %collective-permute-start.1) | collective-permute-done | bytes 393248 | tf_op jit(solution)/shard_map/ppermute | solution.py:325
  44.9 0.0 collective-permute-start.2
  44.9 1.7 collective-permute-start.3
  46.7 3.8 %collective-permute-done.2.xlow = f32[58,8,128]{2,1,0:T(8,128)S(1)} collective-permute-done((f32[58,8,128]{2,1,0:T(8,128)S(1)}, f32[58,8,128]{2,1,0:T(8,128)S(1)}, u32[]{:S(2)}, u32[]{:S(2)}) %collective-permute-start.2) | collective-permute-done | bytes 237600 | tf_op jit(solution)/shard_map/ppermute | solution.py:330
  50.5 0.0 collective-permute-done.3.xhigh
  50.5 2.5 %shard_map.43 = (f32[46,10,8,128]{3,2,1,0:T(8,128)S(1)}, f32[32,4,8,128]{3,2,1,0:T(8,128)S(1)}, f32[32,4,8,128]{3,2,1,0:T(8,128)S(1)}, f32[40,4,8,128]{3,2,1,0:T...) custom-call(s32[1]{0:T(128)} %bitcast.arm, f32[32,4,8,128]{3,2,1,0:T(8,128)S(1)} %bitcast.12, ...), custom_call_target="tpu_custom_call" | custom-call | tf_op jit(solution)/shard_map/pallas_call | solution.py:360
  52.9 1.9 %collective-permute-start.4 = (f32[140,8,128]{2,1,0:T(8,128)S(1)}, f32[140,8,128]{2,1,0:T(8,128)S(1)}, u32[]{:S(2)}, u32[]{:S(2)}) collective-permute-start(f32[140,8,128]{2,1,0:T(8,128)S(1)} %get-tuple-element.36), channel_id=1, source_target_pairs={{0,128},{128,0},{256,384},{384,256},{1,129},{129,1},{257,385},{385... | collective-permute-start | bytes 1720328 | tf_op jit(solution)/shard_map/ppermute | solution.py:324
  54.8 7.0 %collective-permute-start.5 = (f32[140,8,128]{2,1,0:T(8,128)S(1)}, f32[140,8,128]{2,1,0:T(8,128)S(1)}, u32[]{:S(2)}, u32[]{:S(2)}) collective-permute-start(f32[140,8,128]{2,1,0:T(8,128)S(1)} %get-tuple-element.37), channel_id=1, source_target_pairs={{0,399},{128,256},{256,128},{384,1},{1,384},{129,257},{257,129},{3... | collective-permute-start | bytes 1720328 | tf_op jit(solution)/shard_map/ppermute | solution.py:325
  61.8 8.0 %collective-permute-done.4.y1 = f32[140,8,128]{2,1,0:T(8,128)S(1)} collective-permute-done((f32[140,8,128]{2,1,0:T(8,128)S(1)}, f32[140,8,128]{2,1,0:T(8,128)S(1)}, u32[]{:S(2)}, u32[]{:S(2)}) %collective-permute-start.4) | collective-permute-done | bytes 573472 | tf_op jit(solution)/shard_map/ppermute | solution.py:324
  69.8 5.2 %collective-permute-done.5.y2 = f32[140,8,128]{2,1,0:T(8,128)S(1)} collective-permute-done((f32[140,8,128]{2,1,0:T(8,128)S(1)}, f32[140,8,128]{2,1,0:T(8,128)S(1)}, u32[]{:S(2)}, u32[]{:S(2)}) %collective-permute-start.5) | collective-permute-done | bytes 573472 | tf_op jit(solution)/shard_map/ppermute | solution.py:325
  75.1 3.1 %shard_map.44 = (f32[32,4,8,128]{3,2,1,0:T(8,128)S(1)}, f32[32,4,8,128]{3,2,1,0:T(8,128)S(1)}, f32[32,4,8,128]{3,2,1,0:T(8,128)S(1)}, f32[32,4,8,128]{3,2,1,0:T(...) custom-call(s32[1]{0:T(128)} %bitcast.arm, f32[40,4,8,128]{3,2,1,0:T(8,128)S(1)} %get-tuple-element.35.wide.s4, ...), custom_call_target="tpu_custom_call" | custom-call | tf_op jit(solution)/shard_map/pallas_call | solution.py:368
  78.2 7.0 %collective-permute-start.7 = (f32[32,4,8,128]{3,2,1,0:T(8,128)S(1)}, f32[32,4,8,128]{3,2,1,0:T(8,128)S(1)}, u32[]{:S(2)}, u32[]{:S(2)}) collective-permute-start(f32[32,4,8,128]{3,2,1,0:T(8,128)S(1)} %get-tuple-element.40.own), channel_id=1, source_target_pairs={{0,399},{128,256},{256,128},{384,1},{1,384},{129,257},{257,129},{3... | collective-permute-start | bytes 1572872 | tf_op jit(solution)/shard_map/ppermute | solution.py:325
  85.1 1.9 %collective-permute-start.6 = (f32[32,4,8,128]{3,2,1,0:T(8,128)S(1)}, f32[32,4,8,128]{3,2,1,0:T(8,128)S(1)}, u32[]{:S(2)}, u32[]{:S(2)}) collective-permute-start(f32[32,4,8,128]{3,2,1,0:T(8,128)S(1)} %get-tuple-element.40.own), channel_id=1, source_target_pairs={{0,128},{128,0},{256,384},{384,256},{1,129},{129,1},{257,385},{385... | collective-permute-start | bytes 1572872 | tf_op jit(solution)/shard_map/ppermute | solution.py:324
  87.1 8.4 %all_to_all.25.rest_0_ = f32[8,8,128]{2,1,0:T(8,128)S(1)} all-to-all(f32[8,8,128]{2,1,0:T(8,128)S(1)} %get-tuple-element.41), channel_id=1, replica_groups=mesh['arm'=4,'gx'=8,'gy'=16] {'gx'}, dimensions={0} | all-to-all | bytes 65536 | tf_op jit(solution)/shard_map/all_to_all | solution.py:339
  95.5 2.4 %collective-permute-done.7.second.y2 = f32[32,4,8,128]{3,2,1,0:T(8,128)S(1)} collective-permute-done((f32[32,4,8,128]{3,2,1,0:T(8,128)S(1)}, f32[32,4,8,128]{3,2,1,0:T(8,128)S(1)}, u32[]{:S(2)}, u32[]{:S(2)}) %collective-permute-start.7) | collective-permute-done | bytes 524320 | tf_op jit(solution)/shard_map/ppermute | solution.py:325
  97.9 3.4 %collective-permute-done.6.first.y1 = f32[32,4,8,128]{3,2,1,0:T(8,128)S(1)} collective-permute-done((f32[32,4,8,128]{3,2,1,0:T(8,128)S(1)}, f32[32,4,8,128]{3,2,1,0:T(8,128)S(1)}, u32[]{:S(2)}, u32[]{:S(2)}) %collective-permute-start.6) | collective-permute-done | bytes 524320 | tf_op jit(solution)/shard_map/ppermute | solution.py:324
  101.3 0.0 collective-permute-start.8
  101.3 1.7 collective-permute-start.9
  103.1 14.9 %all_to_all.26.got = f32[4,8,128]{2,1,0:T(8,128)S(1)} all-to-all(f32[4,8,128]{2,1,0:T(8,128)S(1)} %get-tuple-element.48), channel_id=1, replica_groups={{0,1,2,3},{4,5,6,7},{8,9,10,11},{12,13,14,15},{16,17,18,19},{20,21,22,2..., dimensions={0} | all-to-all | bytes 32768 | tf_op jit(solution)/shard_map/all_to_all | solution.py:339
  118.0 0.0 collective-permute-done.8.xlow
  118.0 0.0 collective-permute-done.9.xhigh
  118.0 0.0 copy-start.1
  118.0 3.8 %shard_map.46 = (f32[32,4,8,128]{3,2,1,0:T(8,128)S(1)}, f32[40,4,8,128]{3,2,1,0:T(8,128)S(1)}, f32[140,8,128]{2,1,0:T(8,128)S(1)}, f32[140,8,128]{2,1,0:T(8,128)S(1)}, f32[4,8,128]{2,1,0:T(8,128)S(1)}) custom-call(s32[1]{0:T(128)} %bitcast.arm, f32[32,4,8,128]{3,2,1,0:T(8,128)S(1)} %get-tuple-element.40.own, f32[76,8,128]{2,1,0:T(8,128)S(1)} %collective-permute-done.8.xlow, ...), custom_call_target="tpu_custom_call" | custom-call | tf_op jit(solution)/shard_map/pallas_call | solution.py:387
  121.8 2.2 %collective-permute-start.10 = (f32[140,8,128]{2,1,0:T(8,128)S(1)}, f32[140,8,128]{2,1,0:T(8,128)S(1)}, u32[]{:S(2)}, u32[]{:S(2)}) collective-permute-start(f32[140,8,128]{2,1,0:T(8,128)S(1)} %get-tuple-element.50), channel_id=1, source_target_pairs={{0,128},{128,0},{256,384},{384,256},{1,129},{129,1},{257,385},{385... | collective-permute-start | bytes 1720328 | tf_op jit(solution)/shard_map/ppermute | solution.py:324
  124.0 2.6 %collective-permute-start.11 = (f32[140,8,128]{2,1,0:T(8,128)S(1)}, f32[140,8,128]{2,1,0:T(8,128)S(1)}, u32[]{:S(2)}, u32[]{:S(2)}) collective-permute-start(f32[140,8,128]{2,1,0:T(8,128)S(1)} %get-tuple-element.51), channel_id=1, source_target_pairs={{0,399},{128,256},{256,128},{384,1},{1,384},{129,257},{257,129},{3... | collective-permute-start | bytes 1720328 | tf_op jit(solution)/shard_map/ppermute | solution.py:325
  126.6 14.0 %all_to_all.27.got = f32[4,8,128]{2,1,0:T(8,128)S(1)} all-to-all(f32[4,8,128]{2,1,0:T(8,128)S(1)} %get-tuple-element.55), channel_id=1, replica_groups={{0,4,8,12},{1,5,9,13},{2,6,10,14},{3,7,11,15},{16,20,24,28},{17,21,25,2..., dimensions={0} | all-to-all | bytes 32768 | tf_op jit(solution)/shard_map/all_to_all | solution.py:339
  140.6 0.0 collective-permute-done.10.y1
  140.6 1.4 collective-permute-done.11.y2
  142.1 0.0 copy-done.1
  142.1 4.2 %shard_map.47 = f32[4,520,128]{2,1,0:T(8,128)S(1)} custom-call(s32[1]{0:T(128)} %bitcast.arm, f32[4,4]{1,0:T(4,128)S(1)} %copy-done.1, f32[40,4,8,128]{3,2,1,0:T(8,128)S(1)} %get-tuple-element.49.wide, f32[140,8,128]{2,1,0:T(8,128)S(1)} %collective-permute-done.10.y1, f32[140,8,128]{2,1,0:T(8,128)S(1)} %collective-permute-done.11.y2, ...), custom_call_target="tpu_custom_call" | custom-call | tf_op jit(solution)/shard_map/pallas_call | solution.py:396
  146.2 0.0 copy-start
  146.2 25.9 %all_to_all.28.back = f32[4,520,128]{2,1,0:T(8,128)S(1)} all-to-all(f32[4,520,128]{2,1,0:T(8,128)S(1)} %shard_map.47), channel_id=1, replica_groups=mesh['arm'=4,'gx'=8,'gy'=16] {'arm'}, dimensions={0} | all-to-all | bytes 2129920 | tf_op jit(solution)/shard_map/all_to_all | solution.py:404
  172.1 0.0 copy-done
  172.1 2.0 %shard_map.48 = (f32[32,16,256]{2,1,0:T(8,128)}, f32[32,16,256]{2,1,0:T(8,128)}) custom-call(s32[1]{0:T(128)} %bitcast.arm, f32[4,4]{1,0:T(4,128)S(1)} %copy-done.1, f32[4,520,128]{2,1,0:T(8,128)S(1)} %all_to_all.28.back, f32[32,16,256]{2,1,0:T(8,128)S(1)} %bitcast.10), custom_call_target="tpu_custom_call" | custom-call | tf_op jit(solution)/shard_map/pallas_call | solution.py:406
  (2 shorter events, 0.1 us)
Async XLA Ops:
  2.9 20.4 %all-to-all-start = ((f32[4,256,128]{2,1,0:T(8,128)}), f32[4,256,128]{2,1,0:T(8,128)S(1)}, u32[]{:S(2)}, u32[]{:S(2)}) async-start(f32[4,256,128]{2,1,0:T(8,128)} %bitcast.2), calls=%async_computation | async-start | bytes 1048576 | tf_op jit(solution)/shard_map/all_to_all | solution.py:342
  23.5 13.2 %collective-permute-start = (f32[32,3,8,128]{3,2,1,0:T(8,128)S(1)}, f32[32,3,8,128]{3,2,1,0:T(8,128)S(1)}, u32[]{:S(2)}, u32[]{:S(2)}) collective-permute-start(f32[32,3,8,128]{3,2,1,0:T(8,128)S(1)} %get-tuple-element.31), channel_id=1, source_target_pairs={{0,128},{128,0},{256,384},{384,256},{1,129},{129,1},{257,385},{385... | collective-permute-start | bytes 1179656 | tf_op jit(solution)/shard_map/ppermute | solution.py:324
  25.4 19.5 %collective-permute-start.1 = (f32[32,3,8,128]{3,2,1,0:T(8,128)S(1)}, f32[32,3,8,128]{3,2,1,0:T(8,128)S(1)}, u32[]{:S(2)}, u32[]{:S(2)}) collective-permute-start(f32[32,3,8,128]{3,2,1,0:T(8,128)S(1)} %get-tuple-element.32), channel_id=1, source_target_pairs={{0,399},{128,256},{256,128},{384,1},{1,384},{129,257},{257,129},{3... | collective-permute-start | bytes 1179656 | tf_op jit(solution)/shard_map/ppermute | solution.py:325
  44.9 5.5 %collective-permute-start.2 = (f32[58,8,128]{2,1,0:T(8,128)S(1)}, f32[58,8,128]{2,1,0:T(8,128)S(1)}, u32[]{:S(2)}, u32[]{:S(2)}) collective-permute-start(f32[58,8,128]{2,1,0:T(8,128)S(1)} %get-tuple-element.33), channel_id=1, source_target_pairs={{0,16},{16,32},{32,48},{48,64},{64,80},{80,96},{96,112},{112,0},{1... | collective-permute-start | bytes 712712 | tf_op jit(solution)/shard_map/ppermute | solution.py:330
  44.9 5.5 %collective-permute-start.3 = (f32[58,8,128]{2,1,0:T(8,128)S(1)}, f32[58,8,128]{2,1,0:T(8,128)S(1)}, u32[]{:S(2)}, u32[]{:S(2)}) collective-permute-start(f32[58,8,128]{2,1,0:T(8,128)S(1)} %get-tuple-element.34), channel_id=1, source_target_pairs={{0,112},{16,0},{32,16},{48,32},{64,48},{80,64},{96,80},{112,96},{1... | collective-permute-start | bytes 712712 | tf_op jit(solution)/shard_map/ppermute | solution.py:331
  52.9 16.9 %collective-permute-start.4 = (f32[140,8,128]{2,1,0:T(8,128)S(1)}, f32[140,8,128]{2,1,0:T(8,128)S(1)}, u32[]{:S(2)}, u32[]{:S(2)}) collective-permute-start(f32[140,8,128]{2,1,0:T(8,128)S(1)} %get-tuple-element.36), channel_id=1, source_target_pairs={{0,128},{128,0},{256,384},{384,256},{1,129},{129,1},{257,385},{385... | collective-permute-start | bytes 1720328 | tf_op jit(solution)/shard_map/ppermute | solution.py:324
  54.8 20.2 %collective-permute-start.5 = (f32[140,8,128]{2,1,0:T(8,128)S(1)}, f32[140,8,128]{2,1,0:T(8,128)S(1)}, u32[]{:S(2)}, u32[]{:S(2)}) collective-permute-start(f32[140,8,128]{2,1,0:T(8,128)S(1)} %get-tuple-element.37), channel_id=1, source_target_pairs={{0,399},{128,256},{256,128},{384,1},{1,384},{129,257},{257,129},{3... | collective-permute-start | bytes 1720328 | tf_op jit(solution)/shard_map/ppermute | solution.py:325
  78.2 19.7 %collective-permute-start.7 = (f32[32,4,8,128]{3,2,1,0:T(8,128)S(1)}, f32[32,4,8,128]{3,2,1,0:T(8,128)S(1)}, u32[]{:S(2)}, u32[]{:S(2)}) collective-permute-start(f32[32,4,8,128]{3,2,1,0:T(8,128)S(1)} %get-tuple-element.40.own), channel_id=1, source_target_pairs={{0,399},{128,256},{256,128},{384,1},{1,384},{129,257},{257,129},{3... | collective-permute-start | bytes 1572872 | tf_op jit(solution)/shard_map/ppermute | solution.py:325
  85.1 16.1 %collective-permute-start.6 = (f32[32,4,8,128]{3,2,1,0:T(8,128)S(1)}, f32[32,4,8,128]{3,2,1,0:T(8,128)S(1)}, u32[]{:S(2)}, u32[]{:S(2)}) collective-permute-start(f32[32,4,8,128]{3,2,1,0:T(8,128)S(1)} %get-tuple-element.40.own), channel_id=1, source_target_pairs={{0,128},{128,0},{256,384},{384,256},{1,129},{129,1},{257,385},{385... | collective-permute-start | bytes 1572872 | tf_op jit(solution)/shard_map/ppermute | solution.py:324
  101.3 16.7 %collective-permute-start.8 = (f32[76,8,128]{2,1,0:T(8,128)S(1)}, f32[76,8,128]{2,1,0:T(8,128)S(1)}, u32[]{:S(2)}, u32[]{:S(2)}) collective-permute-start(f32[76,8,128]{2,1,0:T(8,128)S(1)} %get-tuple-element.42), channel_id=1, source_target_pairs={{0,16},{16,32},{32,48},{48,64},{64,80},{80,96},{96,112},{112,0},{1... | collective-permute-start | bytes 933896 | tf_op jit(solution)/shard_map/ppermute | solution.py:330
  101.3 16.7 %collective-permute-start.9 = (f32[76,8,128]{2,1,0:T(8,128)S(1)}, f32[76,8,128]{2,1,0:T(8,128)S(1)}, u32[]{:S(2)}, u32[]{:S(2)}) collective-permute-start(f32[76,8,128]{2,1,0:T(8,128)S(1)} %get-tuple-element.43), channel_id=1, source_target_pairs={{0,112},{16,0},{32,16},{48,32},{64,48},{80,64},{96,80},{112,96},{1... | collective-permute-start | bytes 933896 | tf_op jit(solution)/shard_map/ppermute | solution.py:331
  118.0 24.1 %copy-start.1 = (f32[4,4]{1,0:T(4,128)S(1)}, f32[4,4]{1,0:T(4,128)}, u32[]{:S(2)}) copy-start(f32[4,4]{1,0:T(4,128)} %chi.3) | copy-start | bytes 196
  121.8 18.8 %collective-permute-start.10 = (f32[140,8,128]{2,1,0:T(8,128)S(1)}, f32[140,8,128]{2,1,0:T(8,128)S(1)}, u32[]{:S(2)}, u32[]{:S(2)}) collective-permute-start(f32[140,8,128]{2,1,0:T(8,128)S(1)} %get-tuple-element.50), channel_id=1, source_target_pairs={{0,128},{128,0},{256,384},{384,256},{1,129},{129,1},{257,385},{385... | collective-permute-start | bytes 1720328 | tf_op jit(solution)/shard_map/ppermute | solution.py:324
  124.0 18.0 %collective-permute-start.11 = (f32[140,8,128]{2,1,0:T(8,128)S(1)}, f32[140,8,128]{2,1,0:T(8,128)S(1)}, u32[]{:S(2)}, u32[]{:S(2)}) collective-permute-start(f32[140,8,128]{2,1,0:T(8,128)S(1)} %get-tuple-element.51), channel_id=1, source_target_pairs={{0,399},{128,256},{256,128},{384,1},{1,384},{129,257},{257,129},{3... | collective-permute-start | bytes 1720328 | tf_op jit(solution)/shard_map/ppermute | solution.py:325
  146.2 25.9 %copy-start = (f32[1,32,16,256]{3,2,1,0:T(8,128)S(1)}, f32[1,32,16,256]{3,2,1,0:T(8,128)}, u32[]{:S(2)}) copy-start(f32[1,32,16,256]{3,2,1,0:T(8,128)} %param.2) | copy-start | bytes 1572868

commit v4 on v3

--- a/solution.py
+++ b/solution.py
@@ -6,6 +6,7 @@
 from jax.experimental import pallas as pl
 from jax.experimental.pallas import tpu as pltpu
 from jax.sharding import PartitionSpec as P
+
 
 SPECIES = 4
 STEPS = 8
@@ -88,8 +89,8 @@
 
 def pack_sides(reach, arm, own, first, second, *rest):
     if len(rest) == 4:
-        got, left, right, spread = rest
-        spread[...] = jnp.broadcast_to(jnp.sum(got[...], axis=0), spread.shape)
+        got, left, right, total = rest
+        total[...] = jnp.sum(got[...], axis=0)
     else:
         left, right = rest
     width, depth = reach[0] + 1, len(reach)
@@ -210,10 +211,10 @@
 
 
 def outer_first(
-    arm, own, xlow, xhigh, y1, y2, coef, s4, s5, s6, s7, s8, got,
+    arm, own, xlow, xhigh, y1, y2, coef, s4, s5, s6, s7, s8, total,
     dens, wide, e1, e2, spread, a, b
 ):
-    spread[...] = jnp.broadcast_to(jnp.sum(got[...], axis=0), spread.shape)
+    spread[...] = jnp.broadcast_to(total[...], spread.shape)
     surround(arm, a, JUNC_REACH, own, y1, y2, xlow, xhigh, (8, 4))
     here = (slice(8, 8 + BX), slice(4, 8))
     shift = (-1, -1)
@@ -320,10 +321,8 @@
     second_pairs = [(at(r), at(((r + 1) ^ 1) - 1)) for r in range(size)]
 
     def along_y(first, second):
-        return (
-            lax.ppermute(first, ("arm", "gy"), first_pairs),
-            lax.ppermute(second, ("arm", "gy"), second_pairs),
-        )
+        second = lax.ppermute(second, ("arm", "gy"), second_pairs)
+        return lax.ppermute(first, ("arm", "gy"), first_pairs), second
 
     def along_x(left, right):
         m = size_gx
@@ -335,7 +334,11 @@
     z_groups = [[y * parts + z for z in range(parts)] for y in range(size_gy // parts)]
     y_groups = [list(g) for g in zip(*z_groups)]
 
-    def swap(spread, axis, groups=None):
+    xy_groups = [
+        [x * size_gy + g for x in range(size_gx) for g in group] for group in y_groups
+    ]
+
+    def swap(spread, axis, groups):
         return lax.all_to_all(spread, axis, 0, 0, axis_index_groups=groups)
 
     payload = field_here.reshape(BX, arms, BY, 2, LANES).transpose(1, 3, 0, 2, 4)
@@ -367,32 +370,28 @@
     y1, y2 = along_y(e1, e2)
     s5, s6, s7, s8, junction, spread = call(
         inner_second,
-        (own,) * 5 + (tiles(size_gx),),
+        (own,) * 5 + (tiles(len(xy_groups[0])),),
         [scratch(BX + 8, BY + 8)] * 2,
         scalars=1,
         arrays=5,
     )(arm, s4, y1, y2, coef, sums)
 
     y1, y2 = along_y(junction, junction)
-    got = swap(spread, "gx")
+    got = swap(spread, ("gx", "gy"), xy_groups)
     side = tiles(side_size(JUNC_REACH))
-    left, right, spread = call(
-        functools.partial(pack_sides, JUNC_REACH),
-        (side, side, tiles(parts)),
-        scalars=1,
-        arrays=4,
+    left, right, total = call(
+        functools.partial(pack_sides, JUNC_REACH), (side, side, tiles()), scalars=1, arrays=4
     )(arm, junction, y1, y2, got)
     xlow, xhigh = along_x(left, right)
-    got = swap(spread, "gy", z_groups)
     dens, wide, e1, e2, spread = call(
         outer_first,
-        (own, wide_shape, mid, mid, tiles(len(z_groups))),
+        (own, wide_shape, mid, mid, tiles(parts)),
         [scratch(16 + BX, 8 + BY)] * 2,
         scalars=1,
         arrays=12,
-    )(arm, junction, xlow, xhigh, y1, y2, coef, s4, s5, s6, s7, s8, got)
+    )(arm, junction, xlow, xhigh, y1, y2, coef, s4, s5, s6, s7, s8, total)
     y1, y2 = along_y(e1, e2)
-    got = swap(spread, "gy", y_groups)
+    got = swap(spread, "gy", z_groups)
     out = call(
         outer_second,
         jax.ShapeDtypeStruct((arms, 4 * n + 8, LANES), jnp.float32),

time: 176 us -> 171 us (0.972)
  blocking collectives: 63.2 us -> 57 us
  starting transfers between devices: 45.1 us -> 47.2 us
    all_to_all x3 -> x2, blocking collectives: 37.4 us -> 27.1 us  [swap(): return lax.all_to_all(spread, axis, 0, 0, axis_index_groups=groups)]
    ppermute x2, waiting for transfers between devices: 3.79 us -> 8.36 us  [along_x(): low = lax.ppermute(right, 'gx', [(i, (i + 1) % m) for i in range(m)])]
    ppermute x8, waiting for transfers between devices: 28.7 us -> 24.5 us  [the longest x4 14.5 us: along_y(): second = lax.ppermute(second, ('arm', 'gy'), second_pairs)]
    all_to_all x1, blocking collectives: 25.9 us -> 30 us  [local(): back = lax.all_to_all(out, 'arm', 0, 0)]
    ppermute x8, starting transfers between devices: 35.7 us -> 37.8 us  [the longest x4 29.9 us: along_y(): second = lax.ppermute(second, ('arm', 'gy'), second_pairs)]
where the time goes in v4:
time: 171 us
  blocking collectives  57 us (33%)
  waiting for transfers between devices  47.3 us (28%)
  starting transfers between devices  47.2 us (28%)
  Pallas kernels  15.9 us (9%)
  local copies, waits for them, and re-layouts  2.24 us (1%)
    all_to_all x1, blocking collectives, local(): back = lax.all_to_all(out, 'arm', 0, 0)  30 us
    ppermute x4, starting transfers between devices, along_y(): second = lax.ppermute(second, ('arm', 'gy'), second_pairs)  29.9 us
    all_to_all x2, blocking collectives, swap(): return lax.all_to_all(spread, axis, 0, 0, axis_index_groups=groups)  27.1 us
    all_to_all x1, waiting for transfers between devices, local(): recv = lax.all_to_all(payload.reshape(arms, 2 * n, LANES), 'arm', 0, 0)  14.5 us
    ppermute x4, waiting for transfers between devices, along_y(): second = lax.ppermute(second, ('arm', 'gy'), second_pairs)  14.5 us
    ppermute x4, waiting for transfers between devices, along_y(): return (lax.ppermute(first, ('arm', 'gy'), first_pairs), second)  10 us
    ppermute x2, waiting for transfers between devices, along_x(): low = lax.ppermute(right, 'gx', [(i, (i + 1) % m) for i in range(m)])  8.36 us
    ppermute x4, starting transfers between devices, along_y(): return (lax.ppermute(first, ('arm', 'gy'), first_pairs), second)  7.98 us
  transfers between devices with their start and end apart: 13, of which 8 were waited for; matrix products, arithmetic and copies ran while one was open for 0% of the time, Pallas kernels for 0%

profile of v4, /device:TPU:6, one launch (start us, length us, event | category | flops | bytes accessed | tf_op | source)
XLA Modules:
  0.0 170.5 jit_solution(15478810815244626141)
XLA Ops:
  0.6 1.3 reshape_squeeze.3
  1.9 0.9 copy.4
  2.9 5.9 %all-to-all-start = ((f32[4,256,128]{2,1,0:T(8,128)}), f32[4,256,128]{2,1,0:T(8,128)S(1)}, u32[]{:S(2)}, u32[]{:S(2)}) async-start(f32[4,256,128]{2,1,0:T(8,128)} %bitcast.2), calls=%async_computation | async-start | bytes 1048576 | tf_op jit(solution)/shard_map/all_to_all | solution.py:345
  8.8 14.5 %all-to-all-done.recv = f32[4,256,128]{2,1,0:T(8,128)S(1)} async-done(((f32[4,256,128]{2,1,0:T(8,128)}), f32[4,256,128]{2,1,0:T(8,128)S(1)}, u32[]{:S(2)}, u32[]{:S(2)}) %all-to-all-start) | async-done | bytes 524320 | tf_op jit(solution)/shard_map/all_to_all | solution.py:345
  23.2 0.2 shard_map.41
  23.5 1.9 %collective-permute-start = (f32[32,3,8,128]{3,2,1,0:T(8,128)S(1)}, f32[32,3,8,128]{3,2,1,0:T(8,128)S(1)}, u32[]{:S(2)}, u32[]{:S(2)}) collective-permute-start(f32[32,3,8,128]{3,2,1,0:T(8,128)S(1)} %get-tuple-element.31), channel_id=1, source_target_pairs={{0,128},{128,0},{256,384},{384,256},{1,129},{129,1},{257,385},{385... | collective-permute-start | bytes 1179656 | tf_op jit(solution)/shard_map/ppermute | solution.py:325
  25.4 11.2 %collective-permute-start.1 = (f32[32,3,8,128]{3,2,1,0:T(8,128)S(1)}, f32[32,3,8,128]{3,2,1,0:T(8,128)S(1)}, u32[]{:S(2)}, u32[]{:S(2)}) collective-permute-start(f32[32,3,8,128]{3,2,1,0:T(8,128)S(1)} %get-tuple-element.32), channel_id=1, source_target_pairs={{0,399},{128,256},{256,128},{384,1},{1,384},{129,257},{257,129},{3... | collective-permute-start | bytes 1179656 | tf_op jit(solution)/shard_map/ppermute | solution.py:324
  36.6 0.0 collective-permute-done.first.y1
  36.6 8.2 %collective-permute-done.1.second.y2 = f32[32,3,8,128]{3,2,1,0:T(8,128)S(1)} collective-permute-done((f32[32,3,8,128]{3,2,1,0:T(8,128)S(1)}, f32[32,3,8,128]{3,2,1,0:T(8,128)S(1)}, u32[]{:S(2)}, u32[]{:S(2)}) %collective-permute-start.1) | collective-permute-done | bytes 393248 | tf_op jit(solution)/shard_map/ppermute | solution.py:324
  44.9 0.0 collective-permute-start.2
  44.9 1.7 %collective-permute-start.3 = (f32[58,8,128]{2,1,0:T(8,128)S(1)}, f32[58,8,128]{2,1,0:T(8,128)S(1)}, u32[]{:S(2)}, u32[]{:S(2)}) collective-permute-start(f32[58,8,128]{2,1,0:T(8,128)S(1)} %get-tuple-element.34), channel_id=1, source_target_pairs={{0,112},{16,0},{32,16},{48,32},{64,48},{80,64},{96,80},{112,96},{1... | collective-permute-start | bytes 712712 | tf_op jit(solution)/shard_map/ppermute | solution.py:330
  46.7 3.8 %collective-permute-done.2.xlow = f32[58,8,128]{2,1,0:T(8,128)S(1)} collective-permute-done((f32[58,8,128]{2,1,0:T(8,128)S(1)}, f32[58,8,128]{2,1,0:T(8,128)S(1)}, u32[]{:S(2)}, u32[]{:S(2)}) %collective-permute-start.2) | collective-permute-done | bytes 237600 | tf_op jit(solution)/shard_map/ppermute | solution.py:329
  50.5 0.0 collective-permute-done.3.xhigh
  50.5 2.4 %shard_map.43 = (f32[46,10,8,128]{3,2,1,0:T(8,128)S(1)}, f32[32,4,8,128]{3,2,1,0:T(8,128)S(1)}, f32[32,4,8,128]{3,2,1,0:T(8,128)S(1)}, f32[40,4,8,128]{3,2,1,0:T...) custom-call(s32[1]{0:T(128)} %bitcast.arm, f32[32,4,8,128]{3,2,1,0:T(8,128)S(1)} %bitcast.12, ...), custom_call_target="tpu_custom_call" | custom-call | tf_op jit(solution)/shard_map/pallas_call | solution.py:363
  52.9 1.9 %collective-permute-start.4 = (f32[140,8,128]{2,1,0:T(8,128)S(1)}, f32[140,8,128]{2,1,0:T(8,128)S(1)}, u32[]{:S(2)}, u32[]{:S(2)}) collective-permute-start(f32[140,8,128]{2,1,0:T(8,128)S(1)} %get-tuple-element.36), channel_id=1, source_target_pairs={{0,128},{128,0},{256,384},{384,256},{1,129},{129,1},{257,385},{385... | collective-permute-start | bytes 1720328 | tf_op jit(solution)/shard_map/ppermute | solution.py:325
  54.8 7.0 %collective-permute-start.5 = (f32[140,8,128]{2,1,0:T(8,128)S(1)}, f32[140,8,128]{2,1,0:T(8,128)S(1)}, u32[]{:S(2)}, u32[]{:S(2)}) collective-permute-start(f32[140,8,128]{2,1,0:T(8,128)S(1)} %get-tuple-element.37), channel_id=1, source_target_pairs={{0,399},{128,256},{256,128},{384,1},{1,384},{129,257},{257,129},{3... | collective-permute-start | bytes 1720328 | tf_op jit(solution)/shard_map/ppermute | solution.py:324
  61.8 8.0 %collective-permute-done.4.y1 = f32[140,8,128]{2,1,0:T(8,128)S(1)} collective-permute-done((f32[140,8,128]{2,1,0:T(8,128)S(1)}, f32[140,8,128]{2,1,0:T(8,128)S(1)}, u32[]{:S(2)}, u32[]{:S(2)}) %collective-permute-start.4) | collective-permute-done | bytes 573472 | tf_op jit(solution)/shard_map/ppermute | solution.py:325
  69.8 5.2 %collective-permute-done.5.y2 = f32[140,8,128]{2,1,0:T(8,128)S(1)} collective-permute-done((f32[140,8,128]{2,1,0:T(8,128)S(1)}, f32[140,8,128]{2,1,0:T(8,128)S(1)}, u32[]{:S(2)}, u32[]{:S(2)}) %collective-permute-start.5) | collective-permute-done | bytes 573472 | tf_op jit(solution)/shard_map/ppermute | solution.py:324
  75.1 3.1 %shard_map.44 = (f32[32,4,8,128]{3,2,1,0:T(8,128)S(1)}, f32[32,4,8,128]{3,2,1,0:T(8,128)S(1)}, f32[32,4,8,128]{3,2,1,0:T(8,128)S(1)}, f32[32,4,8,128]{3,2,1,0:T(...) custom-call(s32[1]{0:T(128)} %bitcast.arm, f32[40,4,8,128]{3,2,1,0:T(8,128)S(1)} %get-tuple-element.35.wide.s4, ...), custom_call_target="tpu_custom_call" | custom-call | tf_op jit(solution)/shard_map/pallas_call | solution.py:371
  78.2 7.0 %collective-permute-start.7 = (f32[32,4,8,128]{3,2,1,0:T(8,128)S(1)}, f32[32,4,8,128]{3,2,1,0:T(8,128)S(1)}, u32[]{:S(2)}, u32[]{:S(2)}) collective-permute-start(f32[32,4,8,128]{3,2,1,0:T(8,128)S(1)} %get-tuple-element.40.own), channel_id=1, source_target_pairs={{0,399},{128,256},{256,128},{384,1},{1,384},{129,257},{257,129},{3... | collective-permute-start | bytes 1572872 | tf_op jit(solution)/shard_map/ppermute | solution.py:324
  85.2 1.9 %collective-permute-start.6 = (f32[32,4,8,128]{3,2,1,0:T(8,128)S(1)}, f32[32,4,8,128]{3,2,1,0:T(8,128)S(1)}, u32[]{:S(2)}, u32[]{:S(2)}) collective-permute-start(f32[32,4,8,128]{3,2,1,0:T(8,128)S(1)} %get-tuple-element.40.own), channel_id=1, source_target_pairs={{0,128},{128,0},{256,384},{384,256},{1,129},{129,1},{257,385},{385... | collective-permute-start | bytes 1572872 | tf_op jit(solution)/shard_map/ppermute | solution.py:325
  87.1 12.2 %all_to_all.20.rest_0_ = f32[32,8,128]{2,1,0:T(8,128)S(1)} all-to-all(f32[32,8,128]{2,1,0:T(8,128)S(1)} %get-tuple-element.41), channel_id=1, replica_groups={{0,4,8,12,16,20,24,28,32,36,40,44,48,52,56,60,64,68,72,76,80,84,88,92,9..., dimensions={0} | all-to-all | bytes 262144 | tf_op jit(solution)/shard_map/all_to_all | solution.py:342
  99.3 0.0 collective-permute-done.7.second.y2
  99.3 2.0 %collective-permute-done.6.first.y1 = f32[32,4,8,128]{3,2,1,0:T(8,128)S(1)} collective-permute-done((f32[32,4,8,128]{3,2,1,0:T(8,128)S(1)}, f32[32,4,8,128]{3,2,1,0:T(8,128)S(1)}, u32[]{:S(2)}, u32[]{:S(2)}) %collective-permute-start.6) | collective-permute-done | bytes 524320 | tf_op jit(solution)/shard_map/ppermute | solution.py:325
  101.3 0.1 shard_map.45
  101.3 0.0 collective-permute-start.8
  101.3 1.7 %collective-permute-start.9 = (f32[76,8,128]{2,1,0:T(8,128)S(1)}, f32[76,8,128]{2,1,0:T(8,128)S(1)}, u32[]{:S(2)}, u32[]{:S(2)}) collective-permute-start(f32[76,8,128]{2,1,0:T(8,128)S(1)} %get-tuple-element.43), channel_id=1, source_target_pairs={{0,112},{16,0},{32,16},{48,32},{64,48},{80,64},{96,80},{112,96},{1... | collective-permute-start | bytes 933896 | tf_op jit(solution)/shard_map/ppermute | solution.py:330
  103.1 4.6 %collective-permute-done.8.xlow = f32[76,8,128]{2,1,0:T(8,128)S(1)} collective-permute-done((f32[76,8,128]{2,1,0:T(8,128)S(1)}, f32[76,8,128]{2,1,0:T(8,128)S(1)}, u32[]{:S(2)}, u32[]{:S(2)}) %collective-permute-start.8) | collective-permute-done | bytes 311328 | tf_op jit(solution)/shard_map/ppermute | solution.py:329
  107.6 0.0 collective-permute-done.9.xhigh
  107.6 0.0 copy-start.1
  107.7 3.9 %shard_map.46 = (f32[32,4,8,128]{3,2,1,0:T(8,128)S(1)}, f32[40,4,8,128]{3,2,1,0:T(8,128)S(1)}, f32[140,8,128]{2,1,0:T(8,128)S(1)}, f32[140,8,128]{2,1,0:T(8,128)S(1)}, f32[4,8,128]{2,1,0:T(8,128)S(1)}) custom-call(s32[1]{0:T(128)} %bitcast.arm, f32[32,4,8,128]{3,2,1,0:T(8,128)S(1)} %get-tuple-element.40.own, f32[76,8,128]{2,1,0:T(8,128)S(1)} %collective-permute-done.8.xlow, ...), custom_call_target="tpu_custom_call" | custom-call | tf_op jit(solution)/shard_map/pallas_call | solution.py:386
  111.5 2.2 %collective-permute-start.10 = (f32[140,8,128]{2,1,0:T(8,128)S(1)}, f32[140,8,128]{2,1,0:T(8,128)S(1)}, u32[]{:S(2)}, u32[]{:S(2)}) collective-permute-start(f32[140,8,128]{2,1,0:T(8,128)S(1)} %get-tuple-element.50), channel_id=1, source_target_pairs={{0,128},{128,0},{256,384},{384,256},{1,129},{129,1},{257,385},{385... | collective-permute-start | bytes 1720328 | tf_op jit(solution)/shard_map/ppermute | solution.py:325
  113.8 4.7 %collective-permute-start.11 = (f32[140,8,128]{2,1,0:T(8,128)S(1)}, f32[140,8,128]{2,1,0:T(8,128)S(1)}, u32[]{:S(2)}, u32[]{:S(2)}) collective-permute-start(f32[140,8,128]{2,1,0:T(8,128)S(1)} %get-tuple-element.51), channel_id=1, source_target_pairs={{0,399},{128,256},{256,128},{384,1},{1,384},{129,257},{257,129},{3... | collective-permute-start | bytes 1720328 | tf_op jit(solution)/shard_map/ppermute | solution.py:324
  118.5 14.9 %all_to_all.21.got = f32[4,8,128]{2,1,0:T(8,128)S(1)} all-to-all(f32[4,8,128]{2,1,0:T(8,128)S(1)} %get-tuple-element.55), channel_id=1, replica_groups={{0,1,2,3},{4,5,6,7},{8,9,10,11},{12,13,14,15},{16,17,18,19},{20,21,22,2..., dimensions={0} | all-to-all | bytes 32768 | tf_op jit(solution)/shard_map/all_to_all | solution.py:342
  133.4 0.0 collective-permute-done.10.y1
  133.4 1.0 collective-permute-done.11.y2
  134.4 0.0 copy-done.1
  134.4 4.2 %shard_map.47 = f32[4,520,128]{2,1,0:T(8,128)S(1)} custom-call(s32[1]{0:T(128)} %bitcast.arm, f32[4,4]{1,0:T(4,128)S(1)} %copy-done.1, f32[40,4,8,128]{3,2,1,0:T(8,128)S(1)} %get-tuple-element.49.wide, f32[140,8,128]{2,1,0:T(8,128)S(1)} %collective-permute-done.10.y1, f32[140,8,128]{2,1,0:T(8,128)S(1)} %collective-permute-done.11.y2, ...), custom_call_target="tpu_custom_call" | custom-call | tf_op jit(solution)/shard_map/pallas_call | solution.py:395
  138.6 0.0 copy-start
  138.6 30.0 %all_to_all.22.back = f32[4,520,128]{2,1,0:T(8,128)S(1)} all-to-all(f32[4,520,128]{2,1,0:T(8,128)S(1)} %shard_map.47), channel_id=1, replica_groups=mesh['arm'=4,'gx'=8,'gy'=16] {'arm'}, dimensions={0} | all-to-all | bytes 2129920 | tf_op jit(solution)/shard_map/all_to_all | solution.py:403
  168.5 0.0 copy-done
  168.5 2.0 %shard_map.48 = (f32[32,16,256]{2,1,0:T(8,128)}, f32[32,16,256]{2,1,0:T(8,128)}) custom-call(s32[1]{0:T(128)} %bitcast.arm, f32[4,4]{1,0:T(4,128)S(1)} %copy-done.1, f32[4,520,128]{2,1,0:T(8,128)S(1)} %all_to_all.22.back, f32[32,16,256]{2,1,0:T(8,128)S(1)} %bitcast.10), custom_call_target="tpu_custom_call" | custom-call | tf_op jit(solution)/shard_map/pallas_call | solution.py:405
  (1 shorter events, 0.0 us)
Async XLA Ops:
  2.9 20.4 %all-to-all-start = ((f32[4,256,128]{2,1,0:T(8,128)}), f32[4,256,128]{2,1,0:T(8,128)S(1)}, u32[]{:S(2)}, u32[]{:S(2)}) async-start(f32[4,256,128]{2,1,0:T(8,128)} %bitcast.2), calls=%async_computation | async-start | bytes 1048576 | tf_op jit(solution)/shard_map/all_to_all | solution.py:345
  23.5 13.2 %collective-permute-start = (f32[32,3,8,128]{3,2,1,0:T(8,128)S(1)}, f32[32,3,8,128]{3,2,1,0:T(8,128)S(1)}, u32[]{:S(2)}, u32[]{:S(2)}) collective-permute-start(f32[32,3,8,128]{3,2,1,0:T(8,128)S(1)} %get-tuple-element.31), channel_id=1, source_target_pairs={{0,128},{128,0},{256,384},{384,256},{1,129},{129,1},{257,385},{385... | collective-permute-start | bytes 1179656 | tf_op jit(solution)/shard_map/ppermute | solution.py:325
  25.4 19.5 %collective-permute-start.1 = (f32[32,3,8,128]{3,2,1,0:T(8,128)S(1)}, f32[32,3,8,128]{3,2,1,0:T(8,128)S(1)}, u32[]{:S(2)}, u32[]{:S(2)}) collective-permute-start(f32[32,3,8,128]{3,2,1,0:T(8,128)S(1)} %get-tuple-element.32), channel_id=1, source_target_pairs={{0,399},{128,256},{256,128},{384,1},{1,384},{129,257},{257,129},{3... | collective-permute-start | bytes 1179656 | tf_op jit(solution)/shard_map/ppermute | solution.py:324
  44.9 5.5 %collective-permute-start.2 = (f32[58,8,128]{2,1,0:T(8,128)S(1)}, f32[58,8,128]{2,1,0:T(8,128)S(1)}, u32[]{:S(2)}, u32[]{:S(2)}) collective-permute-start(f32[58,8,128]{2,1,0:T(8,128)S(1)} %get-tuple-element.33), channel_id=1, source_target_pairs={{0,16},{16,32},{32,48},{48,64},{64,80},{80,96},{96,112},{112,0},{1... | collective-permute-start | bytes 712712 | tf_op jit(solution)/shard_map/ppermute | solution.py:329
  44.9 5.5 %collective-permute-start.3 = (f32[58,8,128]{2,1,0:T(8,128)S(1)}, f32[58,8,128]{2,1,0:T(8,128)S(1)}, u32[]{:S(2)}, u32[]{:S(2)}) collective-permute-start(f32[58,8,128]{2,1,0:T(8,128)S(1)} %get-tuple-element.34), channel_id=1, source_target_pairs={{0,112},{16,0},{32,16},{48,32},{64,48},{80,64},{96,80},{112,96},{1... | collective-permute-start | bytes 712712 | tf_op jit(solution)/shard_map/ppermute | solution.py:330
  52.9 16.9 %collective-permute-start.4 = (f32[140,8,128]{2,1,0:T(8,128)S(1)}, f32[140,8,128]{2,1,0:T(8,128)S(1)}, u32[]{:S(2)}, u32[]{:S(2)}) collective-permute-start(f32[140,8,128]{2,1,0:T(8,128)S(1)} %get-tuple-element.36), channel_id=1, source_target_pairs={{0,128},{128,0},{256,384},{384,256},{1,129},{129,1},{257,385},{385... | collective-permute-start | bytes 1720328 | tf_op jit(solution)/shard_map/ppermute | solution.py:325
  54.8 20.2 %collective-permute-start.5 = (f32[140,8,128]{2,1,0:T(8,128)S(1)}, f32[140,8,128]{2,1,0:T(8,128)S(1)}, u32[]{:S(2)}, u32[]{:S(2)}) collective-permute-start(f32[140,8,128]{2,1,0:T(8,128)S(1)} %get-tuple-element.37), channel_id=1, source_target_pairs={{0,399},{128,256},{256,128},{384,1},{1,384},{129,257},{257,129},{3... | collective-permute-start | bytes 1720328 | tf_op jit(solution)/shard_map/ppermute | solution.py:324
  78.2 21.1 %collective-permute-start.7 = (f32[32,4,8,128]{3,2,1,0:T(8,128)S(1)}, f32[32,4,8,128]{3,2,1,0:T(8,128)S(1)}, u32[]{:S(2)}, u32[]{:S(2)}) collective-permute-start(f32[32,4,8,128]{3,2,1,0:T(8,128)S(1)} %get-tuple-element.40.own), channel_id=1, source_target_pairs={{0,399},{128,256},{256,128},{384,1},{1,384},{129,257},{257,129},{3... | collective-permute-start | bytes 1572872 | tf_op jit(solution)/shard_map/ppermute | solution.py:324
  85.2 16.1 %collective-permute-start.6 = (f32[32,4,8,128]{3,2,1,0:T(8,128)S(1)}, f32[32,4,8,128]{3,2,1,0:T(8,128)S(1)}, u32[]{:S(2)}, u32[]{:S(2)}) collective-permute-start(f32[32,4,8,128]{3,2,1,0:T(8,128)S(1)} %get-tuple-element.40.own), channel_id=1, source_target_pairs={{0,128},{128,0},{256,384},{384,256},{1,129},{129,1},{257,385},{385... | collective-permute-start | bytes 1572872 | tf_op jit(solution)/shard_map/ppermute | solution.py:325
  101.3 6.3 %collective-permute-start.8 = (f32[76,8,128]{2,1,0:T(8,128)S(1)}, f32[76,8,128]{2,1,0:T(8,128)S(1)}, u32[]{:S(2)}, u32[]{:S(2)}) collective-permute-start(f32[76,8,128]{2,1,0:T(8,128)S(1)} %get-tuple-element.42), channel_id=1, source_target_pairs={{0,16},{16,32},{32,48},{48,64},{64,80},{80,96},{96,112},{112,0},{1... | collective-permute-start | bytes 933896 | tf_op jit(solution)/shard_map/ppermute | solution.py:329
  101.3 6.3 %collective-permute-start.9 = (f32[76,8,128]{2,1,0:T(8,128)S(1)}, f32[76,8,128]{2,1,0:T(8,128)S(1)}, u32[]{:S(2)}, u32[]{:S(2)}) collective-permute-start(f32[76,8,128]{2,1,0:T(8,128)S(1)} %get-tuple-element.43), channel_id=1, source_target_pairs={{0,112},{16,0},{32,16},{48,32},{64,48},{80,64},{96,80},{112,96},{1... | collective-permute-start | bytes 933896 | tf_op jit(solution)/shard_map/ppermute | solution.py:330
  107.6 26.7 %copy-start.1 = (f32[4,4]{1,0:T(4,128)S(1)}, f32[4,4]{1,0:T(4,128)}, u32[]{:S(2)}) copy-start(f32[4,4]{1,0:T(4,128)} %chi.3) | copy-start | bytes 196
  111.5 21.9 %collective-permute-start.10 = (f32[140,8,128]{2,1,0:T(8,128)S(1)}, f32[140,8,128]{2,1,0:T(8,128)S(1)}, u32[]{:S(2)}, u32[]{:S(2)}) collective-permute-start(f32[140,8,128]{2,1,0:T(8,128)S(1)} %get-tuple-element.50), channel_id=1, source_target_pairs={{0,128},{128,0},{256,384},{384,256},{1,129},{129,1},{257,385},{385... | collective-permute-start | bytes 1720328 | tf_op jit(solution)/shard_map/ppermute | solution.py:325
  113.8 20.6 %collective-permute-start.11 = (f32[140,8,128]{2,1,0:T(8,128)S(1)}, f32[140,8,128]{2,1,0:T(8,128)S(1)}, u32[]{:S(2)}, u32[]{:S(2)}) collective-permute-start(f32[140,8,128]{2,1,0:T(8,128)S(1)} %get-tuple-element.51), channel_id=1, source_target_pairs={{0,399},{128,256},{256,128},{384,1},{1,384},{129,257},{257,129},{3... | collective-permute-start | bytes 1720328 | tf_op jit(solution)/shard_map/ppermute | solution.py:324
  138.6 30.0 %copy-start = (f32[1,32,16,256]{3,2,1,0:T(8,128)S(1)}, f32[1,32,16,256]{3,2,1,0:T(8,128)}, u32[]{:S(2)}) copy-start(f32[1,32,16,256]{3,2,1,0:T(8,128)} %param.2) | copy-start | bytes 1572868

commit v5 on v4

--- a/solution.py
+++ b/solution.py
@@ -42,18 +42,30 @@
     return lane == LANES - 1, lane == 0
 
 
-def step(src, dst, coef, xs, ys, coef_shift):
-    (x0, x1), (y0, y1) = xs, ys
-    dx, dy = coef_shift
+def step(src, dst, coef, origin, reach, depth, coef_shift):
+    (ox, oy), (dx, dy) = origin, coef_shift
     last, first = lane_masks()
-    v = src[x0:x1, y0:y1]
-    other = pltpu.roll(v, 4, 2)
-    up = pltpu.roll(jnp.where(last, other, v), 1, 3)
-    down = pltpu.roll(jnp.where(first, other, v), LANES - 1, 3)
-    total = (src[x0 - 1 : x1 - 1, y0:y1] + src[x0 + 1 : x1 + 1, y0:y1]) + (
-        src[x0:x1, y0 - 1 : y1 - 1] + src[x0:x1, y0 + 1 : y1 + 1]
-    )
-    dst[x0:x1, y0:y1] = total + (up + down) + coef[x0 + dx : x1 + dx, y0 + dy : y1 + dy] * v
+    for x in range(ox - reach, ox + BX + reach):
+        outside = max(ox - x, x - (ox + BX - 1), 0)
+        rows = min(depth, reach - outside)
+        for y in range(oy - rows, oy + BY + rows):
+            v = src[x, y]
+            other = pltpu.roll(v, 4, 0)
+            up = pltpu.roll(jnp.where(last, other, v), 1, 1)
+            down = pltpu.roll(jnp.where(first, other, v), LANES - 1, 1)
+            total = (src[x - 1, y] + src[x + 1, y]) + (src[x, y - 1] + src[x, y + 1])
+            dst[x, y] = total + (up + down) + coef[x + dx, y + dy] * v
+
+
+def spread_kernel(field, out):
+    n = BX * BY
+    for x in range(BX):
+        for half in range(2):
+            for q in range(SPECIES):
+                at = half * n + x * BY
+                out[q, at : at + BY, :] = field[
+                    x, q * BY : (q + 1) * BY, half * LANES : (half + 1) * LANES
+                ]
 
 
 def interleave_kernel(arm, recv, coef, sums, first, second):
@@ -168,11 +180,11 @@
     surround(arm, coef, COEF_REACH, own, y1, y2, xlow, xhigh, (7, 3))
     here = (slice(7, 7 + BX), slice(3, 7))
     a[...] = 6.0 + coef[...]
-    step(a, b, coef, (1, 45), (1, 9), (0, 0))
+    step(a, b, coef, (7, 3), 6, 2, (0, 0))
     s2[...] = b[here]
-    step(b, a, coef, (2, 44), (2, 8), (0, 0))
+    step(b, a, coef, (7, 3), 5, 1, (0, 0))
     s3[...] = a[here]
-    step(a, b, coef, (3, 43), (3, 7), (0, 0))
+    step(a, b, coef, (7, 3), 4, 0, (0, 0))
     emit(arm, b, (7, 3), MID_REACH, wide, e1, e2)
 
 
@@ -190,13 +202,13 @@
     a[0 : BX + 8, 4:8] = wide[...]
     unpack(arm, a, MID_REACH, y1, y2, (4, 4))
     here = (slice(4, 4 + BX), slice(4, 8))
-    step(a, b, coef, (1, 39), (1, 11), (3, -1))
+    step(a, b, coef, (4, 4), 3, 3, (3, -1))
     s5[...] = b[here]
-    step(b, a, coef, (2, 38), (2, 10), (3, -1))
+    step(b, a, coef, (4, 4), 2, 2, (3, -1))
     s6[...] = a[here]
-    step(a, b, coef, (3, 37), (3, 9), (3, -1))
+    step(a, b, coef, (4, 4), 1, 1, (3, -1))
     s7[...] = b[here]
-    step(b, a, coef, (4, 36), (4, 8), (3, -1))
+    step(b, a, coef, (4, 4), 0, 0, (3, -1))
     part = jnp.zeros((8, LANES), jnp.float32)
     for x in range(BX):
         q = a[x + 4, 4:8]
@@ -218,13 +230,13 @@
     surround(arm, a, JUNC_REACH, own, y1, y2, xlow, xhigh, (8, 4))
     here = (slice(8, 8 + BX), slice(4, 8))
     shift = (-1, -1)
-    step(a, b, coef, (1, 47), (1, 11), shift)
+    step(a, b, coef, (8, 4), 7, 3, shift)
     dens[...] = 0.5 * s8[...] * own[...] + s7[...] * b[here]
-    step(b, a, coef, (2, 46), (2, 10), shift)
+    step(b, a, coef, (8, 4), 6, 2, shift)
     dens[...] += s6[...] * a[here]
-    step(a, b, coef, (3, 45), (3, 9), shift)
+    step(a, b, coef, (8, 4), 5, 1, shift)
     dens[...] += s5[...] * b[here]
-    step(b, a, coef, (4, 44), (4, 8), shift)
+    step(b, a, coef, (8, 4), 4, 0, shift)
     dens[...] += s4[4 : 4 + BX] * a[here]
     emit(arm, a, (8, 4), MID_REACH, wide, e1, e2)
 
@@ -236,13 +248,13 @@
     unpack(arm, a, MID_REACH, y1, y2, (4, 4))
     here = (slice(4, 4 + BX), slice(4, 8))
     rows = (8 * BX * BY, LANES)
-    step(a, b, coef, (1, 39), (1, 11), (3, -1))
+    step(a, b, coef, (4, 4), 3, 3, (3, -1))
     flat[...] = (dens[...] + s3[...] * b[here]).reshape(rows)
-    step(b, a, coef, (2, 38), (2, 10), (3, -1))
+    step(b, a, coef, (4, 4), 2, 2, (3, -1))
     flat[...] += (s2[...] * a[here]).reshape(rows)
-    step(a, b, coef, (3, 37), (3, 9), (3, -1))
+    step(a, b, coef, (4, 4), 1, 1, (3, -1))
     flat[...] += ((6.0 + coef[7 : 7 + BX, 3:7]) * b[here]).reshape(rows)
-    step(b, a, coef, (4, 36), (4, 8), (3, -1))
+    step(b, a, coef, (4, 4), 0, 0, (3, -1))
     d = flat[...].reshape(BX, BY, 8, LANES) + 0.5 * a[here]
     flat[...] = d.reshape(rows)
     row = lax.broadcasted_iota(jnp.int32, (8, LANES), 0) % 4
@@ -341,8 +353,10 @@
     def swap(spread, axis, groups):
         return lax.all_to_all(spread, axis, 0, 0, axis_index_groups=groups)
 
-    payload = field_here.reshape(BX, arms, BY, 2, LANES).transpose(1, 3, 0, 2, 4)
-    recv = lax.all_to_all(payload.reshape(arms, 2 * n, LANES), "arm", 0, 0)
+    payload = call(
+        spread_kernel, jax.ShapeDtypeStruct((arms, 2 * n, LANES), jnp.float32), arrays=1
+    )(field_here)
+    recv = lax.all_to_all(payload, "arm", 0, 0)
     rows = tiles(BX, len(COEF_REACH))
     coef_flat, sums, e1, e2 = call(
         interleave_kernel,

time: 171 us -> 169 us (0.988)
    another operation x2 -> x0, local copies, waits for them, and re-layouts: 2.23 us -> none  [local(): field_here.reshape(BX, arms, BY, 2, LANES).transpose(1, 3, 0, 2, 4)]
where the time goes in v5:
time: 169 us; the launch traced here: 168 us
  blocking collectives  57 us (34%)
  starting transfers between devices  47.3 us (28%)
  waiting for transfers between devices  47.3 us (28%)
  Pallas kernels  14.7 us (9%)
    all_to_all x1, blocking collectives, local(): back = lax.all_to_all(out, 'arm', 0, 0)  30 us
    ppermute x4, starting transfers between devices, along_y(): second = lax.ppermute(second, ('arm', 'gy'), second_pairs)  29.9 us
    all_to_all x2, blocking collectives, swap(): return lax.all_to_all(spread, axis, 0, 0, axis_index_groups=groups)  27.1 us
    all_to_all x1, waiting for transfers between devices, local(): recv = lax.all_to_all(payload, 'arm', 0, 0)  14.5 us
    ppermute x4, waiting for transfers between devices, along_y(): second = lax.ppermute(second, ('arm', 'gy'), second_pairs)  14.5 us
    ppermute x4, waiting for transfers between devices, along_y(): return (lax.ppermute(first, ('arm', 'gy'), first_pairs), second)  10 us
    ppermute x2, waiting for transfers between devices, along_x(): low = lax.ppermute(right, 'gx', [(i, (i + 1) % m) for i in range(m)])  8.36 us
    ppermute x4, starting transfers between devices, along_y(): return (lax.ppermute(first, ('arm', 'gy'), first_pairs), second)  7.99 us
  transfers between devices with their start and end apart: 13, of which 8 were waited for; matrix products, arithmetic and copies ran while one was open for 0% of the time, Pallas kernels for 0%

profile of v5, /device:TPU:6, one launch (start us, length us, event | category | flops | bytes accessed | tf_op | source)
XLA Modules:
  0.0 168.1 jit_solution(16064351366010034877)
XLA Ops:
  0.6 0.0 copy-start
  0.6 1.0 copy-done
  1.7 0.9 shard_map.41
  2.6 5.9 %all-to-all-start = ((f32[4,256,128]{2,1,0:T(8,128)}), f32[4,256,128]{2,1,0:T(8,128)S(1)}, u32[]{:S(2)}, u32[]{:S(2)}) async-start(f32[4,256,128]{2,1,0:T(8,128)} %shard_map.41), calls=%async_computation | async-start | bytes 1048576 | tf_op jit(solution)/shard_map/all_to_all | solution.py:359
  8.5 14.5 %all-to-all-done.recv = f32[4,256,128]{2,1,0:T(8,128)S(1)} async-done(((f32[4,256,128]{2,1,0:T(8,128)}), f32[4,256,128]{2,1,0:T(8,128)S(1)}, u32[]{:S(2)}, u32[]{:S(2)}) %all-to-all-start) | async-done | bytes 524320 | tf_op jit(solution)/shard_map/all_to_all | solution.py:359
  22.9 0.2 shard_map.42
  23.2 1.9 %collective-permute-start = (f32[32,3,8,128]{3,2,1,0:T(8,128)S(1)}, f32[32,3,8,128]{3,2,1,0:T(8,128)S(1)}, u32[]{:S(2)}, u32[]{:S(2)}) collective-permute-start(f32[32,3,8,128]{3,2,1,0:T(8,128)S(1)} %get-tuple-element.31), channel_id=1, source_target_pairs={{0,128},{128,0},{256,384},{384,256},{1,129},{129,1},{257,385},{385... | collective-permute-start | bytes 1179656 | tf_op jit(solution)/shard_map/ppermute | solution.py:337
  25.1 11.2 %collective-permute-start.1 = (f32[32,3,8,128]{3,2,1,0:T(8,128)S(1)}, f32[32,3,8,128]{3,2,1,0:T(8,128)S(1)}, u32[]{:S(2)}, u32[]{:S(2)}) collective-permute-start(f32[32,3,8,128]{3,2,1,0:T(8,128)S(1)} %get-tuple-element.32), channel_id=1, source_target_pairs={{0,399},{128,256},{256,128},{384,1},{1,384},{129,257},{257,129},{3... | collective-permute-start | bytes 1179656 | tf_op jit(solution)/shard_map/ppermute | solution.py:336
  36.3 0.0 collective-permute-done.first.y1
  36.3 8.2 %collective-permute-done.1.second.y2 = f32[32,3,8,128]{3,2,1,0:T(8,128)S(1)} collective-permute-done((f32[32,3,8,128]{3,2,1,0:T(8,128)S(1)}, f32[32,3,8,128]{3,2,1,0:T(8,128)S(1)}, u32[]{:S(2)}, u32[]{:S(2)}) %collective-permute-start.1) | collective-permute-done | bytes 393248 | tf_op jit(solution)/shard_map/ppermute | solution.py:336
  44.6 0.0 collective-permute-start.2
  44.6 1.7 %collective-permute-start.3 = (f32[58,8,128]{2,1,0:T(8,128)S(1)}, f32[58,8,128]{2,1,0:T(8,128)S(1)}, u32[]{:S(2)}, u32[]{:S(2)}) collective-permute-start(f32[58,8,128]{2,1,0:T(8,128)S(1)} %get-tuple-element.34), channel_id=1, source_target_pairs={{0,112},{16,0},{32,16},{48,32},{64,48},{80,64},{96,80},{112,96},{1... | collective-permute-start | bytes 712712 | tf_op jit(solution)/shard_map/ppermute | solution.py:342
  46.4 3.8 %collective-permute-done.2.xlow = f32[58,8,128]{2,1,0:T(8,128)S(1)} collective-permute-done((f32[58,8,128]{2,1,0:T(8,128)S(1)}, f32[58,8,128]{2,1,0:T(8,128)S(1)}, u32[]{:S(2)}, u32[]{:S(2)}) %collective-permute-start.2) | collective-permute-done | bytes 237600 | tf_op jit(solution)/shard_map/ppermute | solution.py:341
  50.1 0.0 collective-permute-done.3.xhigh
  50.2 1.9 %shard_map.44 = (f32[46,10,8,128]{3,2,1,0:T(8,128)S(1)}, f32[32,4,8,128]{3,2,1,0:T(8,128)S(1)}, f32[32,4,8,128]{3,2,1,0:T(8,128)S(1)}, f32[40,4,8,128]{3,2,1,0:T...) custom-call(s32[1]{0:T(128)} %bitcast.arm, f32[32,4,8,128]{3,2,1,0:T(8,128)S(1)} %bitcast.8, ...), custom_call_target="tpu_custom_call" | custom-call | tf_op jit(solution)/shard_map/pallas_call | solution.py:377
  52.1 1.9 %collective-permute-start.4 = (f32[140,8,128]{2,1,0:T(8,128)S(1)}, f32[140,8,128]{2,1,0:T(8,128)S(1)}, u32[]{:S(2)}, u32[]{:S(2)}) collective-permute-start(f32[140,8,128]{2,1,0:T(8,128)S(1)} %get-tuple-element.36), channel_id=1, source_target_pairs={{0,128},{128,0},{256,384},{384,256},{1,129},{129,1},{257,385},{385... | collective-permute-start | bytes 1720328 | tf_op jit(solution)/shard_map/ppermute | solution.py:337
  54.0 7.0 %collective-permute-start.5 = (f32[140,8,128]{2,1,0:T(8,128)S(1)}, f32[140,8,128]{2,1,0:T(8,128)S(1)}, u32[]{:S(2)}, u32[]{:S(2)}) collective-permute-start(f32[140,8,128]{2,1,0:T(8,128)S(1)} %get-tuple-element.37), channel_id=1, source_target_pairs={{0,399},{128,256},{256,128},{384,1},{1,384},{129,257},{257,129},{3... | collective-permute-start | bytes 1720328 | tf_op jit(solution)/shard_map/ppermute | solution.py:336
  61.0 8.0 %collective-permute-done.4.y1 = f32[140,8,128]{2,1,0:T(8,128)S(1)} collective-permute-done((f32[140,8,128]{2,1,0:T(8,128)S(1)}, f32[140,8,128]{2,1,0:T(8,128)S(1)}, u32[]{:S(2)}, u32[]{:S(2)}) %collective-permute-start.4) | collective-permute-done | bytes 573472 | tf_op jit(solution)/shard_map/ppermute | solution.py:337
  69.0 5.2 %collective-permute-done.5.y2 = f32[140,8,128]{2,1,0:T(8,128)S(1)} collective-permute-done((f32[140,8,128]{2,1,0:T(8,128)S(1)}, f32[140,8,128]{2,1,0:T(8,128)S(1)}, u32[]{:S(2)}, u32[]{:S(2)}) %collective-permute-start.5) | collective-permute-done | bytes 573472 | tf_op jit(solution)/shard_map/ppermute | solution.py:336
  74.3 2.6 %shard_map.45 = (f32[32,4,8,128]{3,2,1,0:T(8,128)S(1)}, f32[32,4,8,128]{3,2,1,0:T(8,128)S(1)}, f32[32,4,8,128]{3,2,1,0:T(8,128)S(1)}, f32[32,4,8,128]{3,2,1,0:T(...) custom-call(s32[1]{0:T(128)} %bitcast.arm, f32[40,4,8,128]{3,2,1,0:T(8,128)S(1)} %get-tuple-element.35.wide.s4, ...), custom_call_target="tpu_custom_call" | custom-call | tf_op jit(solution)/shard_map/pallas_call | solution.py:385
  76.8 7.0 %collective-permute-start.7 = (f32[32,4,8,128]{3,2,1,0:T(8,128)S(1)}, f32[32,4,8,128]{3,2,1,0:T(8,128)S(1)}, u32[]{:S(2)}, u32[]{:S(2)}) collective-permute-start(f32[32,4,8,128]{3,2,1,0:T(8,128)S(1)} %get-tuple-element.40.own), channel_id=1, source_target_pairs={{0,399},{128,256},{256,128},{384,1},{1,384},{129,257},{257,129},{3... | collective-permute-start | bytes 1572872 | tf_op jit(solution)/shard_map/ppermute | solution.py:336
  83.8 1.9 %collective-permute-start.6 = (f32[32,4,8,128]{3,2,1,0:T(8,128)S(1)}, f32[32,4,8,128]{3,2,1,0:T(8,128)S(1)}, u32[]{:S(2)}, u32[]{:S(2)}) collective-permute-start(f32[32,4,8,128]{3,2,1,0:T(8,128)S(1)} %get-tuple-element.40.own), channel_id=1, source_target_pairs={{0,128},{128,0},{256,384},{384,256},{1,129},{129,1},{257,385},{385... | collective-permute-start | bytes 1572872 | tf_op jit(solution)/shard_map/ppermute | solution.py:337
  85.7 12.2 %all_to_all.20.rest_0_ = f32[32,8,128]{2,1,0:T(8,128)S(1)} all-to-all(f32[32,8,128]{2,1,0:T(8,128)S(1)} %get-tuple-element.41), channel_id=1, replica_groups={{0,4,8,12,16,20,24,28,32,36,40,44,48,52,56,60,64,68,72,76,80,84,88,92,9..., dimensions={0} | all-to-all | bytes 262144 | tf_op jit(solution)/shard_map/all_to_all | solution.py:354
  97.9 0.0 collective-permute-done.7.second.y2
  97.9 2.0 %collective-permute-done.6.first.y1 = f32[32,4,8,128]{3,2,1,0:T(8,128)S(1)} collective-permute-done((f32[32,4,8,128]{3,2,1,0:T(8,128)S(1)}, f32[32,4,8,128]{3,2,1,0:T(8,128)S(1)}, u32[]{:S(2)}, u32[]{:S(2)}) %collective-permute-start.6) | collective-permute-done | bytes 524320 | tf_op jit(solution)/shard_map/ppermute | solution.py:337
  99.9 0.1 shard_map.46
  100.0 0.0 collective-permute-start.8
  100.0 1.7 %collective-permute-start.9 = (f32[76,8,128]{2,1,0:T(8,128)S(1)}, f32[76,8,128]{2,1,0:T(8,128)S(1)}, u32[]{:S(2)}, u32[]{:S(2)}) collective-permute-start(f32[76,8,128]{2,1,0:T(8,128)S(1)} %get-tuple-element.43), channel_id=1, source_target_pairs={{0,112},{16,0},{32,16},{48,32},{64,48},{80,64},{96,80},{112,96},{1... | collective-permute-start | bytes 933896 | tf_op jit(solution)/shard_map/ppermute | solution.py:342
  101.7 4.6 %collective-permute-done.8.xlow = f32[76,8,128]{2,1,0:T(8,128)S(1)} collective-permute-done((f32[76,8,128]{2,1,0:T(8,128)S(1)}, f32[76,8,128]{2,1,0:T(8,128)S(1)}, u32[]{:S(2)}, u32[]{:S(2)}) %collective-permute-start.8) | collective-permute-done | bytes 311328 | tf_op jit(solution)/shard_map/ppermute | solution.py:341
  106.3 0.0 collective-permute-done.9.xhigh
  106.3 0.0 copy-start.2
  106.3 3.3 %shard_map.47 = (f32[32,4,8,128]{3,2,1,0:T(8,128)S(1)}, f32[40,4,8,128]{3,2,1,0:T(8,128)S(1)}, f32[140,8,128]{2,1,0:T(8,128)S(1)}, f32[140,8,128]{2,1,0:T(8,128)S(1)}, f32[4,8,128]{2,1,0:T(8,128)S(1)}) custom-call(s32[1]{0:T(128)} %bitcast.arm, f32[32,4,8,128]{3,2,1,0:T(8,128)S(1)} %get-tuple-element.40.own, f32[76,8,128]{2,1,0:T(8,128)S(1)} %collective-permute-done.8.xlow, ...), custom_call_target="tpu_custom_call" | custom-call | tf_op jit(solution)/shard_map/pallas_call | solution.py:400
  109.6 2.2 %collective-permute-start.10 = (f32[140,8,128]{2,1,0:T(8,128)S(1)}, f32[140,8,128]{2,1,0:T(8,128)S(1)}, u32[]{:S(2)}, u32[]{:S(2)}) collective-permute-start(f32[140,8,128]{2,1,0:T(8,128)S(1)} %get-tuple-element.50), channel_id=1, source_target_pairs={{0,128},{128,0},{256,384},{384,256},{1,129},{129,1},{257,385},{385... | collective-permute-start | bytes 1720328 | tf_op jit(solution)/shard_map/ppermute | solution.py:337
  111.8 4.7 %collective-permute-start.11 = (f32[140,8,128]{2,1,0:T(8,128)S(1)}, f32[140,8,128]{2,1,0:T(8,128)S(1)}, u32[]{:S(2)}, u32[]{:S(2)}) collective-permute-start(f32[140,8,128]{2,1,0:T(8,128)S(1)} %get-tuple-element.51), channel_id=1, source_target_pairs={{0,399},{128,256},{256,128},{384,1},{1,384},{129,257},{257,129},{3... | collective-permute-start | bytes 1720328 | tf_op jit(solution)/shard_map/ppermute | solution.py:336
  116.6 14.9 %all_to_all.21.got = f32[4,8,128]{2,1,0:T(8,128)S(1)} all-to-all(f32[4,8,128]{2,1,0:T(8,128)S(1)} %get-tuple-element.55), channel_id=1, replica_groups={{0,1,2,3},{4,5,6,7},{8,9,10,11},{12,13,14,15},{16,17,18,19},{20,21,22,2..., dimensions={0} | all-to-all | bytes 32768 | tf_op jit(solution)/shard_map/all_to_all | solution.py:354
  131.5 0.0 collective-permute-done.10.y1
  131.5 1.0 collective-permute-done.11.y2
  132.5 0.0 copy-done.2
  132.5 3.7 %shard_map.48 = f32[4,520,128]{2,1,0:T(8,128)S(1)} custom-call(s32[1]{0:T(128)} %bitcast.arm, f32[4,4]{1,0:T(4,128)S(1)} %copy-done.2, f32[40,4,8,128]{3,2,1,0:T(8,128)S(1)} %get-tuple-element.49.wide, f32[140,8,128]{2,1,0:T(8,128)S(1)} %collective-permute-done.10.y1, f32[140,8,128]{2,1,0:T(8,128)S(1)} %collective-permute-done.11.y2, ...), custom_call_target="tpu_custom_call" | custom-call | tf_op jit(solution)/shard_map/pallas_call | solution.py:409
  136.2 0.0 copy-start.1
  136.2 30.0 %all_to_all.22.back = f32[4,520,128]{2,1,0:T(8,128)S(1)} all-to-all(f32[4,520,128]{2,1,0:T(8,128)S(1)} %shard_map.48), channel_id=1, replica_groups=mesh['arm'=4,'gx'=8,'gy'=16] {'arm'}, dimensions={0} | all-to-all | bytes 2129920 | tf_op jit(solution)/shard_map/all_to_all | solution.py:417
  166.1 0.0 copy-done.1
  166.1 2.0 %shard_map.49 = (f32[32,16,256]{2,1,0:T(8,128)}, f32[32,16,256]{2,1,0:T(8,128)}) custom-call(s32[1]{0:T(128)} %bitcast.arm, f32[4,4]{1,0:T(4,128)S(1)} %copy-done.2, f32[4,520,128]{2,1,0:T(8,128)S(1)} %all_to_all.22.back, f32[32,16,256]{2,1,0:T(8,128)S(1)} %bitcast.6), custom_call_target="tpu_custom_call" | custom-call | tf_op jit(solution)/shard_map/pallas_call | solution.py:419
  (1 shorter events, 0.0 us)
Async XLA Ops:
  0.6 1.0 copy-start
  2.6 20.4 %all-to-all-start = ((f32[4,256,128]{2,1,0:T(8,128)}), f32[4,256,128]{2,1,0:T(8,128)S(1)}, u32[]{:S(2)}, u32[]{:S(2)}) async-start(f32[4,256,128]{2,1,0:T(8,128)} %shard_map.41), calls=%async_computation | async-start | bytes 1048576 | tf_op jit(solution)/shard_map/all_to_all | solution.py:359
  23.2 13.2 %collective-permute-start = (f32[32,3,8,128]{3,2,1,0:T(8,128)S(1)}, f32[32,3,8,128]{3,2,1,0:T(8,128)S(1)}, u32[]{:S(2)}, u32[]{:S(2)}) collective-permute-start(f32[32,3,8,128]{3,2,1,0:T(8,128)S(1)} %get-tuple-element.31), channel_id=1, source_target_pairs={{0,128},{128,0},{256,384},{384,256},{1,129},{129,1},{257,385},{385... | collective-permute-start | bytes 1179656 | tf_op jit(solution)/shard_map/ppermute | solution.py:337
  25.1 19.5 %collective-permute-start.1 = (f32[32,3,8,128]{3,2,1,0:T(8,128)S(1)}, f32[32,3,8,128]{3,2,1,0:T(8,128)S(1)}, u32[]{:S(2)}, u32[]{:S(2)}) collective-permute-start(f32[32,3,8,128]{3,2,1,0:T(8,128)S(1)} %get-tuple-element.32), channel_id=1, source_target_pairs={{0,399},{128,256},{256,128},{384,1},{1,384},{129,257},{257,129},{3... | collective-permute-start | bytes 1179656 | tf_op jit(solution)/shard_map/ppermute | solution.py:336
  44.6 5.5 %collective-permute-start.2 = (f32[58,8,128]{2,1,0:T(8,128)S(1)}, f32[58,8,128]{2,1,0:T(8,128)S(1)}, u32[]{:S(2)}, u32[]{:S(2)}) collective-permute-start(f32[58,8,128]{2,1,0:T(8,128)S(1)} %get-tuple-element.33), channel_id=1, source_target_pairs={{0,16},{16,32},{32,48},{48,64},{64,80},{80,96},{96,112},{112,0},{1... | collective-permute-start | bytes 712712 | tf_op jit(solution)/shard_map/ppermute | solution.py:341
  44.6 5.5 %collective-permute-start.3 = (f32[58,8,128]{2,1,0:T(8,128)S(1)}, f32[58,8,128]{2,1,0:T(8,128)S(1)}, u32[]{:S(2)}, u32[]{:S(2)}) collective-permute-start(f32[58,8,128]{2,1,0:T(8,128)S(1)} %get-tuple-element.34), channel_id=1, source_target_pairs={{0,112},{16,0},{32,16},{48,32},{64,48},{80,64},{96,80},{112,96},{1... | collective-permute-start | bytes 712712 | tf_op jit(solution)/shard_map/ppermute | solution.py:342
  52.1 16.9 %collective-permute-start.4 = (f32[140,8,128]{2,1,0:T(8,128)S(1)}, f32[140,8,128]{2,1,0:T(8,128)S(1)}, u32[]{:S(2)}, u32[]{:S(2)}) collective-permute-start(f32[140,8,128]{2,1,0:T(8,128)S(1)} %get-tuple-element.36), channel_id=1, source_target_pairs={{0,128},{128,0},{256,384},{384,256},{1,129},{129,1},{257,385},{385... | collective-permute-start | bytes 1720328 | tf_op jit(solution)/shard_map/ppermute | solution.py:337
  54.0 20.2 %collective-permute-start.5 = (f32[140,8,128]{2,1,0:T(8,128)S(1)}, f32[140,8,128]{2,1,0:T(8,128)S(1)}, u32[]{:S(2)}, u32[]{:S(2)}) collective-permute-start(f32[140,8,128]{2,1,0:T(8,128)S(1)} %get-tuple-element.37), channel_id=1, source_target_pairs={{0,399},{128,256},{256,128},{384,1},{1,384},{129,257},{257,129},{3... | collective-permute-start | bytes 1720328 | tf_op jit(solution)/shard_map/ppermute | solution.py:336
  76.8 21.1 %collective-permute-start.7 = (f32[32,4,8,128]{3,2,1,0:T(8,128)S(1)}, f32[32,4,8,128]{3,2,1,0:T(8,128)S(1)}, u32[]{:S(2)}, u32[]{:S(2)}) collective-permute-start(f32[32,4,8,128]{3,2,1,0:T(8,128)S(1)} %get-tuple-element.40.own), channel_id=1, source_target_pairs={{0,399},{128,256},{256,128},{384,1},{1,384},{129,257},{257,129},{3... | collective-permute-start | bytes 1572872 | tf_op jit(solution)/shard_map/ppermute | solution.py:336
  83.8 16.1 %collective-permute-start.6 = (f32[32,4,8,128]{3,2,1,0:T(8,128)S(1)}, f32[32,4,8,128]{3,2,1,0:T(8,128)S(1)}, u32[]{:S(2)}, u32[]{:S(2)}) collective-permute-start(f32[32,4,8,128]{3,2,1,0:T(8,128)S(1)} %get-tuple-element.40.own), channel_id=1, source_target_pairs={{0,128},{128,0},{256,384},{384,256},{1,129},{129,1},{257,385},{385... | collective-permute-start | bytes 1572872 | tf_op jit(solution)/shard_map/ppermute | solution.py:337
  100.0 6.3 %collective-permute-start.8 = (f32[76,8,128]{2,1,0:T(8,128)S(1)}, f32[76,8,128]{2,1,0:T(8,128)S(1)}, u32[]{:S(2)}, u32[]{:S(2)}) collective-permute-start(f32[76,8,128]{2,1,0:T(8,128)S(1)} %get-tuple-element.42), channel_id=1, source_target_pairs={{0,16},{16,32},{32,48},{48,64},{64,80},{80,96},{96,112},{112,0},{1... | collective-permute-start | bytes 933896 | tf_op jit(solution)/shard_map/ppermute | solution.py:341
  100.0 6.3 %collective-permute-start.9 = (f32[76,8,128]{2,1,0:T(8,128)S(1)}, f32[76,8,128]{2,1,0:T(8,128)S(1)}, u32[]{:S(2)}, u32[]{:S(2)}) collective-permute-start(f32[76,8,128]{2,1,0:T(8,128)S(1)} %get-tuple-element.43), channel_id=1, source_target_pairs={{0,112},{16,0},{32,16},{48,32},{64,48},{80,64},{96,80},{112,96},{1... | collective-permute-start | bytes 933896 | tf_op jit(solution)/shard_map/ppermute | solution.py:342
  106.3 26.2 %copy-start.2 = (f32[4,4]{1,0:T(4,128)S(1)}, f32[4,4]{1,0:T(4,128)}, u32[]{:S(2)}) copy-start(f32[4,4]{1,0:T(4,128)} %chi.3) | copy-start | bytes 196
  109.6 21.9 %collective-permute-start.10 = (f32[140,8,128]{2,1,0:T(8,128)S(1)}, f32[140,8,128]{2,1,0:T(8,128)S(1)}, u32[]{:S(2)}, u32[]{:S(2)}) collective-permute-start(f32[140,8,128]{2,1,0:T(8,128)S(1)} %get-tuple-element.50), channel_id=1, source_target_pairs={{0,128},{128,0},{256,384},{384,256},{1,129},{129,1},{257,385},{385... | collective-permute-start | bytes 1720328 | tf_op jit(solution)/shard_map/ppermute | solution.py:337
  111.8 20.6 %collective-permute-start.11 = (f32[140,8,128]{2,1,0:T(8,128)S(1)}, f32[140,8,128]{2,1,0:T(8,128)S(1)}, u32[]{:S(2)}, u32[]{:S(2)}) collective-permute-start(f32[140,8,128]{2,1,0:T(8,128)S(1)} %get-tuple-element.51), channel_id=1, source_target_pairs={{0,399},{128,256},{256,128},{384,1},{1,384},{129,257},{257,129},{3... | collective-permute-start | bytes 1720328 | tf_op jit(solution)/shard_map/ppermute | solution.py:336
  136.2 30.0 %copy-start.1 = (f32[1,32,16,256]{3,2,1,0:T(8,128)S(1)}, f32[1,32,16,256]{3,2,1,0:T(8,128)}, u32[]{:S(2)}) copy-start(f32[1,32,16,256]{3,2,1,0:T(8,128)} %param.2) | copy-start | bytes 1572868

commit v6 on v5

--- a/solution.py
+++ b/solution.py
@@ -68,7 +68,7 @@
                 ]
 
 
-def interleave_kernel(arm, recv, coef, sums, first, second):
+def interleave_kernel(arm, recv, coef, sums, left, right, first, second):
     n = BX * BY
     for s in range(SPECIES):
         for half in range(2):
@@ -78,8 +78,12 @@
         sums[s : s + 1, :] = jnp.sum(recv[s], axis=0, keepdims=True)
     sums[4:8, :] = jnp.zeros((4, LANES), jnp.float32)
 
+    cells = coef[...].reshape(BX, BY, 8, LANES)
+    width = left.shape[0]
+    left[...] = cells[:width]
+    right[...] = cells[BX - width :]
+
     def body(up, down):
-        cells = coef[...].reshape(BX, BY, 8, LANES)
         for j in range(len(COEF_REACH)):
             up[:, j] = cells[:, j]
             down[:, BY - 2 - j] = cells[:, BY - 1 - j]
@@ -99,12 +103,22 @@
         body(first, second)
 
 
-def pack_sides(reach, arm, own, first, second, *rest):
-    if len(rest) == 4:
-        got, left, right, total = rest
-        total[...] = jnp.sum(got[...], axis=0)
-    else:
-        left, right = rest
+def pack_corners(reach, arm, low, high, first, second):
+    width = low.shape[0]
+
+    def body(up, down):
+        at = 0
+        for j, r in enumerate(reach):
+            for dst, y in ((up, j), (down, BY - 1 - j)):
+                dst[at : at + r] = low[width - r : width, y]
+                dst[at + r : at + 2 * r] = high[0:r, y]
+            at += 2 * r
+
+    by_side(arm, first, second, body)
+
+
+def pack_sides(reach, arm, own, first, second, got, left, right, total):
+    total[...] = jnp.sum(got[...], axis=0)
     width, depth = reach[0] + 1, len(reach)
 
     def put(at, src, y, r):
@@ -176,8 +190,27 @@
     by_side(arm, first, second, body)
 
 
-def inner_first(arm, own, xlow, xhigh, y1, y2, coef, s2, s3, wide, e1, e2, a, b):
-    surround(arm, coef, COEF_REACH, own, y1, y2, xlow, xhigh, (7, 3))
+def inner_first(
+    arm, own, xlow, xhigh, y1, y2, c1, c2, coef, s2, s3, wide, e1, e2, a, b
+):
+    coef[0:7, 3:7] = xlow[...]
+    coef[7 : 7 + BX, 3:7] = own[...]
+    coef[7 + BX :, 3:7] = xhigh[...]
+
+    def rows(low, high):
+        coef[7 : 7 + BX, 0:3] = low[...]
+        coef[7 : 7 + BX, 7:10] = high[...]
+
+    def corners(low, high):
+        at = 0
+        for j, r in enumerate(COEF_REACH):
+            for src, y in ((low, 2 - j), (high, 7 + j)):
+                coef[7 - r : 7, y] = src[at : at + r]
+                coef[7 + BX : 7 + BX + r, y] = src[at + r : at + 2 * r]
+            at += 2 * r
+
+    by_side(arm, y1, y2, rows)
+    by_side(arm, c1, c2, corners)
     here = (slice(7, 7 + BX), slice(3, 7))
     a[...] = 6.0 + coef[...]
     step(a, b, coef, (7, 3), 6, 2, (0, 0))
@@ -223,10 +256,10 @@
 
 
 def outer_first(
-    arm, own, xlow, xhigh, y1, y2, coef, s4, s5, s6, s7, s8, total,
-    dens, wide, e1, e2, spread, a, b
+    arm, own, xlow, xhigh, y1, y2, coef, s4, s5, s6, s7, s8, total, other,
+    dens, wide, e1, e2, both, a, b
 ):
-    spread[...] = jnp.broadcast_to(total[...], spread.shape)
+    both[...] = total[...] + other[...]
     surround(arm, a, JUNC_REACH, own, y1, y2, xlow, xhigh, (8, 4))
     here = (slice(8, 8 + BX), slice(4, 8))
     shift = (-1, -1)
@@ -242,7 +275,7 @@
 
 
 def outer_second(
-    arm, chi, wide, y1, y2, coef, s2, s3, dens, got, out, a, b, flat, mixed
+    arm, chi, wide, y1, y2, coef, s2, s3, dens, total, other, out, a, b, flat, mixed
 ):
     a[0 : BX + 8, 4:8] = wide[...]
     unpack(arm, a, MID_REACH, y1, y2, (4, 4))
@@ -258,16 +291,16 @@
     d = flat[...].reshape(BX, BY, 8, LANES) + 0.5 * a[here]
     flat[...] = d.reshape(rows)
     row = lax.broadcasted_iota(jnp.int32, (8, LANES), 0) % 4
-    total = None
+    mixture = None
     for k in range(SPECIES):
         weight = jnp.zeros((8, LANES), jnp.float32)
         for s in range(SPECIES):
             weight = jnp.where(row == s, chi[s, (s + k) % SPECIES] + compress, weight)
         term = weight * (others(d, k) if k else d)
-        total = term if total is None else total + term
-    mixed[...] = total.reshape(rows)
+        mixture = term if mixture is None else mixture + term
+    mixed[...] = mixture.reshape(rows)
     n = BX * BY
-    tail = jnp.sum(got[...], axis=0)
+    tail = total[...] + other[...]
     for s in range(SPECIES):
         for i, src in enumerate((flat, mixed)):
             for half in range(2):
@@ -342,35 +375,38 @@
         high = lax.ppermute(left, "gx", [(i, (i - 1) % m) for i in range(m)])
         return low, high
 
-    parts = size_gy // arms
-    z_groups = [[y * parts + z for z in range(parts)] for y in range(size_gy // parts)]
-    y_groups = [list(g) for g in zip(*z_groups)]
-
+    parts = 4
     xy_groups = [
-        [x * size_gy + g for x in range(size_gx) for g in group] for group in y_groups
+        [x * size_gy + g for x in range(size_gx) for g in range(z, size_gy, parts)]
+        for z in range(parts)
     ]
 
-    def swap(spread, axis, groups):
-        return lax.all_to_all(spread, axis, 0, 0, axis_index_groups=groups)
+    def along_z(tile, bit):
+        return lax.ppermute(tile, "gy", [(i, i ^ bit) for i in range(size_gy)])
 
     payload = call(
         spread_kernel, jax.ShapeDtypeStruct((arms, 2 * n, LANES), jnp.float32), arrays=1
     )(field_here)
     recv = lax.all_to_all(payload, "arm", 0, 0)
     rows = tiles(BX, len(COEF_REACH))
-    coef_flat, sums, e1, e2 = call(
+    edge = tiles(COEF_REACH[0] + 1, BY)
+    coef_flat, sums, left, right, e1, e2 = call(
         interleave_kernel,
-        (jax.ShapeDtypeStruct((8 * n, LANES), jnp.float32), tiles(), rows, rows),
+        (jax.ShapeDtypeStruct((8 * n, LANES), jnp.float32), tiles(), edge, edge, rows, rows),
         scalars=1,
         arrays=1,
     )(arm, recv)
     coef_own = coef_flat.reshape(BX, BY, 8, LANES)
+    corner = tiles(2 * sum(COEF_REACH))
     y1, y2 = along_y(e1, e2)
-    side = tiles(side_size(COEF_REACH))
-    left, right = call(
-        functools.partial(pack_sides, COEF_REACH), (side, side), scalars=1, arrays=3
-    )(arm, coef_own, y1, y2)
     xlow, xhigh = along_x(left, right)
+    c1, c2 = call(
+        functools.partial(pack_corners, COEF_REACH),
+        (corner, corner),
+        scalars=1,
+        arrays=2,
+    )(arm, xlow, xhigh)
+    c1, c2 = along_y(c1, c2)
 
     own, wide_shape = tiles(BX, BY), tiles(BX + 8, BY)
     mid = tiles(packed_size(MID_REACH))
@@ -379,8 +415,8 @@
         (tiles(14 + BX, 6 + BY), own, own, wide_shape, mid, mid),
         [scratch(14 + BX, 6 + BY)] * 2,
         scalars=1,
-        arrays=5,
-    )(arm, coef_own, xlow, xhigh, y1, y2)
+        arrays=7,
+    )(arm, coef_own, xlow, xhigh, y1, y2, c1, c2)
     y1, y2 = along_y(e1, e2)
     s5, s6, s7, s8, junction, spread = call(
         inner_second,
@@ -391,28 +427,32 @@
     )(arm, s4, y1, y2, coef, sums)
 
     y1, y2 = along_y(junction, junction)
-    got = swap(spread, ("gx", "gy"), xy_groups)
+    got = lax.all_to_all(spread, ("gx", "gy"), 0, 0, axis_index_groups=xy_groups)
     side = tiles(side_size(JUNC_REACH))
     left, right, total = call(
-        functools.partial(pack_sides, JUNC_REACH), (side, side, tiles()), scalars=1, arrays=4
+        functools.partial(pack_sides, JUNC_REACH),
+        (side, side, tiles()),
+        scalars=1,
+        arrays=4,
     )(arm, junction, y1, y2, got)
     xlow, xhigh = along_x(left, right)
-    dens, wide, e1, e2, spread = call(
+    other = along_z(total, 1)
+    dens, wide, e1, e2, total = call(
         outer_first,
-        (own, wide_shape, mid, mid, tiles(parts)),
+        (own, wide_shape, mid, mid, tiles()),
         [scratch(16 + BX, 8 + BY)] * 2,
         scalars=1,
-        arrays=12,
-    )(arm, junction, xlow, xhigh, y1, y2, coef, s4, s5, s6, s7, s8, total)
+        arrays=13,
+    )(arm, junction, xlow, xhigh, y1, y2, coef, s4, s5, s6, s7, s8, total, other)
     y1, y2 = along_y(e1, e2)
-    got = swap(spread, "gy", z_groups)
+    other = along_z(total, 2)
     out = call(
         outer_second,
         jax.ShapeDtypeStruct((arms, 4 * n + 8, LANES), jnp.float32),
         [scratch(BX + 8, BY + 8)] * 2 + [pltpu.VMEM((8 * n, LANES), jnp.float32)] * 2,
         scalars=2,
-        arrays=8,
-    )(arm, flory_chi, wide, y1, y2, coef, s2, s3, dens, got)
+        arrays=9,
+    )(arm, flory_chi, wide, y1, y2, coef, s2, s3, dens, total, other)
 
     back = lax.all_to_all(out, "arm", 0, 0)
     result = jax.ShapeDtypeStruct(field_here.shape, jnp.float32)

time: 169 us -> 169 us (level)
  blocking collectives: 57 us -> 39.7 us
  waiting for transfers between devices: 47.3 us -> 56.7 us
  starting transfers between devices: 47.3 us -> 55.7 us
    ppermute x0 -> x2, waiting for transfers between devices: none -> 19.8 us  [along_z(): return lax.ppermute(tile, 'gy', [(i, i ^ bit) for i in range(size_gy)])]
    all_to_all x2 -> x1, blocking collectives: 27.1 us -> 13.2 us  [local(): lax.all_to_all(spread, ('gx', 'gy'), 0, 0, axis_index_groups=xy_groups)]
    ppermute x2, waiting for transfers between devices: 8.36 us -> 2.47 us  [along_x(): low = lax.ppermute(right, 'gx', [(i, (i + 1) % m) for i in range(m)])]
    ppermute x4 -> x5, waiting for transfers between devices: 14.5 us -> 10.1 us  [along_y(): second = lax.ppermute(second, ('arm', 'gy'), second_pairs)]
    ppermute x0 -> x2, starting transfers between devices: none -> 3.83 us  [along_z(): return lax.ppermute(tile, 'gy', [(i, i ^ bit) for i in range(size_gy)])]
    all_to_all x1, blocking collectives: 30 us -> 26.5 us  [local(): back = lax.all_to_all(out, 'arm', 0, 0)]
    ppermute x4 -> x5, starting transfers between devices: 29.9 us -> 32.7 us  [along_y(): second = lax.ppermute(second, ('arm', 'gy'), second_pairs)]
    ppermute x4 -> x5, starting transfers between devices: 7.99 us -> 9.76 us  [along_y(): return (lax.ppermute(first, ('arm', 'gy'), first_pairs), second)]
  transfers between devices with their start and end apart: 13 -> 17, of which waited for: 8 -> 7; matrix products, arithmetic and copies ran while one was open for 0% -> 0% of each run, Pallas kernels for 0% -> 0%
where the time goes in v6:
time: 169 us; the launch traced here: 168 us
  waiting for transfers between devices  56.7 us (34%)
  starting transfers between devices  55.7 us (33%)
  blocking collectives  39.7 us (23%)
  Pallas kernels  14.1 us (8%)
    ppermute x5, starting transfers between devices, along_y(): second = lax.ppermute(second, ('arm', 'gy'), second_pairs)  32.7 us
    all_to_all x1, blocking collectives, local(): back = lax.all_to_all(out, 'arm', 0, 0)  26.5 us
    ppermute x2, waiting for transfers between devices, along_z(): return lax.ppermute(tile, 'gy', [(i, i ^ bit) for i in range(size_gy)])  19.8 us
    all_to_all x1, waiting for transfers between devices, local(): recv = lax.all_to_all(payload, 'arm', 0, 0)  14.5 us
    all_to_all x1, blocking collectives, local(): lax.all_to_all(spread, ('gx', 'gy'), 0, 0, axis_index_groups=xy_groups)  13.2 us
    ppermute x5, waiting for transfers between devices, along_y(): second = lax.ppermute(second, ('arm', 'gy'), second_pairs)  10.1 us
    ppermute x5, waiting for transfers between devices, along_y(): return (lax.ppermute(first, ('arm', 'gy'), first_pairs), second)  9.83 us
    ppermute x5, starting transfers between devices, along_y(): return (lax.ppermute(first, ('arm', 'gy'), first_pairs), second)  9.76 us
  transfers between devices with their start and end apart: 17, of which 7 were waited for; matrix products, arithmetic and copies ran while one was open for 0% of the time, Pallas kernels for 0%

profile of v6, /device:TPU:6, one launch (start us, length us, event | category | flops | bytes accessed | tf_op | source)
XLA Modules:
  0.0 168.0 jit_solution(1140767532257102235)
XLA Ops:
  0.6 0.0 copy-start
  0.6 1.0 copy-done
  1.7 0.9 shard_map.41
  2.6 5.9 %all-to-all-start = ((f32[4,256,128]{2,1,0:T(8,128)}), f32[4,256,128]{2,1,0:T(8,128)S(1)}, u32[]{:S(2)}, u32[]{:S(2)}) async-start(f32[4,256,128]{2,1,0:T(8,128)} %shard_map.41), calls=%async_computation | async-start | bytes 1048576 | tf_op jit(solution)/shard_map/all_to_all | solution.py:390
  8.5 14.5 %all-to-all-done.recv = f32[4,256,128]{2,1,0:T(8,128)S(1)} async-done(((f32[4,256,128]{2,1,0:T(8,128)}), f32[4,256,128]{2,1,0:T(8,128)S(1)}, u32[]{:S(2)}, u32[]{:S(2)}) %all-to-all-start) | async-done | bytes 524320 | tf_op jit(solution)/shard_map/all_to_all | solution.py:390
  22.9 0.3 shard_map.42
  23.2 1.9 %collective-permute-start.2 = (f32[32,3,8,128]{3,2,1,0:T(8,128)S(1)}, f32[32,3,8,128]{3,2,1,0:T(8,128)S(1)}, u32[]{:S(2)}, u32[]{:S(2)}) collective-permute-start(f32[32,3,8,128]{3,2,1,0:T(8,128)S(1)} %get-tuple-element.35), channel_id=1, source_target_pairs={{0,128},{128,0},{256,384},{384,256},{1,129},{129,1},{257,385},{385... | collective-permute-start | bytes 1179656 | tf_op jit(solution)/shard_map/ppermute | solution.py:370
  25.2 11.2 %collective-permute-start.3 = (f32[32,3,8,128]{3,2,1,0:T(8,128)S(1)}, f32[32,3,8,128]{3,2,1,0:T(8,128)S(1)}, u32[]{:S(2)}, u32[]{:S(2)}) collective-permute-start(f32[32,3,8,128]{3,2,1,0:T(8,128)S(1)} %get-tuple-element.36), channel_id=1, source_target_pairs={{0,399},{128,256},{256,128},{384,1},{1,384},{129,257},{257,129},{3... | collective-permute-start | bytes 1179656 | tf_op jit(solution)/shard_map/ppermute | solution.py:369
  36.4 0.0 collective-permute-start
  36.4 1.7 %collective-permute-start.1 = (f32[7,4,8,128]{3,2,1,0:T(8,128)S(1)}, f32[7,4,8,128]{3,2,1,0:T(8,128)S(1)}, u32[]{:S(2)}, u32[]{:S(2)}) collective-permute-start(f32[7,4,8,128]{3,2,1,0:T(8,128)S(1)} %get-tuple-element.34), channel_id=1, source_target_pairs={{0,112},{16,0},{32,16},{48,32},{64,48},{80,64},{96,80},{112,96},{1... | collective-permute-start | bytes 344072 | tf_op jit(solution)/shard_map/ppermute | solution.py:375
  38.1 2.5 %collective-permute-done.low.xlow = f32[7,4,8,128]{3,2,1,0:T(8,128)S(1)} collective-permute-done((f32[7,4,8,128]{3,2,1,0:T(8,128)S(1)}, f32[7,4,8,128]{3,2,1,0:T(8,128)S(1)}, u32[]{:S(2)}, u32[]{:S(2)}) %collective-permute-start) | collective-permute-done | bytes 114720 | tf_op jit(solution)/shard_map/ppermute | solution.py:374
  40.6 0.0 collective-permute-done.1.high.xhigh
  40.6 1.9 %collective-permute-start.4 = (f32[30,8,128]{2,1,0:T(8,128)S(1)}, f32[30,8,128]{2,1,0:T(8,128)S(1)}, u32[]{:S(2)}, u32[]{:S(2)}) collective-permute-start(f32[30,8,128]{2,1,0:T(8,128)S(1)} %get-tuple-element.37), channel_id=1, source_target_pairs={{0,128},{128,0},{256,384},{384,256},{1,129},{129,1},{257,385},{385... | collective-permute-start | bytes 368648 | tf_op jit(solution)/shard_map/ppermute | solution.py:370
  42.6 5.4 %collective-permute-start.5 = (f32[30,8,128]{2,1,0:T(8,128)S(1)}, f32[30,8,128]{2,1,0:T(8,128)S(1)}, u32[]{:S(2)}, u32[]{:S(2)}) collective-permute-start(f32[30,8,128]{2,1,0:T(8,128)S(1)} %get-tuple-element.38), channel_id=1, source_target_pairs={{0,399},{128,256},{256,128},{384,1},{1,384},{129,257},{257,129},{3... | collective-permute-start | bytes 368648 | tf_op jit(solution)/shard_map/ppermute | solution.py:369
  48.0 0.0 collective-permute-done.4.c1
  48.0 4.9 %collective-permute-done.5.c2 = f32[30,8,128]{2,1,0:T(8,128)S(1)} collective-permute-done((f32[30,8,128]{2,1,0:T(8,128)S(1)}, f32[30,8,128]{2,1,0:T(8,128)S(1)}, u32[]{:S(2)}, u32[]{:S(2)}) %collective-permute-start.5) | collective-permute-done | bytes 122912 | tf_op jit(solution)/shard_map/ppermute | solution.py:369
  52.8 0.0 collective-permute-done.2.y1
  52.8 0.0 collective-permute-done.3.y2
  52.9 1.9 %shard_map.44 = (f32[46,10,8,128]{3,2,1,0:T(8,128)S(1)}, f32[32,4,8,128]{3,2,1,0:T(8,128)S(1)}, f32[32,4,8,128]{3,2,1,0:T(8,128)S(1)}, f32[40,4,8,128]{3,2,1,0:T...) custom-call(s32[1]{0:T(128)} %bitcast.arm, f32[32,4,8,128]{3,2,1,0:T(8,128)S(1)} %bitcast.7, ...), custom_call_target="tpu_custom_call" | custom-call | tf_op jit(solution)/shard_map/pallas_call | solution.py:413
  54.7 1.9 %collective-permute-start.6 = (f32[140,8,128]{2,1,0:T(8,128)S(1)}, f32[140,8,128]{2,1,0:T(8,128)S(1)}, u32[]{:S(2)}, u32[]{:S(2)}) collective-permute-start(f32[140,8,128]{2,1,0:T(8,128)S(1)} %get-tuple-element.40), channel_id=1, source_target_pairs={{0,128},{128,0},{256,384},{384,256},{1,129},{129,1},{257,385},{385... | collective-permute-start | bytes 1720328 | tf_op jit(solution)/shard_map/ppermute | solution.py:370
  56.7 6.0 %collective-permute-start.7 = (f32[140,8,128]{2,1,0:T(8,128)S(1)}, f32[140,8,128]{2,1,0:T(8,128)S(1)}, u32[]{:S(2)}, u32[]{:S(2)}) collective-permute-start(f32[140,8,128]{2,1,0:T(8,128)S(1)} %get-tuple-element.41), channel_id=1, source_target_pairs={{0,399},{128,256},{256,128},{384,1},{1,384},{129,257},{257,129},{3... | collective-permute-start | bytes 1720328 | tf_op jit(solution)/shard_map/ppermute | solution.py:369
  62.6 9.8 %collective-permute-done.6.y1 = f32[140,8,128]{2,1,0:T(8,128)S(1)} collective-permute-done((f32[140,8,128]{2,1,0:T(8,128)S(1)}, f32[140,8,128]{2,1,0:T(8,128)S(1)}, u32[]{:S(2)}, u32[]{:S(2)}) %collective-permute-start.6) | collective-permute-done | bytes 573472 | tf_op jit(solution)/shard_map/ppermute | solution.py:370
  72.5 5.2 %collective-permute-done.7.y2 = f32[140,8,128]{2,1,0:T(8,128)S(1)} collective-permute-done((f32[140,8,128]{2,1,0:T(8,128)S(1)}, f32[140,8,128]{2,1,0:T(8,128)S(1)}, u32[]{:S(2)}, u32[]{:S(2)}) %collective-permute-start.7) | collective-permute-done | bytes 573472 | tf_op jit(solution)/shard_map/ppermute | solution.py:369
  77.7 2.4 %shard_map.45 = (f32[32,4,8,128]{3,2,1,0:T(8,128)S(1)}, f32[32,4,8,128]{3,2,1,0:T(8,128)S(1)}, f32[32,4,8,128]{3,2,1,0:T(8,128)S(1)}, f32[32,4,8,128]{3,2,1,0:T(...) custom-call(s32[1]{0:T(128)} %bitcast.arm, f32[40,4,8,128]{3,2,1,0:T(8,128)S(1)} %get-tuple-element.39.wide.s4, ...), custom_call_target="tpu_custom_call" | custom-call | tf_op jit(solution)/shard_map/pallas_call | solution.py:421
  80.2 5.4 %collective-permute-start.9 = (f32[32,4,8,128]{3,2,1,0:T(8,128)S(1)}, f32[32,4,8,128]{3,2,1,0:T(8,128)S(1)}, u32[]{:S(2)}, u32[]{:S(2)}) collective-permute-start(f32[32,4,8,128]{3,2,1,0:T(8,128)S(1)} %get-tuple-element.44.own), channel_id=1, source_target_pairs={{0,399},{128,256},{256,128},{384,1},{1,384},{129,257},{257,129},{3... | collective-permute-start | bytes 1572872 | tf_op jit(solution)/shard_map/ppermute | solution.py:369
  85.6 1.9 %collective-permute-start.8 = (f32[32,4,8,128]{3,2,1,0:T(8,128)S(1)}, f32[32,4,8,128]{3,2,1,0:T(8,128)S(1)}, u32[]{:S(2)}, u32[]{:S(2)}) collective-permute-start(f32[32,4,8,128]{3,2,1,0:T(8,128)S(1)} %get-tuple-element.44.own), channel_id=1, source_target_pairs={{0,128},{128,0},{256,384},{384,256},{1,129},{129,1},{257,385},{385... | collective-permute-start | bytes 1572872 | tf_op jit(solution)/shard_map/ppermute | solution.py:370
  87.5 13.2 %all_to_all.15.got = f32[32,8,128]{2,1,0:T(8,128)S(1)} all-to-all(f32[32,8,128]{2,1,0:T(8,128)S(1)} %get-tuple-element.45), channel_id=1, replica_groups={{0,4,8,12,16,20,24,28,32,36,40,44,48,52,56,60,64,68,72,76,80,84,88,92,9..., dimensions={0} | all-to-all | bytes 262144 | tf_op jit(solution)/shard_map/all_to_all | solution.py:430
  100.7 0.0 collective-permute-done.9.second.y2
  100.7 0.0 collective-permute-done.8.first.y1
  100.7 0.1 shard_map.46
  100.7 0.1 collective-permute-start.10
  100.9 1.6 collective-permute-start.11
  102.5 1.9 %collective-permute-start.12 = (f32[8,128]{1,0:T(8,128)S(1)}, f32[8,128]{1,0:T(8,128)S(1)}, u32[]{:S(2)}, u32[]{:S(2)}) collective-permute-start(f32[8,128]{1,0:T(8,128)S(1)} %get-tuple-element.52.total), channel_id=1, source_target_pairs={{0,1},{1,0},{2,3},{3,2},{4,5},{5,4},{6,7},{7,6},{8,9},{9,8},{10,11... | collective-permute-start | bytes 12296 | tf_op jit(solution)/shard_map/ppermute | solution.py:385
  104.4 7.5 %collective-permute-done.12.other = f32[8,128]{1,0:T(8,128)S(1)} collective-permute-done((f32[8,128]{1,0:T(8,128)S(1)}, f32[8,128]{1,0:T(8,128)S(1)}, u32[]{:S(2)}, u32[]{:S(2)}) %collective-permute-start.12) | collective-permute-done | bytes 4128 | tf_op jit(solution)/shard_map/ppermute | solution.py:385
  111.9 0.0 collective-permute-done.10.xlow
  111.9 0.0 collective-permute-done.11.xhigh
  111.9 3.1 %shard_map.47 = (f32[32,4,8,128]{3,2,1,0:T(8,128)S(1)}, f32[40,4,8,128]{3,2,1,0:T(8,128)S(1)}, f32[140,8,128]{2,1,0:T(8,128)S(1)}, f32[140,8,128]{2,1,0:T(8,128)S(1)}, f32[8,128]{1,0:T(8,128)S(1)}) custom-call(s32[1]{0:T(128)} %bitcast.arm, f32[32,4,8,128]{3,2,1,0:T(8,128)S(1)} %get-tuple-element.44.own, f32[76,8,128]{2,1,0:T(8,128)S(1)} %collective-permute-done.10.xlow, ...), custom_call_target="tpu_custom_call" | custom-call | tf_op jit(solution)/shard_map/pallas_call | solution.py:440
  115.0 2.1 %collective-permute-start.13 = (f32[140,8,128]{2,1,0:T(8,128)S(1)}, f32[140,8,128]{2,1,0:T(8,128)S(1)}, u32[]{:S(2)}, u32[]{:S(2)}) collective-permute-start(f32[140,8,128]{2,1,0:T(8,128)S(1)} %get-tuple-element.54), channel_id=1, source_target_pairs={{0,128},{128,0},{256,384},{384,256},{1,129},{129,1},{257,385},{385... | collective-permute-start | bytes 1720328 | tf_op jit(solution)/shard_map/ppermute | solution.py:370
  117.1 4.7 %collective-permute-start.14 = (f32[140,8,128]{2,1,0:T(8,128)S(1)}, f32[140,8,128]{2,1,0:T(8,128)S(1)}, u32[]{:S(2)}, u32[]{:S(2)}) collective-permute-start(f32[140,8,128]{2,1,0:T(8,128)S(1)} %get-tuple-element.55), channel_id=1, source_target_pairs={{0,399},{128,256},{256,128},{384,1},{1,384},{129,257},{257,129},{3... | collective-permute-start | bytes 1720328 | tf_op jit(solution)/shard_map/ppermute | solution.py:369
  121.8 1.9 %collective-permute-start.15 = (f32[8,128]{1,0:T(8,128)S(1)}, f32[8,128]{1,0:T(8,128)S(1)}, u32[]{:S(2)}, u32[]{:S(2)}) collective-permute-start(f32[8,128]{1,0:T(8,128)S(1)} %get-tuple-element.59.total), channel_id=1, source_target_pairs={{0,2},{1,3},{2,0},{3,1},{4,6},{5,7},{6,4},{7,5},{8,10},{9,11},{10,... | collective-permute-start | bytes 12296 | tf_op jit(solution)/shard_map/ppermute | solution.py:385
  123.7 12.3 %collective-permute-done.15.other = f32[8,128]{1,0:T(8,128)S(1)} collective-permute-done((f32[8,128]{1,0:T(8,128)S(1)}, f32[8,128]{1,0:T(8,128)S(1)}, u32[]{:S(2)}, u32[]{:S(2)}) %collective-permute-start.15) | collective-permute-done | bytes 4128 | tf_op jit(solution)/shard_map/ppermute | solution.py:385
  136.0 0.0 collective-permute-done.13.y1
  136.0 0.0 collective-permute-done.14.y2
  136.0 0.0 copy-done.2
  136.0 3.5 %shard_map.48 = f32[4,520,128]{2,1,0:T(8,128)S(1)} custom-call(s32[1]{0:T(128)} %bitcast.arm, f32[4,4]{1,0:T(4,128)S(1)} %copy-done.2, f32[40,4,8,128]{3,2,1,0:T(8,128)S(1)} %get-tuple-element.53.wide, f32[140,8,128]{2,1,0:T(8,128)S(1)} %collective-permute-done.13.y1, f32[140,8,128]{2,1,0:T(8,128)S(1)} %collective-permute-done.14.y2, ...), custom_call_target="tpu_custom_call" | custom-call | tf_op jit(solution)/shard_map/pallas_call | solution.py:449
  139.5 0.0 copy-start.1
  139.5 26.5 %all_to_all.16.back = f32[4,520,128]{2,1,0:T(8,128)S(1)} all-to-all(f32[4,520,128]{2,1,0:T(8,128)S(1)} %shard_map.48), channel_id=1, replica_groups=mesh['arm'=4,'gx'=8,'gy'=16] {'arm'}, dimensions={0} | all-to-all | bytes 2129920 | tf_op jit(solution)/shard_map/all_to_all | solution.py:457
  166.0 2.0 %shard_map.49 = (f32[32,16,256]{2,1,0:T(8,128)}, f32[32,16,256]{2,1,0:T(8,128)}) custom-call(s32[1]{0:T(128)} %bitcast.arm, f32[4,4]{1,0:T(4,128)S(1)} %copy-done.2, f32[4,520,128]{2,1,0:T(8,128)S(1)} %all_to_all.16.back, f32[32,16,256]{2,1,0:T(8,128)S(1)} %bitcast.6), custom_call_target="tpu_custom_call" | custom-call | tf_op jit(solution)/shard_map/pallas_call | solution.py:459
  (3 shorter events, 0.0 us)
Async XLA Ops:
  0.6 1.0 copy-start
  2.6 20.4 %all-to-all-start = ((f32[4,256,128]{2,1,0:T(8,128)}), f32[4,256,128]{2,1,0:T(8,128)S(1)}, u32[]{:S(2)}, u32[]{:S(2)}) async-start(f32[4,256,128]{2,1,0:T(8,128)} %shard_map.41), calls=%async_computation | async-start | bytes 1048576 | tf_op jit(solution)/shard_map/all_to_all | solution.py:390
  23.2 29.6 %collective-permute-start.2 = (f32[32,3,8,128]{3,2,1,0:T(8,128)S(1)}, f32[32,3,8,128]{3,2,1,0:T(8,128)S(1)}, u32[]{:S(2)}, u32[]{:S(2)}) collective-permute-start(f32[32,3,8,128]{3,2,1,0:T(8,128)S(1)} %get-tuple-element.35), channel_id=1, source_target_pairs={{0,128},{128,0},{256,384},{384,256},{1,129},{129,1},{257,385},{385... | collective-permute-start | bytes 1179656 | tf_op jit(solution)/shard_map/ppermute | solution.py:370
  25.2 27.7 %collective-permute-start.3 = (f32[32,3,8,128]{3,2,1,0:T(8,128)S(1)}, f32[32,3,8,128]{3,2,1,0:T(8,128)S(1)}, u32[]{:S(2)}, u32[]{:S(2)}) collective-permute-start(f32[32,3,8,128]{3,2,1,0:T(8,128)S(1)} %get-tuple-element.36), channel_id=1, source_target_pairs={{0,399},{128,256},{256,128},{384,1},{1,384},{129,257},{257,129},{3... | collective-permute-start | bytes 1179656 | tf_op jit(solution)/shard_map/ppermute | solution.py:369
  36.4 4.2 %collective-permute-start = (f32[7,4,8,128]{3,2,1,0:T(8,128)S(1)}, f32[7,4,8,128]{3,2,1,0:T(8,128)S(1)}, u32[]{:S(2)}, u32[]{:S(2)}) collective-permute-start(f32[7,4,8,128]{3,2,1,0:T(8,128)S(1)} %get-tuple-element.33), channel_id=1, source_target_pairs={{0,16},{16,32},{32,48},{48,64},{64,80},{80,96},{96,112},{112,0},{1... | collective-permute-start | bytes 344072 | tf_op jit(solution)/shard_map/ppermute | solution.py:374
  36.4 4.2 %collective-permute-start.1 = (f32[7,4,8,128]{3,2,1,0:T(8,128)S(1)}, f32[7,4,8,128]{3,2,1,0:T(8,128)S(1)}, u32[]{:S(2)}, u32[]{:S(2)}) collective-permute-start(f32[7,4,8,128]{3,2,1,0:T(8,128)S(1)} %get-tuple-element.34), channel_id=1, source_target_pairs={{0,112},{16,0},{32,16},{48,32},{64,48},{80,64},{96,80},{112,96},{1... | collective-permute-start | bytes 344072 | tf_op jit(solution)/shard_map/ppermute | solution.py:375
  40.6 7.3 %collective-permute-start.4 = (f32[30,8,128]{2,1,0:T(8,128)S(1)}, f32[30,8,128]{2,1,0:T(8,128)S(1)}, u32[]{:S(2)}, u32[]{:S(2)}) collective-permute-start(f32[30,8,128]{2,1,0:T(8,128)S(1)} %get-tuple-element.37), channel_id=1, source_target_pairs={{0,128},{128,0},{256,384},{384,256},{1,129},{129,1},{257,385},{385... | collective-permute-start | bytes 368648 | tf_op jit(solution)/shard_map/ppermute | solution.py:370
  42.6 10.3 %collective-permute-start.5 = (f32[30,8,128]{2,1,0:T(8,128)S(1)}, f32[30,8,128]{2,1,0:T(8,128)S(1)}, u32[]{:S(2)}, u32[]{:S(2)}) collective-permute-start(f32[30,8,128]{2,1,0:T(8,128)S(1)} %get-tuple-element.38), channel_id=1, source_target_pairs={{0,399},{128,256},{256,128},{384,1},{1,384},{129,257},{257,129},{3... | collective-permute-start | bytes 368648 | tf_op jit(solution)/shard_map/ppermute | solution.py:369
  54.7 17.7 %collective-permute-start.6 = (f32[140,8,128]{2,1,0:T(8,128)S(1)}, f32[140,8,128]{2,1,0:T(8,128)S(1)}, u32[]{:S(2)}, u32[]{:S(2)}) collective-permute-start(f32[140,8,128]{2,1,0:T(8,128)S(1)} %get-tuple-element.40), channel_id=1, source_target_pairs={{0,128},{128,0},{256,384},{384,256},{1,129},{129,1},{257,385},{385... | collective-permute-start | bytes 1720328 | tf_op jit(solution)/shard_map/ppermute | solution.py:370
  56.7 21.0 %collective-permute-start.7 = (f32[140,8,128]{2,1,0:T(8,128)S(1)}, f32[140,8,128]{2,1,0:T(8,128)S(1)}, u32[]{:S(2)}, u32[]{:S(2)}) collective-permute-start(f32[140,8,128]{2,1,0:T(8,128)S(1)} %get-tuple-element.41), channel_id=1, source_target_pairs={{0,399},{128,256},{256,128},{384,1},{1,384},{129,257},{257,129},{3... | collective-permute-start | bytes 1720328 | tf_op jit(solution)/shard_map/ppermute | solution.py:369
  80.2 20.5 %collective-permute-start.9 = (f32[32,4,8,128]{3,2,1,0:T(8,128)S(1)}, f32[32,4,8,128]{3,2,1,0:T(8,128)S(1)}, u32[]{:S(2)}, u32[]{:S(2)}) collective-permute-start(f32[32,4,8,128]{3,2,1,0:T(8,128)S(1)} %get-tuple-element.44.own), channel_id=1, source_target_pairs={{0,399},{128,256},{256,128},{384,1},{1,384},{129,257},{257,129},{3... | collective-permute-start | bytes 1572872 | tf_op jit(solution)/shard_map/ppermute | solution.py:369
  85.6 15.1 %collective-permute-start.8 = (f32[32,4,8,128]{3,2,1,0:T(8,128)S(1)}, f32[32,4,8,128]{3,2,1,0:T(8,128)S(1)}, u32[]{:S(2)}, u32[]{:S(2)}) collective-permute-start(f32[32,4,8,128]{3,2,1,0:T(8,128)S(1)} %get-tuple-element.44.own), channel_id=1, source_target_pairs={{0,128},{128,0},{256,384},{384,256},{1,129},{129,1},{257,385},{385... | collective-permute-start | bytes 1572872 | tf_op jit(solution)/shard_map/ppermute | solution.py:370
  100.7 11.2 %collective-permute-start.10 = (f32[76,8,128]{2,1,0:T(8,128)S(1)}, f32[76,8,128]{2,1,0:T(8,128)S(1)}, u32[]{:S(2)}, u32[]{:S(2)}) collective-permute-start(f32[76,8,128]{2,1,0:T(8,128)S(1)} %get-tuple-element.46), channel_id=1, source_target_pairs={{0,16},{16,32},{32,48},{48,64},{64,80},{80,96},{96,112},{112,0},{1... | collective-permute-start | bytes 933896 | tf_op jit(solution)/shard_map/ppermute | solution.py:374
  100.9 11.0 %collective-permute-start.11 = (f32[76,8,128]{2,1,0:T(8,128)S(1)}, f32[76,8,128]{2,1,0:T(8,128)S(1)}, u32[]{:S(2)}, u32[]{:S(2)}) collective-permute-start(f32[76,8,128]{2,1,0:T(8,128)S(1)} %get-tuple-element.47), channel_id=1, source_target_pairs={{0,112},{16,0},{32,16},{48,32},{64,48},{80,64},{96,80},{112,96},{1... | collective-permute-start | bytes 933896 | tf_op jit(solution)/shard_map/ppermute | solution.py:375
  102.5 9.4 %collective-permute-start.12 = (f32[8,128]{1,0:T(8,128)S(1)}, f32[8,128]{1,0:T(8,128)S(1)}, u32[]{:S(2)}, u32[]{:S(2)}) collective-permute-start(f32[8,128]{1,0:T(8,128)S(1)} %get-tuple-element.52.total), channel_id=1, source_target_pairs={{0,1},{1,0},{2,3},{3,2},{4,5},{5,4},{6,7},{7,6},{8,9},{9,8},{10,11... | collective-permute-start | bytes 12296 | tf_op jit(solution)/shard_map/ppermute | solution.py:385
  111.9 24.1 %copy-start.2 = (f32[4,4]{1,0:T(4,128)S(1)}, f32[4,4]{1,0:T(4,128)}, u32[]{:S(2)}) copy-start(f32[4,4]{1,0:T(4,128)} %chi.3) | copy-start | bytes 196
  115.0 21.0 %collective-permute-start.13 = (f32[140,8,128]{2,1,0:T(8,128)S(1)}, f32[140,8,128]{2,1,0:T(8,128)S(1)}, u32[]{:S(2)}, u32[]{:S(2)}) collective-permute-start(f32[140,8,128]{2,1,0:T(8,128)S(1)} %get-tuple-element.54), channel_id=1, source_target_pairs={{0,128},{128,0},{256,384},{384,256},{1,129},{129,1},{257,385},{385... | collective-permute-start | bytes 1720328 | tf_op jit(solution)/shard_map/ppermute | solution.py:370
  117.1 19.0 %collective-permute-start.14 = (f32[140,8,128]{2,1,0:T(8,128)S(1)}, f32[140,8,128]{2,1,0:T(8,128)S(1)}, u32[]{:S(2)}, u32[]{:S(2)}) collective-permute-start(f32[140,8,128]{2,1,0:T(8,128)S(1)} %get-tuple-element.55), channel_id=1, source_target_pairs={{0,399},{128,256},{256,128},{384,1},{1,384},{129,257},{257,129},{3... | collective-permute-start | bytes 1720328 | tf_op jit(solution)/shard_map/ppermute | solution.py:369
  121.8 14.2 %collective-permute-start.15 = (f32[8,128]{1,0:T(8,128)S(1)}, f32[8,128]{1,0:T(8,128)S(1)}, u32[]{:S(2)}, u32[]{:S(2)}) collective-permute-start(f32[8,128]{1,0:T(8,128)S(1)} %get-tuple-element.59.total), channel_id=1, source_target_pairs={{0,2},{1,3},{2,0},{3,1},{4,6},{5,7},{6,4},{7,5},{8,10},{9,11},{10,... | collective-permute-start | bytes 12296 | tf_op jit(solution)/shard_map/ppermute | solution.py:385
  139.5 26.5 %copy-start.1 = (f32[1,32,16,256]{3,2,1,0:T(8,128)S(1)}, f32[1,32,16,256]{3,2,1,0:T(8,128)}, u32[]{:S(2)}) copy-start(f32[1,32,16,256]{3,2,1,0:T(8,128)} %param.2) | copy-start | bytes 1572868

commit v7 on v6

--- a/solution.py
+++ b/solution.py
@@ -256,10 +256,10 @@
 
 
 def outer_first(
-    arm, own, xlow, xhigh, y1, y2, coef, s4, s5, s6, s7, s8, total, other,
-    dens, wide, e1, e2, both, a, b
+    arm, own, xlow, xhigh, y1, y2, coef, s4, s5, s6, s7, s8, total,
+    dens, wide, e1, e2, kept, a, b
 ):
-    both[...] = total[...] + other[...]
+    kept[...] = total[...]
     surround(arm, a, JUNC_REACH, own, y1, y2, xlow, xhigh, (8, 4))
     here = (slice(8, 8 + BX), slice(4, 8))
     shift = (-1, -1)
@@ -442,9 +442,10 @@
         (own, wide_shape, mid, mid, tiles()),
         [scratch(16 + BX, 8 + BY)] * 2,
         scalars=1,
-        arrays=13,
-    )(arm, junction, xlow, xhigh, y1, y2, coef, s4, s5, s6, s7, s8, total, other)
+        arrays=12,
+    )(arm, junction, xlow, xhigh, y1, y2, coef, s4, s5, s6, s7, s8, total)
     y1, y2 = along_y(e1, e2)
+    total = total + other
     other = along_z(total, 2)
     out = call(
         outer_second,

time: 169 us -> 180 us (1.065)
  blocking collectives: 39.7 us -> 43.9 us
  waiting for transfers between devices: 56.7 us -> 60.3 us
  starting transfers between devices: 55.7 us -> 58.4 us
    ppermute x2, waiting for transfers between devices: 2.47 us -> 7.05 us  [along_x(): low = lax.ppermute(right, 'gx', [(i, (i + 1) % m) for i in range(m)])]
    ppermute x2, starting transfers between devices: 3.83 us -> 6.55 us  [along_z(): return lax.ppermute(tile, 'gy', [(i, i ^ bit) for i in range(size_gy)])]
    all_to_all x1, blocking collectives: 26.5 us -> 28.8 us  [local(): back = lax.all_to_all(out, 'arm', 0, 0)]
    all_to_all x1, blocking collectives: 13.2 us -> 15.1 us  [local(): lax.all_to_all(spread, ('gx', 'gy'), 0, 0, axis_index_groups=xy_groups)]
  transfers between devices with their start and end apart: 17 -> 17, of which waited for: 7 -> 8; matrix products, arithmetic and copies ran while one was open for 0% -> 0% of each run, Pallas kernels for 0% -> 0%
where the time goes in v7:
time: 180 us; the launch traced here: 179 us
  waiting for transfers between devices  60.3 us (34%)
  starting transfers between devices  58.4 us (32%)
  blocking collectives  43.9 us (24%)
  Pallas kernels  14.8 us (8%)
    ppermute x5, starting transfers between devices, along_y(): second = lax.ppermute(second, ('arm', 'gy'), second_pairs)  32.8 us
    all_to_all x1, blocking collectives, local(): back = lax.all_to_all(out, 'arm', 0, 0)  28.8 us
    ppermute x2, waiting for transfers between devices, along_z(): return lax.ppermute(tile, 'gy', [(i, i ^ bit) for i in range(size_gy)])  18.7 us
    all_to_all x1, blocking collectives, local(): lax.all_to_all(spread, ('gx', 'gy'), 0, 0, axis_index_groups=xy_groups)  15.1 us
    all_to_all x1, waiting for transfers between devices, local(): recv = lax.all_to_all(payload, 'arm', 0, 0)  14.5 us
    ppermute x5, waiting for transfers between devices, along_y(): second = lax.ppermute(second, ('arm', 'gy'), second_pairs)  10.1 us
    ppermute x5, waiting for transfers between devices, along_y(): return (lax.ppermute(first, ('arm', 'gy'), first_pairs), second)  9.83 us
    ppermute x5, starting transfers between devices, along_y(): return (lax.ppermute(first, ('arm', 'gy'), first_pairs), second)  9.6 us
  transfers between devices with their start and end apart: 17, of which 8 were waited for; matrix products, arithmetic and copies ran while one was open for 0% of the time, Pallas kernels for 0%

profile of v7, /device:TPU:6, one launch (start us, length us, event | category | flops | bytes accessed | tf_op | source)
XLA Modules:
  0.0 179.2 jit_solution(16743300004378398553)
XLA Ops:
  0.6 0.0 copy-start
  0.6 1.0 copy-done
  1.7 0.9 shard_map.41
  2.6 5.9 %all-to-all-start = ((f32[4,256,128]{2,1,0:T(8,128)}), f32[4,256,128]{2,1,0:T(8,128)S(1)}, u32[]{:S(2)}, u32[]{:S(2)}) async-start(f32[4,256,128]{2,1,0:T(8,128)} %shard_map.41), calls=%async_computation | async-start | bytes 1048576 | tf_op jit(solution)/shard_map/all_to_all | solution.py:390
  8.5 14.5 %all-to-all-done.recv = f32[4,256,128]{2,1,0:T(8,128)S(1)} async-done(((f32[4,256,128]{2,1,0:T(8,128)}), f32[4,256,128]{2,1,0:T(8,128)S(1)}, u32[]{:S(2)}, u32[]{:S(2)}) %all-to-all-start) | async-done | bytes 524320 | tf_op jit(solution)/shard_map/all_to_all | solution.py:390
  22.9 0.3 shard_map.42
  23.2 1.9 %collective-permute-start.2 = (f32[32,3,8,128]{3,2,1,0:T(8,128)S(1)}, f32[32,3,8,128]{3,2,1,0:T(8,128)S(1)}, u32[]{:S(2)}, u32[]{:S(2)}) collective-permute-start(f32[32,3,8,128]{3,2,1,0:T(8,128)S(1)} %get-tuple-element.35), channel_id=1, source_target_pairs={{0,128},{128,0},{256,384},{384,256},{1,129},{129,1},{257,385},{385... | collective-permute-start | bytes 1179656 | tf_op jit(solution)/shard_map/ppermute | solution.py:370
  25.2 11.2 %collective-permute-start.3 = (f32[32,3,8,128]{3,2,1,0:T(8,128)S(1)}, f32[32,3,8,128]{3,2,1,0:T(8,128)S(1)}, u32[]{:S(2)}, u32[]{:S(2)}) collective-permute-start(f32[32,3,8,128]{3,2,1,0:T(8,128)S(1)} %get-tuple-element.36), channel_id=1, source_target_pairs={{0,399},{128,256},{256,128},{384,1},{1,384},{129,257},{257,129},{3... | collective-permute-start | bytes 1179656 | tf_op jit(solution)/shard_map/ppermute | solution.py:369
  36.4 0.0 collective-permute-start
  36.4 1.7 collective-permute-start.1
  38.1 2.5 %collective-permute-done.low.xlow = f32[7,4,8,128]{3,2,1,0:T(8,128)S(1)} collective-permute-done((f32[7,4,8,128]{3,2,1,0:T(8,128)S(1)}, f32[7,4,8,128]{3,2,1,0:T(8,128)S(1)}, u32[]{:S(2)}, u32[]{:S(2)}) %collective-permute-start) | collective-permute-done | bytes 114720 | tf_op jit(solution)/shard_map/ppermute | solution.py:374
  40.6 0.0 collective-permute-done.1.high.xhigh
  40.6 1.9 %collective-permute-start.4 = (f32[30,8,128]{2,1,0:T(8,128)S(1)}, f32[30,8,128]{2,1,0:T(8,128)S(1)}, u32[]{:S(2)}, u32[]{:S(2)}) collective-permute-start(f32[30,8,128]{2,1,0:T(8,128)S(1)} %get-tuple-element.37), channel_id=1, source_target_pairs={{0,128},{128,0},{256,384},{384,256},{1,129},{129,1},{257,385},{385... | collective-permute-start | bytes 368648 | tf_op jit(solution)/shard_map/ppermute | solution.py:370
  42.6 5.4 %collective-permute-start.5 = (f32[30,8,128]{2,1,0:T(8,128)S(1)}, f32[30,8,128]{2,1,0:T(8,128)S(1)}, u32[]{:S(2)}, u32[]{:S(2)}) collective-permute-start(f32[30,8,128]{2,1,0:T(8,128)S(1)} %get-tuple-element.38), channel_id=1, source_target_pairs={{0,399},{128,256},{256,128},{384,1},{1,384},{129,257},{257,129},{3... | collective-permute-start | bytes 368648 | tf_op jit(solution)/shard_map/ppermute | solution.py:369
  48.0 0.0 collective-permute-done.4.c1
  48.0 4.9 %collective-permute-done.5.c2 = f32[30,8,128]{2,1,0:T(8,128)S(1)} collective-permute-done((f32[30,8,128]{2,1,0:T(8,128)S(1)}, f32[30,8,128]{2,1,0:T(8,128)S(1)}, u32[]{:S(2)}, u32[]{:S(2)}) %collective-permute-start.5) | collective-permute-done | bytes 122912 | tf_op jit(solution)/shard_map/ppermute | solution.py:369
  52.8 0.0 collective-permute-done.2.y1
  52.8 0.0 collective-permute-done.3.y2
  52.9 2.0 %shard_map.44 = (f32[46,10,8,128]{3,2,1,0:T(8,128)S(1)}, f32[32,4,8,128]{3,2,1,0:T(8,128)S(1)}, f32[32,4,8,128]{3,2,1,0:T(8,128)S(1)}, f32[40,4,8,128]{3,2,1,0:T...) custom-call(s32[1]{0:T(128)} %bitcast.arm, f32[32,4,8,128]{3,2,1,0:T(8,128)S(1)} %bitcast.7, ...), custom_call_target="tpu_custom_call" | custom-call | tf_op jit(solution)/shard_map/pallas_call | solution.py:413
  54.8 1.9 %collective-permute-start.6 = (f32[140,8,128]{2,1,0:T(8,128)S(1)}, f32[140,8,128]{2,1,0:T(8,128)S(1)}, u32[]{:S(2)}, u32[]{:S(2)}) collective-permute-start(f32[140,8,128]{2,1,0:T(8,128)S(1)} %get-tuple-element.40), channel_id=1, source_target_pairs={{0,128},{128,0},{256,384},{384,256},{1,129},{129,1},{257,385},{385... | collective-permute-start | bytes 1720328 | tf_op jit(solution)/shard_map/ppermute | solution.py:370
  56.7 6.0 %collective-permute-start.7 = (f32[140,8,128]{2,1,0:T(8,128)S(1)}, f32[140,8,128]{2,1,0:T(8,128)S(1)}, u32[]{:S(2)}, u32[]{:S(2)}) collective-permute-start(f32[140,8,128]{2,1,0:T(8,128)S(1)} %get-tuple-element.41), channel_id=1, source_target_pairs={{0,399},{128,256},{256,128},{384,1},{1,384},{129,257},{257,129},{3... | collective-permute-start | bytes 1720328 | tf_op jit(solution)/shard_map/ppermute | solution.py:369
  62.7 9.8 %collective-permute-done.6.y1 = f32[140,8,128]{2,1,0:T(8,128)S(1)} collective-permute-done((f32[140,8,128]{2,1,0:T(8,128)S(1)}, f32[140,8,128]{2,1,0:T(8,128)S(1)}, u32[]{:S(2)}, u32[]{:S(2)}) %collective-permute-start.6) | collective-permute-done | bytes 573472 | tf_op jit(solution)/shard_map/ppermute | solution.py:370
  72.5 5.2 %collective-permute-done.7.y2 = f32[140,8,128]{2,1,0:T(8,128)S(1)} collective-permute-done((f32[140,8,128]{2,1,0:T(8,128)S(1)}, f32[140,8,128]{2,1,0:T(8,128)S(1)}, u32[]{:S(2)}, u32[]{:S(2)}) %collective-permute-start.7) | collective-permute-done | bytes 573472 | tf_op jit(solution)/shard_map/ppermute | solution.py:369
  77.8 2.6 %shard_map.45 = (f32[32,4,8,128]{3,2,1,0:T(8,128)S(1)}, f32[32,4,8,128]{3,2,1,0:T(8,128)S(1)}, f32[32,4,8,128]{3,2,1,0:T(8,128)S(1)}, f32[32,4,8,128]{3,2,1,0:T(...) custom-call(s32[1]{0:T(128)} %bitcast.arm, f32[40,4,8,128]{3,2,1,0:T(8,128)S(1)} %get-tuple-element.39.wide.s4, ...), custom_call_target="tpu_custom_call" | custom-call | tf_op jit(solution)/shard_map/pallas_call | solution.py:421
  80.4 1.9 %collective-permute-start.8 = (f32[32,4,8,128]{3,2,1,0:T(8,128)S(1)}, f32[32,4,8,128]{3,2,1,0:T(8,128)S(1)}, u32[]{:S(2)}, u32[]{:S(2)}) collective-permute-start(f32[32,4,8,128]{3,2,1,0:T(8,128)S(1)} %get-tuple-element.44.own), channel_id=1, source_target_pairs={{0,128},{128,0},{256,384},{384,256},{1,129},{129,1},{257,385},{385... | collective-permute-start | bytes 1572872 | tf_op jit(solution)/shard_map/ppermute | solution.py:370
  82.3 5.4 %collective-permute-start.9 = (f32[32,4,8,128]{3,2,1,0:T(8,128)S(1)}, f32[32,4,8,128]{3,2,1,0:T(8,128)S(1)}, u32[]{:S(2)}, u32[]{:S(2)}) collective-permute-start(f32[32,4,8,128]{3,2,1,0:T(8,128)S(1)} %get-tuple-element.44.own), channel_id=1, source_target_pairs={{0,399},{128,256},{256,128},{384,1},{1,384},{129,257},{257,129},{3... | collective-permute-start | bytes 1572872 | tf_op jit(solution)/shard_map/ppermute | solution.py:369
  87.7 15.1 %all_to_all.15.got = f32[32,8,128]{2,1,0:T(8,128)S(1)} all-to-all(f32[32,8,128]{2,1,0:T(8,128)S(1)} %get-tuple-element.45), channel_id=1, replica_groups={{0,4,8,12,16,20,24,28,32,36,40,44,48,52,56,60,64,68,72,76,80,84,88,92,9..., dimensions={0} | all-to-all | bytes 262144 | tf_op jit(solution)/shard_map/all_to_all | solution.py:430
  102.8 0.0 collective-permute-done.8.first.y1
  102.8 0.0 collective-permute-done.9.second.y2
  102.8 0.1 shard_map.46
  102.9 0.1 collective-permute-start.10
  103.0 1.6 collective-permute-start.11
  104.6 4.6 %collective-permute-done.10.xlow = f32[76,8,128]{2,1,0:T(8,128)S(1)} collective-permute-done((f32[76,8,128]{2,1,0:T(8,128)S(1)}, f32[76,8,128]{2,1,0:T(8,128)S(1)}, u32[]{:S(2)}, u32[]{:S(2)}) %collective-permute-start.10) | collective-permute-done | bytes 311328 | tf_op jit(solution)/shard_map/ppermute | solution.py:374
  109.2 0.0 collective-permute-done.11.xhigh
  109.2 3.3 %shard_map.47 = (f32[32,4,8,128]{3,2,1,0:T(8,128)S(1)}, f32[40,4,8,128]{3,2,1,0:T(8,128)S(1)}, f32[140,8,128]{2,1,0:T(8,128)S(1)}, f32[140,8,128]{2,1,0:T(8,128)S(1)}, f32[8,128]{1,0:T(8,128)S(1)}) custom-call(s32[1]{0:T(128)} %bitcast.arm, f32[32,4,8,128]{3,2,1,0:T(8,128)S(1)} %get-tuple-element.44.own, f32[76,8,128]{2,1,0:T(8,128)S(1)} %collective-permute-done.10.xlow, ...), custom_call_target="tpu_custom_call" | custom-call | tf_op jit(solution)/shard_map/pallas_call | solution.py:440
  112.5 1.9 %collective-permute-start.12 = (f32[140,8,128]{2,1,0:T(8,128)S(1)}, f32[140,8,128]{2,1,0:T(8,128)S(1)}, u32[]{:S(2)}, u32[]{:S(2)}) collective-permute-start(f32[140,8,128]{2,1,0:T(8,128)S(1)} %get-tuple-element.54), channel_id=1, source_target_pairs={{0,128},{128,0},{256,384},{384,256},{1,129},{129,1},{257,385},{385... | collective-permute-start | bytes 1720328 | tf_op jit(solution)/shard_map/ppermute | solution.py:370
  114.4 4.9 %collective-permute-start.13 = (f32[140,8,128]{2,1,0:T(8,128)S(1)}, f32[140,8,128]{2,1,0:T(8,128)S(1)}, u32[]{:S(2)}, u32[]{:S(2)}) collective-permute-start(f32[140,8,128]{2,1,0:T(8,128)S(1)} %get-tuple-element.55), channel_id=1, source_target_pairs={{0,399},{128,256},{256,128},{384,1},{1,384},{129,257},{257,129},{3... | collective-permute-start | bytes 1720328 | tf_op jit(solution)/shard_map/ppermute | solution.py:369
  119.3 1.9 %collective-permute-start.14 = (f32[8,128]{1,0:T(8,128)S(1)}, f32[8,128]{1,0:T(8,128)S(1)}, u32[]{:S(2)}, u32[]{:S(2)}) collective-permute-start(f32[8,128]{1,0:T(8,128)S(1)} %get-tuple-element.52.total), channel_id=1, source_target_pairs={{0,1},{1,0},{2,3},{3,2},{4,5},{5,4},{6,7},{7,6},{8,9},{9,8},{10,11... | collective-permute-start | bytes 12296 | tf_op jit(solution)/shard_map/ppermute | solution.py:385
  121.3 9.2 %collective-permute-done.14 = f32[8,128]{1,0:T(8,128)S(1)} collective-permute-done((f32[8,128]{1,0:T(8,128)S(1)}, f32[8,128]{1,0:T(8,128)S(1)}, u32[]{:S(2)}, u32[]{:S(2)}) %collective-permute-start.14) | collective-permute-done | bytes 4128 | tf_op jit(solution)/shard_map/ppermute | solution.py:385
  130.4 4.6 %collective-permute-start.15 = (f32[8,128]{1,0:T(8,128)S(1)}, f32[8,128]{1,0:T(8,128)S(1)}, u32[]{:S(2)}, u32[]{:S(2)}) collective-permute-start(f32[8,128]{1,0:T(8,128)S(1)} %add.3.total), channel_id=1, source_target_pairs={{0,2},{1,3},{2,0},{3,1},{4,6},{5,7},{6,4},{7,5},{8,10},{9,11},{10,... | collective-permute-start | bytes 12296 | tf_op jit(solution)/shard_map/ppermute | solution.py:385
  135.1 9.6 %collective-permute-done.15.other = f32[8,128]{1,0:T(8,128)S(1)} collective-permute-done((f32[8,128]{1,0:T(8,128)S(1)}, f32[8,128]{1,0:T(8,128)S(1)}, u32[]{:S(2)}, u32[]{:S(2)}) %collective-permute-start.15) | collective-permute-done | bytes 4128 | tf_op jit(solution)/shard_map/ppermute | solution.py:385
  144.6 0.0 collective-permute-done.12.y1
  144.6 0.0 collective-permute-done.13.y2
  144.6 0.0 copy-done.2
  144.6 3.7 %shard_map.48 = f32[4,520,128]{2,1,0:T(8,128)S(1)} custom-call(s32[1]{0:T(128)} %bitcast.arm, f32[4,4]{1,0:T(4,128)S(1)} %copy-done.2, f32[40,4,8,128]{3,2,1,0:T(8,128)S(1)} %get-tuple-element.53.wide, f32[140,8,128]{2,1,0:T(8,128)S(1)} %collective-permute-done.12.y1, f32[140,8,128]{2,1,0:T(8,128)S(1)} %collective-permute-done.13.y2, ...), custom_call_target="tpu_custom_call" | custom-call | tf_op jit(solution)/shard_map/pallas_call | solution.py:450
  148.4 0.0 copy-start.1
  148.4 28.8 %all_to_all.16.back = f32[4,520,128]{2,1,0:T(8,128)S(1)} all-to-all(f32[4,520,128]{2,1,0:T(8,128)S(1)} %shard_map.48), channel_id=1, replica_groups=mesh['arm'=4,'gx'=8,'gy'=16] {'arm'}, dimensions={0} | all-to-all | bytes 2129920 | tf_op jit(solution)/shard_map/all_to_all | solution.py:458
  177.2 2.0 %shard_map.49 = (f32[32,16,256]{2,1,0:T(8,128)}, f32[32,16,256]{2,1,0:T(8,128)}) custom-call(s32[1]{0:T(128)} %bitcast.arm, f32[4,4]{1,0:T(4,128)S(1)} %copy-done.2, f32[4,520,128]{2,1,0:T(8,128)S(1)} %all_to_all.16.back, f32[32,16,256]{2,1,0:T(8,128)S(1)} %bitcast.6), custom_call_target="tpu_custom_call" | custom-call | tf_op jit(solution)/shard_map/pallas_call | solution.py:460
  (4 shorter events, 0.0 us)
Async XLA Ops:
  0.6 1.0 copy-start
  2.6 20.4 %all-to-all-start = ((f32[4,256,128]{2,1,0:T(8,128)}), f32[4,256,128]{2,1,0:T(8,128)S(1)}, u32[]{:S(2)}, u32[]{:S(2)}) async-start(f32[4,256,128]{2,1,0:T(8,128)} %shard_map.41), calls=%async_computation | async-start | bytes 1048576 | tf_op jit(solution)/shard_map/all_to_all | solution.py:390
  23.2 29.6 %collective-permute-start.2 = (f32[32,3,8,128]{3,2,1,0:T(8,128)S(1)}, f32[32,3,8,128]{3,2,1,0:T(8,128)S(1)}, u32[]{:S(2)}, u32[]{:S(2)}) collective-permute-start(f32[32,3,8,128]{3,2,1,0:T(8,128)S(1)} %get-tuple-element.35), channel_id=1, source_target_pairs={{0,128},{128,0},{256,384},{384,256},{1,129},{129,1},{257,385},{385... | collective-permute-start | bytes 1179656 | tf_op jit(solution)/shard_map/ppermute | solution.py:370
  25.2 27.7 %collective-permute-start.3 = (f32[32,3,8,128]{3,2,1,0:T(8,128)S(1)}, f32[32,3,8,128]{3,2,1,0:T(8,128)S(1)}, u32[]{:S(2)}, u32[]{:S(2)}) collective-permute-start(f32[32,3,8,128]{3,2,1,0:T(8,128)S(1)} %get-tuple-element.36), channel_id=1, source_target_pairs={{0,399},{128,256},{256,128},{384,1},{1,384},{129,257},{257,129},{3... | collective-permute-start | bytes 1179656 | tf_op jit(solution)/shard_map/ppermute | solution.py:369
  36.4 4.2 %collective-permute-start = (f32[7,4,8,128]{3,2,1,0:T(8,128)S(1)}, f32[7,4,8,128]{3,2,1,0:T(8,128)S(1)}, u32[]{:S(2)}, u32[]{:S(2)}) collective-permute-start(f32[7,4,8,128]{3,2,1,0:T(8,128)S(1)} %get-tuple-element.33), channel_id=1, source_target_pairs={{0,16},{16,32},{32,48},{48,64},{64,80},{80,96},{96,112},{112,0},{1... | collective-permute-start | bytes 344072 | tf_op jit(solution)/shard_map/ppermute | solution.py:374
  36.4 4.2 %collective-permute-start.1 = (f32[7,4,8,128]{3,2,1,0:T(8,128)S(1)}, f32[7,4,8,128]{3,2,1,0:T(8,128)S(1)}, u32[]{:S(2)}, u32[]{:S(2)}) collective-permute-start(f32[7,4,8,128]{3,2,1,0:T(8,128)S(1)} %get-tuple-element.34), channel_id=1, source_target_pairs={{0,112},{16,0},{32,16},{48,32},{64,48},{80,64},{96,80},{112,96},{1... | collective-permute-start | bytes 344072 | tf_op jit(solution)/shard_map/ppermute | solution.py:375
  40.6 7.3 %collective-permute-start.4 = (f32[30,8,128]{2,1,0:T(8,128)S(1)}, f32[30,8,128]{2,1,0:T(8,128)S(1)}, u32[]{:S(2)}, u32[]{:S(2)}) collective-permute-start(f32[30,8,128]{2,1,0:T(8,128)S(1)} %get-tuple-element.37), channel_id=1, source_target_pairs={{0,128},{128,0},{256,384},{384,256},{1,129},{129,1},{257,385},{385... | collective-permute-start | bytes 368648 | tf_op jit(solution)/shard_map/ppermute | solution.py:370
  42.6 10.3 %collective-permute-start.5 = (f32[30,8,128]{2,1,0:T(8,128)S(1)}, f32[30,8,128]{2,1,0:T(8,128)S(1)}, u32[]{:S(2)}, u32[]{:S(2)}) collective-permute-start(f32[30,8,128]{2,1,0:T(8,128)S(1)} %get-tuple-element.38), channel_id=1, source_target_pairs={{0,399},{128,256},{256,128},{384,1},{1,384},{129,257},{257,129},{3... | collective-permute-start | bytes 368648 | tf_op jit(solution)/shard_map/ppermute | solution.py:369
  54.8 17.7 %collective-permute-start.6 = (f32[140,8,128]{2,1,0:T(8,128)S(1)}, f32[140,8,128]{2,1,0:T(8,128)S(1)}, u32[]{:S(2)}, u32[]{:S(2)}) collective-permute-start(f32[140,8,128]{2,1,0:T(8,128)S(1)} %get-tuple-element.40), channel_id=1, source_target_pairs={{0,128},{128,0},{256,384},{384,256},{1,129},{129,1},{257,385},{385... | collective-permute-start | bytes 1720328 | tf_op jit(solution)/shard_map/ppermute | solution.py:370
  56.7 21.0 %collective-permute-start.7 = (f32[140,8,128]{2,1,0:T(8,128)S(1)}, f32[140,8,128]{2,1,0:T(8,128)S(1)}, u32[]{:S(2)}, u32[]{:S(2)}) collective-permute-start(f32[140,8,128]{2,1,0:T(8,128)S(1)} %get-tuple-element.41), channel_id=1, source_target_pairs={{0,399},{128,256},{256,128},{384,1},{1,384},{129,257},{257,129},{3... | collective-permute-start | bytes 1720328 | tf_op jit(solution)/shard_map/ppermute | solution.py:369
  80.4 22.4 %collective-permute-start.8 = (f32[32,4,8,128]{3,2,1,0:T(8,128)S(1)}, f32[32,4,8,128]{3,2,1,0:T(8,128)S(1)}, u32[]{:S(2)}, u32[]{:S(2)}) collective-permute-start(f32[32,4,8,128]{3,2,1,0:T(8,128)S(1)} %get-tuple-element.44.own), channel_id=1, source_target_pairs={{0,128},{128,0},{256,384},{384,256},{1,129},{129,1},{257,385},{385... | collective-permute-start | bytes 1572872 | tf_op jit(solution)/shard_map/ppermute | solution.py:370
  82.3 20.5 %collective-permute-start.9 = (f32[32,4,8,128]{3,2,1,0:T(8,128)S(1)}, f32[32,4,8,128]{3,2,1,0:T(8,128)S(1)}, u32[]{:S(2)}, u32[]{:S(2)}) collective-permute-start(f32[32,4,8,128]{3,2,1,0:T(8,128)S(1)} %get-tuple-element.44.own), channel_id=1, source_target_pairs={{0,399},{128,256},{256,128},{384,1},{1,384},{129,257},{257,129},{3... | collective-permute-start | bytes 1572872 | tf_op jit(solution)/shard_map/ppermute | solution.py:369
  102.9 6.3 %collective-permute-start.10 = (f32[76,8,128]{2,1,0:T(8,128)S(1)}, f32[76,8,128]{2,1,0:T(8,128)S(1)}, u32[]{:S(2)}, u32[]{:S(2)}) collective-permute-start(f32[76,8,128]{2,1,0:T(8,128)S(1)} %get-tuple-element.46), channel_id=1, source_target_pairs={{0,16},{16,32},{32,48},{48,64},{64,80},{80,96},{96,112},{112,0},{1... | collective-permute-start | bytes 933896 | tf_op jit(solution)/shard_map/ppermute | solution.py:374
  103.0 6.2 %collective-permute-start.11 = (f32[76,8,128]{2,1,0:T(8,128)S(1)}, f32[76,8,128]{2,1,0:T(8,128)S(1)}, u32[]{:S(2)}, u32[]{:S(2)}) collective-permute-start(f32[76,8,128]{2,1,0:T(8,128)S(1)} %get-tuple-element.47), channel_id=1, source_target_pairs={{0,112},{16,0},{32,16},{48,32},{64,48},{80,64},{96,80},{112,96},{1... | collective-permute-start | bytes 933896 | tf_op jit(solution)/shard_map/ppermute | solution.py:375
  109.2 35.4 %copy-start.2 = (f32[4,4]{1,0:T(4,128)S(1)}, f32[4,4]{1,0:T(4,128)}, u32[]{:S(2)}) copy-start(f32[4,4]{1,0:T(4,128)} %chi.3) | copy-start | bytes 196
  112.5 32.1 %collective-permute-start.12 = (f32[140,8,128]{2,1,0:T(8,128)S(1)}, f32[140,8,128]{2,1,0:T(8,128)S(1)}, u32[]{:S(2)}, u32[]{:S(2)}) collective-permute-start(f32[140,8,128]{2,1,0:T(8,128)S(1)} %get-tuple-element.54), channel_id=1, source_target_pairs={{0,128},{128,0},{256,384},{384,256},{1,129},{129,1},{257,385},{385... | collective-permute-start | bytes 1720328 | tf_op jit(solution)/shard_map/ppermute | solution.py:370
  114.4 30.2 %collective-permute-start.13 = (f32[140,8,128]{2,1,0:T(8,128)S(1)}, f32[140,8,128]{2,1,0:T(8,128)S(1)}, u32[]{:S(2)}, u32[]{:S(2)}) collective-permute-start(f32[140,8,128]{2,1,0:T(8,128)S(1)} %get-tuple-element.55), channel_id=1, source_target_pairs={{0,399},{128,256},{256,128},{384,1},{1,384},{129,257},{257,129},{3... | collective-permute-start | bytes 1720328 | tf_op jit(solution)/shard_map/ppermute | solution.py:369
  119.3 11.1 %collective-permute-start.14 = (f32[8,128]{1,0:T(8,128)S(1)}, f32[8,128]{1,0:T(8,128)S(1)}, u32[]{:S(2)}, u32[]{:S(2)}) collective-permute-start(f32[8,128]{1,0:T(8,128)S(1)} %get-tuple-element.52.total), channel_id=1, source_target_pairs={{0,1},{1,0},{2,3},{3,2},{4,5},{5,4},{6,7},{7,6},{8,9},{9,8},{10,11... | collective-permute-start | bytes 12296 | tf_op jit(solution)/shard_map/ppermute | solution.py:385
  130.4 14.2 %collective-permute-start.15 = (f32[8,128]{1,0:T(8,128)S(1)}, f32[8,128]{1,0:T(8,128)S(1)}, u32[]{:S(2)}, u32[]{:S(2)}) collective-permute-start(f32[8,128]{1,0:T(8,128)S(1)} %add.3.total), channel_id=1, source_target_pairs={{0,2},{1,3},{2,0},{3,1},{4,6},{5,7},{6,4},{7,5},{8,10},{9,11},{10,... | collective-permute-start | bytes 12296 | tf_op jit(solution)/shard_map/ppermute | solution.py:385
  148.4 28.8 %copy-start.1 = (f32[1,32,16,256]{3,2,1,0:T(8,128)S(1)}, f32[1,32,16,256]{3,2,1,0:T(8,128)}, u32[]{:S(2)}) copy-start(f32[1,32,16,256]{3,2,1,0:T(8,128)} %param.2) | copy-start | bytes 1572868

commit v8 on v7

--- a/solution.py
+++ b/solution.py
@@ -42,19 +42,46 @@
     return lane == LANES - 1, lane == 0
 
 
+def lane_matrix():
+    i = lax.broadcasted_iota(jnp.int32, (LANES, 2 * LANES), 0)
+    j = lax.broadcasted_iota(jnp.int32, (LANES, 2 * LANES), 1)
+    inside = (j < LANES) & ((i == j + 1) | (j == i + 1))
+    across = ((i == LANES - 1) & (j == LANES)) | ((i == 0) & (j == 2 * LANES - 1))
+    return jnp.where(inside | across, 1.0, 0.0).astype(jnp.bfloat16)
+
+
+def lane_sums(column, matrix):
+    n = column.shape[0]
+    flat = column.reshape(n * 8, LANES)
+    high = flat.astype(jnp.bfloat16)
+    low = (flat - high.astype(jnp.float32)).astype(jnp.bfloat16)
+    got = jnp.dot(high, matrix, preferred_element_type=jnp.float32)
+    got = got + jnp.dot(low, matrix, preferred_element_type=jnp.float32)
+    inside = got[:, :LANES].reshape(n, 8, LANES)
+    across = got[:, LANES:].reshape(n, 8, LANES)
+    return [inside[k] + pltpu.roll(across[k], 4, 0) for k in range(n)]
+
+
 def step(src, dst, coef, origin, reach, depth, coef_shift):
     (ox, oy), (dx, dy) = origin, coef_shift
     last, first = lane_masks()
+    matrix = lane_matrix()
     for x in range(ox - reach, ox + BX + reach):
         outside = max(ox - x, x - (ox + BX - 1), 0)
         rows = min(depth, reach - outside)
-        for y in range(oy - rows, oy + BY + rows):
+        y0, y1 = oy - rows, oy + BY + rows
+        sums = lane_sums(src[x, y0:y1], matrix) if x % 3 == 0 else None
+        for y in range(y0, y1):
             v = src[x, y]
-            other = pltpu.roll(v, 4, 0)
-            up = pltpu.roll(jnp.where(last, other, v), 1, 1)
-            down = pltpu.roll(jnp.where(first, other, v), LANES - 1, 1)
+            if sums is None:
+                other = pltpu.roll(v, 4, 0)
+                up = pltpu.roll(jnp.where(last, other, v), 1, 1)
+                down = pltpu.roll(jnp.where(first, other, v), LANES - 1, 1)
+                lanes = up + down
+            else:
+                lanes = sums[y - y0]
             total = (src[x - 1, y] + src[x + 1, y]) + (src[x, y - 1] + src[x, y + 1])
-            dst[x, y] = total + (up + down) + coef[x + dx, y + dy] * v
+            dst[x, y] = total + lanes + coef[x + dx, y + dy] * v
 
 
 def spread_kernel(field, out):
@@ -275,7 +302,7 @@
 
 
 def outer_second(
-    arm, chi, wide, y1, y2, coef, s2, s3, dens, total, other, out, a, b, flat, mixed
+    arm, chi, wide, y1, y2, coef, s2, s3, dens, out, a, b, flat, mixed
 ):
     a[0 : BX + 8, 4:8] = wide[...]
     unpack(arm, a, MID_REACH, y1, y2, (4, 4))
@@ -300,13 +327,11 @@
         mixture = term if mixture is None else mixture + term
     mixed[...] = mixture.reshape(rows)
     n = BX * BY
-    tail = total[...] + other[...]
     for s in range(SPECIES):
         for i, src in enumerate((flat, mixed)):
             for half in range(2):
                 at = (2 * i + half) * n
                 out[s, at : at + n, :] = src[pl.ds(half * 4 + s, n, stride=8), :]
-        out[s, 4 * n : 4 * n + 8, :] = tail
 
 
 def finish(cell_count, arm, chi, back, field, new, volume):
@@ -452,8 +477,10 @@
         jax.ShapeDtypeStruct((arms, 4 * n + 8, LANES), jnp.float32),
         [scratch(BX + 8, BY + 8)] * 2 + [pltpu.VMEM((8 * n, LANES), jnp.float32)] * 2,
         scalars=2,
-        arrays=9,
-    )(arm, flory_chi, wide, y1, y2, coef, s2, s3, dens, total, other)
+        arrays=7,
+    )(arm, flory_chi, wide, y1, y2, coef, s2, s3, dens)
+    tail = jnp.broadcast_to(total + other, (arms, 8, LANES))
+    out = lax.dynamic_update_slice(out, tail, (0, 4 * n, 0))
 
     back = lax.all_to_all(out, "arm", 0, 0)
     result = jax.ShapeDtypeStruct(field_here.shape, jnp.float32)

time: 180 us -> 179 us (level)
  no operation moved by 1% of the time
where the time goes in v8:
time: 179 us
  waiting for transfers between devices  60.3 us (34%)
  starting transfers between devices  58.3 us (33%)
  blocking collectives  43.9 us (25%)
  Pallas kernels  14.1 us (8%)
    ppermute x5, starting transfers between devices, along_y(): second = lax.ppermute(second, ('arm', 'gy'), second_pairs)  32.8 us
    all_to_all x1, blocking collectives, local(): back = lax.all_to_all(out, 'arm', 0, 0)  28.8 us
    ppermute x2, waiting for transfers between devices, along_z(): return lax.ppermute(tile, 'gy', [(i, i ^ bit) for i in range(size_gy)])  18.8 us
    all_to_all x1, blocking collectives, local(): lax.all_to_all(spread, ('gx', 'gy'), 0, 0, axis_index_groups=xy_groups)  15.1 us
    all_to_all x1, waiting for transfers between devices, local(): recv = lax.all_to_all(payload, 'arm', 0, 0)  14.5 us
    ppermute x5, waiting for transfers between devices, along_y(): second = lax.ppermute(second, ('arm', 'gy'), second_pairs)  10.1 us
    ppermute x5, waiting for transfers between devices, along_y(): return (lax.ppermute(first, ('arm', 'gy'), first_pairs), second)  9.85 us
    ppermute x5, starting transfers between devices, along_y(): return (lax.ppermute(first, ('arm', 'gy'), first_pairs), second)  9.6 us
  transfers between devices with their start and end apart: 17, of which 8 were waited for; matrix products, arithmetic and copies ran while one was open for 0% of the time, Pallas kernels for 0%

profile of v8, /device:TPU:6, one launch (start us, length us, event | category | flops | bytes accessed | tf_op | source)
XLA Modules:
  0.0 178.6 jit_solution(1375363956862574056)
XLA Ops:
  0.6 0.0 copy-start
  0.6 1.0 copy-done
  1.7 0.9 shard_map.41
  2.6 5.9 %all-to-all-start = ((f32[4,256,128]{2,1,0:T(8,128)}), f32[4,256,128]{2,1,0:T(8,128)S(1)}, u32[]{:S(2)}, u32[]{:S(2)}) async-start(f32[4,256,128]{2,1,0:T(8,128)} %shard_map.41), calls=%async_computation | async-start | bytes 1048576 | tf_op jit(solution)/shard_map/all_to_all | solution.py:415
  8.5 14.5 %all-to-all-done.recv = f32[4,256,128]{2,1,0:T(8,128)S(1)} async-done(((f32[4,256,128]{2,1,0:T(8,128)}), f32[4,256,128]{2,1,0:T(8,128)S(1)}, u32[]{:S(2)}, u32[]{:S(2)}) %all-to-all-start) | async-done | bytes 524320 | tf_op jit(solution)/shard_map/all_to_all | solution.py:415
  22.9 0.3 shard_map.42
  23.2 1.9 %collective-permute-start.2 = (f32[32,3,8,128]{3,2,1,0:T(8,128)S(1)}, f32[32,3,8,128]{3,2,1,0:T(8,128)S(1)}, u32[]{:S(2)}, u32[]{:S(2)}) collective-permute-start(f32[32,3,8,128]{3,2,1,0:T(8,128)S(1)} %get-tuple-element.35), channel_id=1, source_target_pairs={{0,128},{128,0},{256,384},{384,256},{1,129},{129,1},{257,385},{385... | collective-permute-start | bytes 1179656 | tf_op jit(solution)/shard_map/ppermute | solution.py:395
  25.2 11.2 %collective-permute-start.3 = (f32[32,3,8,128]{3,2,1,0:T(8,128)S(1)}, f32[32,3,8,128]{3,2,1,0:T(8,128)S(1)}, u32[]{:S(2)}, u32[]{:S(2)}) collective-permute-start(f32[32,3,8,128]{3,2,1,0:T(8,128)S(1)} %get-tuple-element.36), channel_id=1, source_target_pairs={{0,399},{128,256},{256,128},{384,1},{1,384},{129,257},{257,129},{3... | collective-permute-start | bytes 1179656 | tf_op jit(solution)/shard_map/ppermute | solution.py:394
  36.4 0.0 collective-permute-start
  36.4 1.7 collective-permute-start.1
  38.1 2.5 %collective-permute-done.low.xlow = f32[7,4,8,128]{3,2,1,0:T(8,128)S(1)} collective-permute-done((f32[7,4,8,128]{3,2,1,0:T(8,128)S(1)}, f32[7,4,8,128]{3,2,1,0:T(8,128)S(1)}, u32[]{:S(2)}, u32[]{:S(2)}) %collective-permute-start) | collective-permute-done | bytes 114720 | tf_op jit(solution)/shard_map/ppermute | solution.py:399
  40.6 0.0 collective-permute-done.1.high.xhigh
  40.6 1.9 %collective-permute-start.4 = (f32[30,8,128]{2,1,0:T(8,128)S(1)}, f32[30,8,128]{2,1,0:T(8,128)S(1)}, u32[]{:S(2)}, u32[]{:S(2)}) collective-permute-start(f32[30,8,128]{2,1,0:T(8,128)S(1)} %get-tuple-element.37), channel_id=1, source_target_pairs={{0,128},{128,0},{256,384},{384,256},{1,129},{129,1},{257,385},{385... | collective-permute-start | bytes 368648 | tf_op jit(solution)/shard_map/ppermute | solution.py:395
  42.6 5.4 %collective-permute-start.5 = (f32[30,8,128]{2,1,0:T(8,128)S(1)}, f32[30,8,128]{2,1,0:T(8,128)S(1)}, u32[]{:S(2)}, u32[]{:S(2)}) collective-permute-start(f32[30,8,128]{2,1,0:T(8,128)S(1)} %get-tuple-element.38), channel_id=1, source_target_pairs={{0,399},{128,256},{256,128},{384,1},{1,384},{129,257},{257,129},{3... | collective-permute-start | bytes 368648 | tf_op jit(solution)/shard_map/ppermute | solution.py:394
  48.0 0.0 collective-permute-done.4.c1
  48.0 4.9 %collective-permute-done.5.c2 = f32[30,8,128]{2,1,0:T(8,128)S(1)} collective-permute-done((f32[30,8,128]{2,1,0:T(8,128)S(1)}, f32[30,8,128]{2,1,0:T(8,128)S(1)}, u32[]{:S(2)}, u32[]{:S(2)}) %collective-permute-start.5) | collective-permute-done | bytes 122912 | tf_op jit(solution)/shard_map/ppermute | solution.py:394
  52.8 0.0 collective-permute-done.2.y1
  52.8 0.0 collective-permute-done.3.y2
  52.9 2.1 %shard_map.44 = (f32[46,10,8,128]{3,2,1,0:T(8,128)S(1)}, f32[32,4,8,128]{3,2,1,0:T(8,128)S(1)}, f32[32,4,8,128]{3,2,1,0:T(8,128)S(1)}, f32[40,4,8,128]{3,2,1,0:T...) custom-call(s32[1]{0:T(128)} %bitcast.arm, f32[32,4,8,128]{3,2,1,0:T(8,128)S(1)} %bitcast.7, ...), custom_call_target="tpu_custom_call" | custom-call | tf_op jit(solution)/shard_map/pallas_call | solution.py:438
  54.9 1.9 %collective-permute-start.6 = (f32[140,8,128]{2,1,0:T(8,128)S(1)}, f32[140,8,128]{2,1,0:T(8,128)S(1)}, u32[]{:S(2)}, u32[]{:S(2)}) collective-permute-start(f32[140,8,128]{2,1,0:T(8,128)S(1)} %get-tuple-element.40), channel_id=1, source_target_pairs={{0,128},{128,0},{256,384},{384,256},{1,129},{129,1},{257,385},{385... | collective-permute-start | bytes 1720328 | tf_op jit(solution)/shard_map/ppermute | solution.py:395
  56.9 6.0 %collective-permute-start.7 = (f32[140,8,128]{2,1,0:T(8,128)S(1)}, f32[140,8,128]{2,1,0:T(8,128)S(1)}, u32[]{:S(2)}, u32[]{:S(2)}) collective-permute-start(f32[140,8,128]{2,1,0:T(8,128)S(1)} %get-tuple-element.41), channel_id=1, source_target_pairs={{0,399},{128,256},{256,128},{384,1},{1,384},{129,257},{257,129},{3... | collective-permute-start | bytes 1720328 | tf_op jit(solution)/shard_map/ppermute | solution.py:394
  62.8 9.8 %collective-permute-done.6.y1 = f32[140,8,128]{2,1,0:T(8,128)S(1)} collective-permute-done((f32[140,8,128]{2,1,0:T(8,128)S(1)}, f32[140,8,128]{2,1,0:T(8,128)S(1)}, u32[]{:S(2)}, u32[]{:S(2)}) %collective-permute-start.6) | collective-permute-done | bytes 573472 | tf_op jit(solution)/shard_map/ppermute | solution.py:395
  72.7 5.2 %collective-permute-done.7.y2 = f32[140,8,128]{2,1,0:T(8,128)S(1)} collective-permute-done((f32[140,8,128]{2,1,0:T(8,128)S(1)}, f32[140,8,128]{2,1,0:T(8,128)S(1)}, u32[]{:S(2)}, u32[]{:S(2)}) %collective-permute-start.7) | collective-permute-done | bytes 573472 | tf_op jit(solution)/shard_map/ppermute | solution.py:394
  77.9 2.4 %shard_map.45 = (f32[32,4,8,128]{3,2,1,0:T(8,128)S(1)}, f32[32,4,8,128]{3,2,1,0:T(8,128)S(1)}, f32[32,4,8,128]{3,2,1,0:T(8,128)S(1)}, f32[32,4,8,128]{3,2,1,0:T(...) custom-call(s32[1]{0:T(128)} %bitcast.arm, f32[40,4,8,128]{3,2,1,0:T(8,128)S(1)} %get-tuple-element.39.wide.s4, ...), custom_call_target="tpu_custom_call" | custom-call | tf_op jit(solution)/shard_map/pallas_call | solution.py:446
  80.4 1.9 %collective-permute-start.8 = (f32[32,4,8,128]{3,2,1,0:T(8,128)S(1)}, f32[32,4,8,128]{3,2,1,0:T(8,128)S(1)}, u32[]{:S(2)}, u32[]{:S(2)}) collective-permute-start(f32[32,4,8,128]{3,2,1,0:T(8,128)S(1)} %get-tuple-element.44.own), channel_id=1, source_target_pairs={{0,128},{128,0},{256,384},{384,256},{1,129},{129,1},{257,385},{385... | collective-permute-start | bytes 1572872 | tf_op jit(solution)/shard_map/ppermute | solution.py:395
  82.3 5.4 %collective-permute-start.9 = (f32[32,4,8,128]{3,2,1,0:T(8,128)S(1)}, f32[32,4,8,128]{3,2,1,0:T(8,128)S(1)}, u32[]{:S(2)}, u32[]{:S(2)}) collective-permute-start(f32[32,4,8,128]{3,2,1,0:T(8,128)S(1)} %get-tuple-element.44.own), channel_id=1, source_target_pairs={{0,399},{128,256},{256,128},{384,1},{1,384},{129,257},{257,129},{3... | collective-permute-start | bytes 1572872 | tf_op jit(solution)/shard_map/ppermute | solution.py:394
  87.7 15.1 %all_to_all.15.got = f32[32,8,128]{2,1,0:T(8,128)S(1)} all-to-all(f32[32,8,128]{2,1,0:T(8,128)S(1)} %get-tuple-element.45), channel_id=1, replica_groups={{0,4,8,12,16,20,24,28,32,36,40,44,48,52,56,60,64,68,72,76,80,84,88,92,9..., dimensions={0} | all-to-all | bytes 262144 | tf_op jit(solution)/shard_map/all_to_all | solution.py:455
  102.8 0.0 collective-permute-done.8.first.y1
  102.8 0.0 collective-permute-done.9.second.y2
  102.8 0.1 shard_map.46
  102.9 0.1 collective-permute-start.10
  103.0 1.6 collective-permute-start.11
  104.6 4.6 %collective-permute-done.10.xlow = f32[76,8,128]{2,1,0:T(8,128)S(1)} collective-permute-done((f32[76,8,128]{2,1,0:T(8,128)S(1)}, f32[76,8,128]{2,1,0:T(8,128)S(1)}, u32[]{:S(2)}, u32[]{:S(2)}) %collective-permute-start.10) | collective-permute-done | bytes 311328 | tf_op jit(solution)/shard_map/ppermute | solution.py:399
  109.2 0.0 collective-permute-done.11.xhigh
  109.2 2.9 %shard_map.47 = (f32[32,4,8,128]{3,2,1,0:T(8,128)S(1)}, f32[40,4,8,128]{3,2,1,0:T(8,128)S(1)}, f32[140,8,128]{2,1,0:T(8,128)S(1)}, f32[140,8,128]{2,1,0:T(8,128)S(1)}, f32[8,128]{1,0:T(8,128)S(1)}) custom-call(s32[1]{0:T(128)} %bitcast.arm, f32[32,4,8,128]{3,2,1,0:T(8,128)S(1)} %get-tuple-element.44.own, f32[76,8,128]{2,1,0:T(8,128)S(1)} %collective-permute-done.10.xlow, ...), custom_call_target="tpu_custom_call" | custom-call | tf_op jit(solution)/shard_map/pallas_call | solution.py:465
  112.1 1.9 %collective-permute-start.12 = (f32[140,8,128]{2,1,0:T(8,128)S(1)}, f32[140,8,128]{2,1,0:T(8,128)S(1)}, u32[]{:S(2)}, u32[]{:S(2)}) collective-permute-start(f32[140,8,128]{2,1,0:T(8,128)S(1)} %get-tuple-element.54), channel_id=1, source_target_pairs={{0,128},{128,0},{256,384},{384,256},{1,129},{129,1},{257,385},{385... | collective-permute-start | bytes 1720328 | tf_op jit(solution)/shard_map/ppermute | solution.py:395
  114.0 4.9 %collective-permute-start.13 = (f32[140,8,128]{2,1,0:T(8,128)S(1)}, f32[140,8,128]{2,1,0:T(8,128)S(1)}, u32[]{:S(2)}, u32[]{:S(2)}) collective-permute-start(f32[140,8,128]{2,1,0:T(8,128)S(1)} %get-tuple-element.55), channel_id=1, source_target_pairs={{0,399},{128,256},{256,128},{384,1},{1,384},{129,257},{257,129},{3... | collective-permute-start | bytes 1720328 | tf_op jit(solution)/shard_map/ppermute | solution.py:394
  118.9 1.9 %collective-permute-start.14 = (f32[8,128]{1,0:T(8,128)S(1)}, f32[8,128]{1,0:T(8,128)S(1)}, u32[]{:S(2)}, u32[]{:S(2)}) collective-permute-start(f32[8,128]{1,0:T(8,128)S(1)} %get-tuple-element.52.total), channel_id=1, source_target_pairs={{0,1},{1,0},{2,3},{3,2},{4,5},{5,4},{6,7},{7,6},{8,9},{9,8},{10,11... | collective-permute-start | bytes 12296 | tf_op jit(solution)/shard_map/ppermute | solution.py:410
  120.8 9.2 %collective-permute-done.14 = f32[8,128]{1,0:T(8,128)S(1)} collective-permute-done((f32[8,128]{1,0:T(8,128)S(1)}, f32[8,128]{1,0:T(8,128)S(1)}, u32[]{:S(2)}, u32[]{:S(2)}) %collective-permute-start.14) | collective-permute-done | bytes 4128 | tf_op jit(solution)/shard_map/ppermute | solution.py:410
  130.0 4.6 %collective-permute-start.15 = (f32[8,128]{1,0:T(8,128)S(1)}, f32[8,128]{1,0:T(8,128)S(1)}, u32[]{:S(2)}, u32[]{:S(2)}) collective-permute-start(f32[8,128]{1,0:T(8,128)S(1)} %add.6), channel_id=1, source_target_pairs={{0,2},{1,3},{2,0},{3,1},{4,6},{5,7},{6,4},{7,5},{8,10},{9,11},{10,... | collective-permute-start | bytes 12296 | tf_op jit(solution)/shard_map/ppermute | solution.py:410
  134.6 9.6 %collective-permute-done.15 = f32[8,128]{1,0:T(8,128)S(1)} collective-permute-done((f32[8,128]{1,0:T(8,128)S(1)}, f32[8,128]{1,0:T(8,128)S(1)}, u32[]{:S(2)}, u32[]{:S(2)}) %collective-permute-start.15) | collective-permute-done | bytes 4128 | tf_op jit(solution)/shard_map/ppermute | solution.py:410
  144.2 0.0 collective-permute-done.12.y1
  144.2 0.0 collective-permute-done.13.y2
  144.3 3.5 %shard_map.48 = f32[4,520,128]{2,1,0:T(8,128)S(1)} custom-call(s32[1]{0:T(128)} %bitcast.arm, f32[4,4]{1,0:T(4,128)S(1)} %copy-done.2, f32[40,4,8,128]{3,2,1,0:T(8,128)S(1)} %get-tuple-element.53.wide, f32[140,8,128]{2,1,0:T(8,128)S(1)} %collective-permute-done.12.y1, f32[140,8,128]{2,1,0:T(8,128)S(1)} %collective-permute-done.13.y2, ...), custom_call_target="tpu_custom_call" | custom-call | tf_op jit(solution)/shard_map/pallas_call | solution.py:475
  147.8 0.0 copy-start.1
  147.8 28.8 %all_to_all.16.back = f32[4,520,128]{2,1,0:T(8,128)S(1)} all-to-all(f32[4,520,128]{2,1,0:T(8,128)S(1)} %broadcast_dynamic-update-slice_fusion), channel_id=1, replica_groups=mesh['arm'=4,'gx'=8,'gy'=16] {'arm'}, dimensions={0} | all-to-all | bytes 2129920 | tf_op jit(solution)/shard_map/all_to_all | solution.py:485
  176.6 0.0 copy-done.1
  176.6 2.0 %shard_map.49 = (f32[32,16,256]{2,1,0:T(8,128)}, f32[32,16,256]{2,1,0:T(8,128)}) custom-call(s32[1]{0:T(128)} %bitcast.arm, f32[4,4]{1,0:T(4,128)S(1)} %copy-done.2, f32[4,520,128]{2,1,0:T(8,128)S(1)} %all_to_all.16.back, f32[32,16,256]{2,1,0:T(8,128)S(1)} %bitcast.6), custom_call_target="tpu_custom_call" | custom-call | tf_op jit(solution)/shard_map/pallas_call | solution.py:487
  (6 shorter events, 0.0 us)
Async XLA Ops:
  0.6 1.0 copy-start
  2.6 20.4 %all-to-all-start = ((f32[4,256,128]{2,1,0:T(8,128)}), f32[4,256,128]{2,1,0:T(8,128)S(1)}, u32[]{:S(2)}, u32[]{:S(2)}) async-start(f32[4,256,128]{2,1,0:T(8,128)} %shard_map.41), calls=%async_computation | async-start | bytes 1048576 | tf_op jit(solution)/shard_map/all_to_all | solution.py:415
  23.2 29.6 %collective-permute-start.2 = (f32[32,3,8,128]{3,2,1,0:T(8,128)S(1)}, f32[32,3,8,128]{3,2,1,0:T(8,128)S(1)}, u32[]{:S(2)}, u32[]{:S(2)}) collective-permute-start(f32[32,3,8,128]{3,2,1,0:T(8,128)S(1)} %get-tuple-element.35), channel_id=1, source_target_pairs={{0,128},{128,0},{256,384},{384,256},{1,129},{129,1},{257,385},{385... | collective-permute-start | bytes 1179656 | tf_op jit(solution)/shard_map/ppermute | solution.py:395
  25.2 27.7 %collective-permute-start.3 = (f32[32,3,8,128]{3,2,1,0:T(8,128)S(1)}, f32[32,3,8,128]{3,2,1,0:T(8,128)S(1)}, u32[]{:S(2)}, u32[]{:S(2)}) collective-permute-start(f32[32,3,8,128]{3,2,1,0:T(8,128)S(1)} %get-tuple-element.36), channel_id=1, source_target_pairs={{0,399},{128,256},{256,128},{384,1},{1,384},{129,257},{257,129},{3... | collective-permute-start | bytes 1179656 | tf_op jit(solution)/shard_map/ppermute | solution.py:394
  36.4 4.2 %collective-permute-start = (f32[7,4,8,128]{3,2,1,0:T(8,128)S(1)}, f32[7,4,8,128]{3,2,1,0:T(8,128)S(1)}, u32[]{:S(2)}, u32[]{:S(2)}) collective-permute-start(f32[7,4,8,128]{3,2,1,0:T(8,128)S(1)} %get-tuple-element.33), channel_id=1, source_target_pairs={{0,16},{16,32},{32,48},{48,64},{64,80},{80,96},{96,112},{112,0},{1... | collective-permute-start | bytes 344072 | tf_op jit(solution)/shard_map/ppermute | solution.py:399
  36.4 4.2 %collective-permute-start.1 = (f32[7,4,8,128]{3,2,1,0:T(8,128)S(1)}, f32[7,4,8,128]{3,2,1,0:T(8,128)S(1)}, u32[]{:S(2)}, u32[]{:S(2)}) collective-permute-start(f32[7,4,8,128]{3,2,1,0:T(8,128)S(1)} %get-tuple-element.34), channel_id=1, source_target_pairs={{0,112},{16,0},{32,16},{48,32},{64,48},{80,64},{96,80},{112,96},{1... | collective-permute-start | bytes 344072 | tf_op jit(solution)/shard_map/ppermute | solution.py:400
  40.6 7.3 %collective-permute-start.4 = (f32[30,8,128]{2,1,0:T(8,128)S(1)}, f32[30,8,128]{2,1,0:T(8,128)S(1)}, u32[]{:S(2)}, u32[]{:S(2)}) collective-permute-start(f32[30,8,128]{2,1,0:T(8,128)S(1)} %get-tuple-element.37), channel_id=1, source_target_pairs={{0,128},{128,0},{256,384},{384,256},{1,129},{129,1},{257,385},{385... | collective-permute-start | bytes 368648 | tf_op jit(solution)/shard_map/ppermute | solution.py:395
  42.6 10.3 %collective-permute-start.5 = (f32[30,8,128]{2,1,0:T(8,128)S(1)}, f32[30,8,128]{2,1,0:T(8,128)S(1)}, u32[]{:S(2)}, u32[]{:S(2)}) collective-permute-start(f32[30,8,128]{2,1,0:T(8,128)S(1)} %get-tuple-element.38), channel_id=1, source_target_pairs={{0,399},{128,256},{256,128},{384,1},{1,384},{129,257},{257,129},{3... | collective-permute-start | bytes 368648 | tf_op jit(solution)/shard_map/ppermute | solution.py:394
  54.9 17.7 %collective-permute-start.6 = (f32[140,8,128]{2,1,0:T(8,128)S(1)}, f32[140,8,128]{2,1,0:T(8,128)S(1)}, u32[]{:S(2)}, u32[]{:S(2)}) collective-permute-start(f32[140,8,128]{2,1,0:T(8,128)S(1)} %get-tuple-element.40), channel_id=1, source_target_pairs={{0,128},{128,0},{256,384},{384,256},{1,129},{129,1},{257,385},{385... | collective-permute-start | bytes 1720328 | tf_op jit(solution)/shard_map/ppermute | solution.py:395
  56.9 21.1 %collective-permute-start.7 = (f32[140,8,128]{2,1,0:T(8,128)S(1)}, f32[140,8,128]{2,1,0:T(8,128)S(1)}, u32[]{:S(2)}, u32[]{:S(2)}) collective-permute-start(f32[140,8,128]{2,1,0:T(8,128)S(1)} %get-tuple-element.41), channel_id=1, source_target_pairs={{0,399},{128,256},{256,128},{384,1},{1,384},{129,257},{257,129},{3... | collective-permute-start | bytes 1720328 | tf_op jit(solution)/shard_map/ppermute | solution.py:394
  80.4 22.4 %collective-permute-start.8 = (f32[32,4,8,128]{3,2,1,0:T(8,128)S(1)}, f32[32,4,8,128]{3,2,1,0:T(8,128)S(1)}, u32[]{:S(2)}, u32[]{:S(2)}) collective-permute-start(f32[32,4,8,128]{3,2,1,0:T(8,128)S(1)} %get-tuple-element.44.own), channel_id=1, source_target_pairs={{0,128},{128,0},{256,384},{384,256},{1,129},{129,1},{257,385},{385... | collective-permute-start | bytes 1572872 | tf_op jit(solution)/shard_map/ppermute | solution.py:395
  82.3 20.5 %collective-permute-start.9 = (f32[32,4,8,128]{3,2,1,0:T(8,128)S(1)}, f32[32,4,8,128]{3,2,1,0:T(8,128)S(1)}, u32[]{:S(2)}, u32[]{:S(2)}) collective-permute-start(f32[32,4,8,128]{3,2,1,0:T(8,128)S(1)} %get-tuple-element.44.own), channel_id=1, source_target_pairs={{0,399},{128,256},{256,128},{384,1},{1,384},{129,257},{257,129},{3... | collective-permute-start | bytes 1572872 | tf_op jit(solution)/shard_map/ppermute | solution.py:394
  102.9 6.3 %collective-permute-start.10 = (f32[76,8,128]{2,1,0:T(8,128)S(1)}, f32[76,8,128]{2,1,0:T(8,128)S(1)}, u32[]{:S(2)}, u32[]{:S(2)}) collective-permute-start(f32[76,8,128]{2,1,0:T(8,128)S(1)} %get-tuple-element.46), channel_id=1, source_target_pairs={{0,16},{16,32},{32,48},{48,64},{64,80},{80,96},{96,112},{112,0},{1... | collective-permute-start | bytes 933896 | tf_op jit(solution)/shard_map/ppermute | solution.py:399
  103.0 6.2 %collective-permute-start.11 = (f32[76,8,128]{2,1,0:T(8,128)S(1)}, f32[76,8,128]{2,1,0:T(8,128)S(1)}, u32[]{:S(2)}, u32[]{:S(2)}) collective-permute-start(f32[76,8,128]{2,1,0:T(8,128)S(1)} %get-tuple-element.47), channel_id=1, source_target_pairs={{0,112},{16,0},{32,16},{48,32},{64,48},{80,64},{96,80},{112,96},{1... | collective-permute-start | bytes 933896 | tf_op jit(solution)/shard_map/ppermute | solution.py:400
  109.2 35.1 %copy-start.2 = (f32[4,4]{1,0:T(4,128)S(1)}, f32[4,4]{1,0:T(4,128)}, u32[]{:S(2)}) copy-start(f32[4,4]{1,0:T(4,128)} %chi.3) | copy-start | bytes 196
  112.1 32.1 %collective-permute-start.12 = (f32[140,8,128]{2,1,0:T(8,128)S(1)}, f32[140,8,128]{2,1,0:T(8,128)S(1)}, u32[]{:S(2)}, u32[]{:S(2)}) collective-permute-start(f32[140,8,128]{2,1,0:T(8,128)S(1)} %get-tuple-element.54), channel_id=1, source_target_pairs={{0,128},{128,0},{256,384},{384,256},{1,129},{129,1},{257,385},{385... | collective-permute-start | bytes 1720328 | tf_op jit(solution)/shard_map/ppermute | solution.py:395
  114.0 30.2 %collective-permute-start.13 = (f32[140,8,128]{2,1,0:T(8,128)S(1)}, f32[140,8,128]{2,1,0:T(8,128)S(1)}, u32[]{:S(2)}, u32[]{:S(2)}) collective-permute-start(f32[140,8,128]{2,1,0:T(8,128)S(1)} %get-tuple-element.55), channel_id=1, source_target_pairs={{0,399},{128,256},{256,128},{384,1},{1,384},{129,257},{257,129},{3... | collective-permute-start | bytes 1720328 | tf_op jit(solution)/shard_map/ppermute | solution.py:394
  118.9 11.1 %collective-permute-start.14 = (f32[8,128]{1,0:T(8,128)S(1)}, f32[8,128]{1,0:T(8,128)S(1)}, u32[]{:S(2)}, u32[]{:S(2)}) collective-permute-start(f32[8,128]{1,0:T(8,128)S(1)} %get-tuple-element.52.total), channel_id=1, source_target_pairs={{0,1},{1,0},{2,3},{3,2},{4,5},{5,4},{6,7},{7,6},{8,9},{9,8},{10,11... | collective-permute-start | bytes 12296 | tf_op jit(solution)/shard_map/ppermute | solution.py:410
  130.0 14.2 %collective-permute-start.15 = (f32[8,128]{1,0:T(8,128)S(1)}, f32[8,128]{1,0:T(8,128)S(1)}, u32[]{:S(2)}, u32[]{:S(2)}) collective-permute-start(f32[8,128]{1,0:T(8,128)S(1)} %add.6), channel_id=1, source_target_pairs={{0,2},{1,3},{2,0},{3,1},{4,6},{5,7},{6,4},{7,5},{8,10},{9,11},{10,... | collective-permute-start | bytes 12296 | tf_op jit(solution)/shard_map/ppermute | solution.py:410
  147.8 28.8 %copy-start.1 = (f32[1,32,16,256]{3,2,1,0:T(8,128)S(1)}, f32[1,32,16,256]{3,2,1,0:T(8,128)}, u32[]{:S(2)}) copy-start(f32[1,32,16,256]{3,2,1,0:T(8,128)} %param.2) | copy-start | bytes 1572868

commit v9 on v8

--- a/solution.py
+++ b/solution.py
@@ -84,13 +84,24 @@
             dst[x, y] = total + lanes + coef[x + dx, y + dy] * v
 
 
-def spread_kernel(field, out):
+PARTS = 4
+PART = BX // PARTS
+
+
+def spread_kernel(field, out, held, sems):
     n = BX * BY
+    copies = []
+    for p in range(PARTS):
+        part = pl.ds(p * PART, PART)
+        copies.append(pltpu.make_async_copy(field.at[part], held.at[part], sems.at[p]))
+        copies[p].start()
     for x in range(BX):
+        if x % PART == 0:
+            copies[x // PART].wait()
         for half in range(2):
             for q in range(SPECIES):
                 at = half * n + x * BY
-                out[q, at : at + BY, :] = field[
+                out[q, at : at + BY, :] = held[
                     x, q * BY : (q + 1) * BY, half * LANES : (half + 1) * LANES
                 ]
 
@@ -334,7 +345,7 @@
                 out[s, at : at + n, :] = src[pl.ds(half * 4 + s, n, stride=8), :]
 
 
-def finish(cell_count, arm, chi, back, field, new, volume):
+def finish(cell_count, arm, chi, back, field, new_out, volume_out, new, volume, sems):
     n = BX * BY
     here = arm[0]
     tail = jnp.sum(back[:, 4 * n : 4 * n + 8], axis=0)
@@ -346,16 +357,27 @@
     for s in range(1, SPECIES):
         chi_sum = chi_sum + chi[here, s]
     mean_new = (1.0 - mixing) / cell_count * field_sum + mixing * chi_sum / SPECIES
-    for q in range(SPECIES):
-        for half in range(2):
-            lanes = slice(half * LANES, (half + 1) * LANES)
-            for x in range(BX):
-                at = half * n + x * BY
-                ys = slice(q * BY, (q + 1) * BY)
-                volume[x, ys, lanes] = scale * back[q, at : at + BY, :]
-                mixture = scale * back[q, 2 * n + at : 2 * n + at + BY, :]
-                old = field[x, ys, lanes]
-                new[x, ys, lanes] = old + mixing * (mixture - compress - old) - mean_new
+    copies = []
+    for p in range(PARTS):
+        for q in range(SPECIES):
+            for half in range(2):
+                lanes = slice(half * LANES, (half + 1) * LANES)
+                for x in range(p * PART, (p + 1) * PART):
+                    at = half * n + x * BY
+                    ys = slice(q * BY, (q + 1) * BY)
+                    volume[x, ys, lanes] = scale * back[q, at : at + BY, :]
+                    mixture = scale * back[q, 2 * n + at : 2 * n + at + BY, :]
+                    old = field[x, ys, lanes]
+                    new[x, ys, lanes] = (
+                        old + mixing * (mixture - compress - old) - mean_new
+                    )
+        part = pl.ds(p * PART, PART)
+        for i, (src, dst) in enumerate(((volume, volume_out), (new, new_out))):
+            copy = pltpu.make_async_copy(src.at[part], dst.at[part], sems.at[i, p])
+            copy.start()
+            copies.append(copy)
+    for copy in copies:
+        copy.wait()
 
 
 def tiles(*lead):
@@ -409,8 +431,14 @@
     def along_z(tile, bit):
         return lax.ppermute(tile, "gy", [(i, i ^ bit) for i in range(size_gy)])
 
-    payload = call(
-        spread_kernel, jax.ShapeDtypeStruct((arms, 2 * n, LANES), jnp.float32), arrays=1
+    block = pltpu.VMEM(field_here.shape, jnp.float32)
+    in_hbm = pl.BlockSpec(memory_space=pltpu.HBM)
+    payload = pl.pallas_call(
+        spread_kernel,
+        out_shape=jax.ShapeDtypeStruct((arms, 2 * n, LANES), jnp.float32),
+        in_specs=[in_hbm],
+        scratch_shapes=[block, pltpu.SemaphoreType.DMA((PARTS,))],
+        compiler_params=pltpu.CompilerParams(vmem_limit_bytes=60 * 1024 * 1024),
     )(field_here)
     recv = lax.all_to_all(payload, "arm", 0, 0)
     rows = tiles(BX, len(COEF_REACH))
@@ -484,8 +512,14 @@
 
     back = lax.all_to_all(out, "arm", 0, 0)
     result = jax.ShapeDtypeStruct(field_here.shape, jnp.float32)
-    field_out, volume = call(
-        functools.partial(finish, cell_count), (result, result), scalars=2, arrays=2
+    field_out, volume = pl.pallas_call(
+        functools.partial(finish, cell_count),
+        out_shape=(result, result),
+        in_specs=[pl.BlockSpec(memory_space=pltpu.SMEM)] * 2
+        + [pl.BlockSpec(memory_space=pltpu.VMEM)] * 2,
+        out_specs=(in_hbm, in_hbm),
+        scratch_shapes=[block, block, pltpu.SemaphoreType.DMA((2, PARTS))],
+        compiler_params=pltpu.CompilerParams(vmem_limit_bytes=VMEM_LIMIT),
     )(arm, flory_chi, back, field_here)
     return (field_out[None], volume[None])
 

time: 179 us -> 178 us (level)
  no operation moved by 1% of the time
where the time goes in v9:
time: 178 us
  waiting for transfers between devices  60.2 us (34%)
  starting transfers between devices  58.4 us (33%)
  blocking collectives  43.9 us (25%)
  Pallas kernels  14.3 us (8%)
    ppermute x5, starting transfers between devices, along_y(): second = lax.ppermute(second, ('arm', 'gy'), second_pairs)  32.8 us
    all_to_all x1, blocking collectives, local(): back = lax.all_to_all(out, 'arm', 0, 0)  28.8 us
    ppermute x2, waiting for transfers between devices, along_z(): return lax.ppermute(tile, 'gy', [(i, i ^ bit) for i in range(size_gy)])  18.7 us
    all_to_all x1, blocking collectives, local(): lax.all_to_all(spread, ('gx', 'gy'), 0, 0, axis_index_groups=xy_groups)  15.1 us
    all_to_all x1, waiting for transfers between devices, local(): recv = lax.all_to_all(payload, 'arm', 0, 0)  14.5 us
    ppermute x5, waiting for transfers between devices, along_y(): second = lax.ppermute(second, ('arm', 'gy'), second_pairs)  10.1 us
    ppermute x5, waiting for transfers between devices, along_y(): return (lax.ppermute(first, ('arm', 'gy'), first_pairs), second)  9.84 us
    ppermute x5, starting transfers between devices, along_y(): return (lax.ppermute(first, ('arm', 'gy'), first_pairs), second)  9.6 us
  transfers between devices with their start and end apart: 17, of which 8 were waited for; matrix products, arithmetic and copies ran while one was open for 0% of the time, Pallas kernels for 0%

profile of v9, /device:TPU:6, one launch (start us, length us, event | category | flops | bytes accessed | tf_op | source)
XLA Modules:
  0.0 177.8 jit_solution(17257607748390768119)
XLA Ops:
  0.6 1.9 %shard_map.41 = f32[4,256,128]{2,1,0:T(8,128)} custom-call(f32[32,16,256]{2,1,0:T(8,128)} %bitcast.5), custom_call_target="tpu_custom_call" | custom-call | tf_op jit(solution)/shard_map/pallas_call | solution.py:436
  2.6 5.9 %all-to-all-start = ((f32[4,256,128]{2,1,0:T(8,128)}), f32[4,256,128]{2,1,0:T(8,128)S(1)}, u32[]{:S(2)}, u32[]{:S(2)}) async-start(f32[4,256,128]{2,1,0:T(8,128)} %shard_map.41), calls=%async_computation | async-start | bytes 1048576 | tf_op jit(solution)/shard_map/all_to_all | solution.py:443
  8.5 14.5 %all-to-all-done.recv = f32[4,256,128]{2,1,0:T(8,128)S(1)} async-done(((f32[4,256,128]{2,1,0:T(8,128)}), f32[4,256,128]{2,1,0:T(8,128)S(1)}, u32[]{:S(2)}, u32[]{:S(2)}) %all-to-all-start) | async-done | bytes 524320 | tf_op jit(solution)/shard_map/all_to_all | solution.py:443
  23.0 0.3 shard_map.42
  23.3 1.9 %collective-permute-start.2 = (f32[32,3,8,128]{3,2,1,0:T(8,128)S(1)}, f32[32,3,8,128]{3,2,1,0:T(8,128)S(1)}, u32[]{:S(2)}, u32[]{:S(2)}) collective-permute-start(f32[32,3,8,128]{3,2,1,0:T(8,128)S(1)} %get-tuple-element.35), channel_id=1, source_target_pairs={{0,128},{128,0},{256,384},{384,256},{1,129},{129,1},{257,385},{385... | collective-permute-start | bytes 1179656 | tf_op jit(solution)/shard_map/ppermute | solution.py:417
  25.2 11.2 %collective-permute-start.3 = (f32[32,3,8,128]{3,2,1,0:T(8,128)S(1)}, f32[32,3,8,128]{3,2,1,0:T(8,128)S(1)}, u32[]{:S(2)}, u32[]{:S(2)}) collective-permute-start(f32[32,3,8,128]{3,2,1,0:T(8,128)S(1)} %get-tuple-element.36), channel_id=1, source_target_pairs={{0,399},{128,256},{256,128},{384,1},{1,384},{129,257},{257,129},{3... | collective-permute-start | bytes 1179656 | tf_op jit(solution)/shard_map/ppermute | solution.py:416
  36.4 0.0 collective-permute-start
  36.4 1.7 collective-permute-start.1
  38.2 2.5 %collective-permute-done.low.xlow = f32[7,4,8,128]{3,2,1,0:T(8,128)S(1)} collective-permute-done((f32[7,4,8,128]{3,2,1,0:T(8,128)S(1)}, f32[7,4,8,128]{3,2,1,0:T(8,128)S(1)}, u32[]{:S(2)}, u32[]{:S(2)}) %collective-permute-start) | collective-permute-done | bytes 114720 | tf_op jit(solution)/shard_map/ppermute | solution.py:421
  40.6 0.0 collective-permute-done.1.high.xhigh
  40.7 1.9 %collective-permute-start.4 = (f32[30,8,128]{2,1,0:T(8,128)S(1)}, f32[30,8,128]{2,1,0:T(8,128)S(1)}, u32[]{:S(2)}, u32[]{:S(2)}) collective-permute-start(f32[30,8,128]{2,1,0:T(8,128)S(1)} %get-tuple-element.37), channel_id=1, source_target_pairs={{0,128},{128,0},{256,384},{384,256},{1,129},{129,1},{257,385},{385... | collective-permute-start | bytes 368648 | tf_op jit(solution)/shard_map/ppermute | solution.py:417
  42.6 5.4 %collective-permute-start.5 = (f32[30,8,128]{2,1,0:T(8,128)S(1)}, f32[30,8,128]{2,1,0:T(8,128)S(1)}, u32[]{:S(2)}, u32[]{:S(2)}) collective-permute-start(f32[30,8,128]{2,1,0:T(8,128)S(1)} %get-tuple-element.38), channel_id=1, source_target_pairs={{0,399},{128,256},{256,128},{384,1},{1,384},{129,257},{257,129},{3... | collective-permute-start | bytes 368648 | tf_op jit(solution)/shard_map/ppermute | solution.py:416
  48.0 0.0 collective-permute-done.4.c1
  48.0 4.9 %collective-permute-done.5.c2 = f32[30,8,128]{2,1,0:T(8,128)S(1)} collective-permute-done((f32[30,8,128]{2,1,0:T(8,128)S(1)}, f32[30,8,128]{2,1,0:T(8,128)S(1)}, u32[]{:S(2)}, u32[]{:S(2)}) %collective-permute-start.5) | collective-permute-done | bytes 122912 | tf_op jit(solution)/shard_map/ppermute | solution.py:416
  52.9 0.0 collective-permute-done.2.y1
  52.9 0.0 collective-permute-done.3.y2
  52.9 1.9 %shard_map.44 = (f32[46,10,8,128]{3,2,1,0:T(8,128)S(1)}, f32[32,4,8,128]{3,2,1,0:T(8,128)S(1)}, f32[32,4,8,128]{3,2,1,0:T(8,128)S(1)}, f32[40,4,8,128]{3,2,1,0:T...) custom-call(s32[1]{0:T(128)} %bitcast.arm, f32[32,4,8,128]{3,2,1,0:T(8,128)S(1)} %bitcast.7, ...), custom_call_target="tpu_custom_call" | custom-call | tf_op jit(solution)/shard_map/pallas_call | solution.py:466
  54.8 1.9 %collective-permute-start.6 = (f32[140,8,128]{2,1,0:T(8,128)S(1)}, f32[140,8,128]{2,1,0:T(8,128)S(1)}, u32[]{:S(2)}, u32[]{:S(2)}) collective-permute-start(f32[140,8,128]{2,1,0:T(8,128)S(1)} %get-tuple-element.40), channel_id=1, source_target_pairs={{0,128},{128,0},{256,384},{384,256},{1,129},{129,1},{257,385},{385... | collective-permute-start | bytes 1720328 | tf_op jit(solution)/shard_map/ppermute | solution.py:417
  56.7 6.0 %collective-permute-start.7 = (f32[140,8,128]{2,1,0:T(8,128)S(1)}, f32[140,8,128]{2,1,0:T(8,128)S(1)}, u32[]{:S(2)}, u32[]{:S(2)}) collective-permute-start(f32[140,8,128]{2,1,0:T(8,128)S(1)} %get-tuple-element.41), channel_id=1, source_target_pairs={{0,399},{128,256},{256,128},{384,1},{1,384},{129,257},{257,129},{3... | collective-permute-start | bytes 1720328 | tf_op jit(solution)/shard_map/ppermute | solution.py:416
  62.7 9.8 %collective-permute-done.6.y1 = f32[140,8,128]{2,1,0:T(8,128)S(1)} collective-permute-done((f32[140,8,128]{2,1,0:T(8,128)S(1)}, f32[140,8,128]{2,1,0:T(8,128)S(1)}, u32[]{:S(2)}, u32[]{:S(2)}) %collective-permute-start.6) | collective-permute-done | bytes 573472 | tf_op jit(solution)/shard_map/ppermute | solution.py:417
  72.5 5.2 %collective-permute-done.7.y2 = f32[140,8,128]{2,1,0:T(8,128)S(1)} collective-permute-done((f32[140,8,128]{2,1,0:T(8,128)S(1)}, f32[140,8,128]{2,1,0:T(8,128)S(1)}, u32[]{:S(2)}, u32[]{:S(2)}) %collective-permute-start.7) | collective-permute-done | bytes 573472 | tf_op jit(solution)/shard_map/ppermute | solution.py:416
  77.8 2.3 %shard_map.45 = (f32[32,4,8,128]{3,2,1,0:T(8,128)S(1)}, f32[32,4,8,128]{3,2,1,0:T(8,128)S(1)}, f32[32,4,8,128]{3,2,1,0:T(8,128)S(1)}, f32[32,4,8,128]{3,2,1,0:T(...) custom-call(s32[1]{0:T(128)} %bitcast.arm, f32[40,4,8,128]{3,2,1,0:T(8,128)S(1)} %get-tuple-element.39.wide.s4, ...), custom_call_target="tpu_custom_call" | custom-call | tf_op jit(solution)/shard_map/pallas_call | solution.py:474
  80.1 1.9 %collective-permute-start.8 = (f32[32,4,8,128]{3,2,1,0:T(8,128)S(1)}, f32[32,4,8,128]{3,2,1,0:T(8,128)S(1)}, u32[]{:S(2)}, u32[]{:S(2)}) collective-permute-start(f32[32,4,8,128]{3,2,1,0:T(8,128)S(1)} %get-tuple-element.44.own), channel_id=1, source_target_pairs={{0,128},{128,0},{256,384},{384,256},{1,129},{129,1},{257,385},{385... | collective-permute-start | bytes 1572872 | tf_op jit(solution)/shard_map/ppermute | solution.py:417
  82.0 5.4 %collective-permute-start.9 = (f32[32,4,8,128]{3,2,1,0:T(8,128)S(1)}, f32[32,4,8,128]{3,2,1,0:T(8,128)S(1)}, u32[]{:S(2)}, u32[]{:S(2)}) collective-permute-start(f32[32,4,8,128]{3,2,1,0:T(8,128)S(1)} %get-tuple-element.44.own), channel_id=1, source_target_pairs={{0,399},{128,256},{256,128},{384,1},{1,384},{129,257},{257,129},{3... | collective-permute-start | bytes 1572872 | tf_op jit(solution)/shard_map/ppermute | solution.py:416
  87.4 15.1 %all_to_all.15.got = f32[32,8,128]{2,1,0:T(8,128)S(1)} all-to-all(f32[32,8,128]{2,1,0:T(8,128)S(1)} %get-tuple-element.45), channel_id=1, replica_groups={{0,4,8,12,16,20,24,28,32,36,40,44,48,52,56,60,64,68,72,76,80,84,88,92,9..., dimensions={0} | all-to-all | bytes 262144 | tf_op jit(solution)/shard_map/all_to_all | solution.py:483
  102.5 0.0 collective-permute-done.8.first.y1
  102.5 0.0 collective-permute-done.9.second.y2
  102.5 0.1 shard_map.46
  102.6 0.1 collective-permute-start.10
  102.7 1.6 collective-permute-start.11
  104.3 4.6 %collective-permute-done.10.xlow = f32[76,8,128]{2,1,0:T(8,128)S(1)} collective-permute-done((f32[76,8,128]{2,1,0:T(8,128)S(1)}, f32[76,8,128]{2,1,0:T(8,128)S(1)}, u32[]{:S(2)}, u32[]{:S(2)}) %collective-permute-start.10) | collective-permute-done | bytes 311328 | tf_op jit(solution)/shard_map/ppermute | solution.py:421
  108.9 0.0 collective-permute-done.11.xhigh
  108.9 0.0 copy-start.1
  108.9 2.7 %shard_map.47 = (f32[32,4,8,128]{3,2,1,0:T(8,128)S(1)}, f32[40,4,8,128]{3,2,1,0:T(8,128)S(1)}, f32[140,8,128]{2,1,0:T(8,128)S(1)}, f32[140,8,128]{2,1,0:T(8,128)S(1)}, f32[8,128]{1,0:T(8,128)S(1)}) custom-call(s32[1]{0:T(128)} %bitcast.arm, f32[32,4,8,128]{3,2,1,0:T(8,128)S(1)} %get-tuple-element.44.own, f32[76,8,128]{2,1,0:T(8,128)S(1)} %collective-permute-done.10.xlow, ...), custom_call_target="tpu_custom_call" | custom-call | tf_op jit(solution)/shard_map/pallas_call | solution.py:493
  111.6 1.9 %collective-permute-start.12 = (f32[140,8,128]{2,1,0:T(8,128)S(1)}, f32[140,8,128]{2,1,0:T(8,128)S(1)}, u32[]{:S(2)}, u32[]{:S(2)}) collective-permute-start(f32[140,8,128]{2,1,0:T(8,128)S(1)} %get-tuple-element.54), channel_id=1, source_target_pairs={{0,128},{128,0},{256,384},{384,256},{1,129},{129,1},{257,385},{385... | collective-permute-start | bytes 1720328 | tf_op jit(solution)/shard_map/ppermute | solution.py:417
  113.5 4.9 %collective-permute-start.13 = (f32[140,8,128]{2,1,0:T(8,128)S(1)}, f32[140,8,128]{2,1,0:T(8,128)S(1)}, u32[]{:S(2)}, u32[]{:S(2)}) collective-permute-start(f32[140,8,128]{2,1,0:T(8,128)S(1)} %get-tuple-element.55), channel_id=1, source_target_pairs={{0,399},{128,256},{256,128},{384,1},{1,384},{129,257},{257,129},{3... | collective-permute-start | bytes 1720328 | tf_op jit(solution)/shard_map/ppermute | solution.py:416
  118.4 1.9 %collective-permute-start.14 = (f32[8,128]{1,0:T(8,128)S(1)}, f32[8,128]{1,0:T(8,128)S(1)}, u32[]{:S(2)}, u32[]{:S(2)}) collective-permute-start(f32[8,128]{1,0:T(8,128)S(1)} %get-tuple-element.52.total), channel_id=1, source_target_pairs={{0,1},{1,0},{2,3},{3,2},{4,5},{5,4},{6,7},{7,6},{8,9},{9,8},{10,11... | collective-permute-start | bytes 12296 | tf_op jit(solution)/shard_map/ppermute | solution.py:432
  120.3 9.2 %collective-permute-done.14 = f32[8,128]{1,0:T(8,128)S(1)} collective-permute-done((f32[8,128]{1,0:T(8,128)S(1)}, f32[8,128]{1,0:T(8,128)S(1)}, u32[]{:S(2)}, u32[]{:S(2)}) %collective-permute-start.14) | collective-permute-done | bytes 4128 | tf_op jit(solution)/shard_map/ppermute | solution.py:432
  129.5 4.6 %collective-permute-start.15 = (f32[8,128]{1,0:T(8,128)S(1)}, f32[8,128]{1,0:T(8,128)S(1)}, u32[]{:S(2)}, u32[]{:S(2)}) collective-permute-start(f32[8,128]{1,0:T(8,128)S(1)} %add.6), channel_id=1, source_target_pairs={{0,2},{1,3},{2,0},{3,1},{4,6},{5,7},{6,4},{7,5},{8,10},{9,11},{10,... | collective-permute-start | bytes 12296 | tf_op jit(solution)/shard_map/ppermute | solution.py:432
  134.1 9.6 %collective-permute-done.15 = f32[8,128]{1,0:T(8,128)S(1)} collective-permute-done((f32[8,128]{1,0:T(8,128)S(1)}, f32[8,128]{1,0:T(8,128)S(1)}, u32[]{:S(2)}, u32[]{:S(2)}) %collective-permute-start.15) | collective-permute-done | bytes 4128 | tf_op jit(solution)/shard_map/ppermute | solution.py:432
  143.7 0.0 collective-permute-done.12.y1
  143.7 0.0 collective-permute-done.13.y2
  143.7 0.0 copy-done.1
  143.7 3.3 %shard_map.48 = f32[4,520,128]{2,1,0:T(8,128)S(1)} custom-call(s32[1]{0:T(128)} %bitcast.arm, f32[4,4]{1,0:T(4,128)S(1)} %copy-done.1, f32[40,4,8,128]{3,2,1,0:T(8,128)S(1)} %get-tuple-element.53.wide, f32[140,8,128]{2,1,0:T(8,128)S(1)} %collective-permute-done.12.y1, f32[140,8,128]{2,1,0:T(8,128)S(1)} %collective-permute-done.13.y2, ...), custom_call_target="tpu_custom_call" | custom-call | tf_op jit(solution)/shard_map/pallas_call | solution.py:503
  147.0 0.0 copy-start
  147.0 28.8 %all_to_all.16.back = f32[4,520,128]{2,1,0:T(8,128)S(1)} all-to-all(f32[4,520,128]{2,1,0:T(8,128)S(1)} %broadcast_dynamic-update-slice_fusion), channel_id=1, replica_groups=mesh['arm'=4,'gx'=8,'gy'=16] {'arm'}, dimensions={0} | all-to-all | bytes 2129920 | tf_op jit(solution)/shard_map/all_to_all | solution.py:513
  175.8 0.0 copy-done
  175.8 1.8 %shard_map.49 = (f32[32,16,256]{2,1,0:T(8,128)}, f32[32,16,256]{2,1,0:T(8,128)}) custom-call(s32[1]{0:T(128)} %bitcast.arm, f32[4,4]{1,0:T(4,128)S(1)} %copy-done.1, f32[4,520,128]{2,1,0:T(8,128)S(1)} %all_to_all.16.back, f32[32,16,256]{2,1,0:T(8,128)S(1)} %bitcast.6), custom_call_target="tpu_custom_call" | custom-call | tf_op jit(solution)/shard_map/pallas_call | solution.py:515
  (4 shorter events, 0.0 us)
Async XLA Ops:
  2.6 20.4 %all-to-all-start = ((f32[4,256,128]{2,1,0:T(8,128)}), f32[4,256,128]{2,1,0:T(8,128)S(1)}, u32[]{:S(2)}, u32[]{:S(2)}) async-start(f32[4,256,128]{2,1,0:T(8,128)} %shard_map.41), calls=%async_computation | async-start | bytes 1048576 | tf_op jit(solution)/shard_map/all_to_all | solution.py:443
  23.3 29.6 %collective-permute-start.2 = (f32[32,3,8,128]{3,2,1,0:T(8,128)S(1)}, f32[32,3,8,128]{3,2,1,0:T(8,128)S(1)}, u32[]{:S(2)}, u32[]{:S(2)}) collective-permute-start(f32[32,3,8,128]{3,2,1,0:T(8,128)S(1)} %get-tuple-element.35), channel_id=1, source_target_pairs={{0,128},{128,0},{256,384},{384,256},{1,129},{129,1},{257,385},{385... | collective-permute-start | bytes 1179656 | tf_op jit(solution)/shard_map/ppermute | solution.py:417
  25.2 27.7 %collective-permute-start.3 = (f32[32,3,8,128]{3,2,1,0:T(8,128)S(1)}, f32[32,3,8,128]{3,2,1,0:T(8,128)S(1)}, u32[]{:S(2)}, u32[]{:S(2)}) collective-permute-start(f32[32,3,8,128]{3,2,1,0:T(8,128)S(1)} %get-tuple-element.36), channel_id=1, source_target_pairs={{0,399},{128,256},{256,128},{384,1},{1,384},{129,257},{257,129},{3... | collective-permute-start | bytes 1179656 | tf_op jit(solution)/shard_map/ppermute | solution.py:416
  36.4 4.2 %collective-permute-start = (f32[7,4,8,128]{3,2,1,0:T(8,128)S(1)}, f32[7,4,8,128]{3,2,1,0:T(8,128)S(1)}, u32[]{:S(2)}, u32[]{:S(2)}) collective-permute-start(f32[7,4,8,128]{3,2,1,0:T(8,128)S(1)} %get-tuple-element.33), channel_id=1, source_target_pairs={{0,16},{16,32},{32,48},{48,64},{64,80},{80,96},{96,112},{112,0},{1... | collective-permute-start | bytes 344072 | tf_op jit(solution)/shard_map/ppermute | solution.py:421
  36.4 4.2 %collective-permute-start.1 = (f32[7,4,8,128]{3,2,1,0:T(8,128)S(1)}, f32[7,4,8,128]{3,2,1,0:T(8,128)S(1)}, u32[]{:S(2)}, u32[]{:S(2)}) collective-permute-start(f32[7,4,8,128]{3,2,1,0:T(8,128)S(1)} %get-tuple-element.34), channel_id=1, source_target_pairs={{0,112},{16,0},{32,16},{48,32},{64,48},{80,64},{96,80},{112,96},{1... | collective-permute-start | bytes 344072 | tf_op jit(solution)/shard_map/ppermute | solution.py:422
  40.7 7.3 %collective-permute-start.4 = (f32[30,8,128]{2,1,0:T(8,128)S(1)}, f32[30,8,128]{2,1,0:T(8,128)S(1)}, u32[]{:S(2)}, u32[]{:S(2)}) collective-permute-start(f32[30,8,128]{2,1,0:T(8,128)S(1)} %get-tuple-element.37), channel_id=1, source_target_pairs={{0,128},{128,0},{256,384},{384,256},{1,129},{129,1},{257,385},{385... | collective-permute-start | bytes 368648 | tf_op jit(solution)/shard_map/ppermute | solution.py:417
  42.6 10.3 %collective-permute-start.5 = (f32[30,8,128]{2,1,0:T(8,128)S(1)}, f32[30,8,128]{2,1,0:T(8,128)S(1)}, u32[]{:S(2)}, u32[]{:S(2)}) collective-permute-start(f32[30,8,128]{2,1,0:T(8,128)S(1)} %get-tuple-element.38), channel_id=1, source_target_pairs={{0,399},{128,256},{256,128},{384,1},{1,384},{129,257},{257,129},{3... | collective-permute-start | bytes 368648 | tf_op jit(solution)/shard_map/ppermute | solution.py:416
  54.8 17.7 %collective-permute-start.6 = (f32[140,8,128]{2,1,0:T(8,128)S(1)}, f32[140,8,128]{2,1,0:T(8,128)S(1)}, u32[]{:S(2)}, u32[]{:S(2)}) collective-permute-start(f32[140,8,128]{2,1,0:T(8,128)S(1)} %get-tuple-element.40), channel_id=1, source_target_pairs={{0,128},{128,0},{256,384},{384,256},{1,129},{129,1},{257,385},{385... | collective-permute-start | bytes 1720328 | tf_op jit(solution)/shard_map/ppermute | solution.py:417
  56.7 21.0 %collective-permute-start.7 = (f32[140,8,128]{2,1,0:T(8,128)S(1)}, f32[140,8,128]{2,1,0:T(8,128)S(1)}, u32[]{:S(2)}, u32[]{:S(2)}) collective-permute-start(f32[140,8,128]{2,1,0:T(8,128)S(1)} %get-tuple-element.41), channel_id=1, source_target_pairs={{0,399},{128,256},{256,128},{384,1},{1,384},{129,257},{257,129},{3... | collective-permute-start | bytes 1720328 | tf_op jit(solution)/shard_map/ppermute | solution.py:416
  80.1 22.4 %collective-permute-start.8 = (f32[32,4,8,128]{3,2,1,0:T(8,128)S(1)}, f32[32,4,8,128]{3,2,1,0:T(8,128)S(1)}, u32[]{:S(2)}, u32[]{:S(2)}) collective-permute-start(f32[32,4,8,128]{3,2,1,0:T(8,128)S(1)} %get-tuple-element.44.own), channel_id=1, source_target_pairs={{0,128},{128,0},{256,384},{384,256},{1,129},{129,1},{257,385},{385... | collective-permute-start | bytes 1572872 | tf_op jit(solution)/shard_map/ppermute | solution.py:417
  82.0 20.5 %collective-permute-start.9 = (f32[32,4,8,128]{3,2,1,0:T(8,128)S(1)}, f32[32,4,8,128]{3,2,1,0:T(8,128)S(1)}, u32[]{:S(2)}, u32[]{:S(2)}) collective-permute-start(f32[32,4,8,128]{3,2,1,0:T(8,128)S(1)} %get-tuple-element.44.own), channel_id=1, source_target_pairs={{0,399},{128,256},{256,128},{384,1},{1,384},{129,257},{257,129},{3... | collective-permute-start | bytes 1572872 | tf_op jit(solution)/shard_map/ppermute | solution.py:416
  102.6 6.3 %collective-permute-start.10 = (f32[76,8,128]{2,1,0:T(8,128)S(1)}, f32[76,8,128]{2,1,0:T(8,128)S(1)}, u32[]{:S(2)}, u32[]{:S(2)}) collective-permute-start(f32[76,8,128]{2,1,0:T(8,128)S(1)} %get-tuple-element.46), channel_id=1, source_target_pairs={{0,16},{16,32},{32,48},{48,64},{64,80},{80,96},{96,112},{112,0},{1... | collective-permute-start | bytes 933896 | tf_op jit(solution)/shard_map/ppermute | solution.py:421
  102.7 6.2 %collective-permute-start.11 = (f32[76,8,128]{2,1,0:T(8,128)S(1)}, f32[76,8,128]{2,1,0:T(8,128)S(1)}, u32[]{:S(2)}, u32[]{:S(2)}) collective-permute-start(f32[76,8,128]{2,1,0:T(8,128)S(1)} %get-tuple-element.47), channel_id=1, source_target_pairs={{0,112},{16,0},{32,16},{48,32},{64,48},{80,64},{96,80},{112,96},{1... | collective-permute-start | bytes 933896 | tf_op jit(solution)/shard_map/ppermute | solution.py:422
  108.9 34.8 %copy-start.1 = (f32[4,4]{1,0:T(4,128)S(1)}, f32[4,4]{1,0:T(4,128)}, u32[]{:S(2)}) copy-start(f32[4,4]{1,0:T(4,128)} %chi.3) | copy-start | bytes 196
  111.6 32.1 %collective-permute-start.12 = (f32[140,8,128]{2,1,0:T(8,128)S(1)}, f32[140,8,128]{2,1,0:T(8,128)S(1)}, u32[]{:S(2)}, u32[]{:S(2)}) collective-permute-start(f32[140,8,128]{2,1,0:T(8,128)S(1)} %get-tuple-element.54), channel_id=1, source_target_pairs={{0,128},{128,0},{256,384},{384,256},{1,129},{129,1},{257,385},{385... | collective-permute-start | bytes 1720328 | tf_op jit(solution)/shard_map/ppermute | solution.py:417
  113.5 30.2 %collective-permute-start.13 = (f32[140,8,128]{2,1,0:T(8,128)S(1)}, f32[140,8,128]{2,1,0:T(8,128)S(1)}, u32[]{:S(2)}, u32[]{:S(2)}) collective-permute-start(f32[140,8,128]{2,1,0:T(8,128)S(1)} %get-tuple-element.55), channel_id=1, source_target_pairs={{0,399},{128,256},{256,128},{384,1},{1,384},{129,257},{257,129},{3... | collective-permute-start | bytes 1720328 | tf_op jit(solution)/shard_map/ppermute | solution.py:416
  118.4 11.1 %collective-permute-start.14 = (f32[8,128]{1,0:T(8,128)S(1)}, f32[8,128]{1,0:T(8,128)S(1)}, u32[]{:S(2)}, u32[]{:S(2)}) collective-permute-start(f32[8,128]{1,0:T(8,128)S(1)} %get-tuple-element.52.total), channel_id=1, source_target_pairs={{0,1},{1,0},{2,3},{3,2},{4,5},{5,4},{6,7},{7,6},{8,9},{9,8},{10,11... | collective-permute-start | bytes 12296 | tf_op jit(solution)/shard_map/ppermute | solution.py:432
  129.5 14.2 %collective-permute-start.15 = (f32[8,128]{1,0:T(8,128)S(1)}, f32[8,128]{1,0:T(8,128)S(1)}, u32[]{:S(2)}, u32[]{:S(2)}) collective-permute-start(f32[8,128]{1,0:T(8,128)S(1)} %add.6), channel_id=1, source_target_pairs={{0,2},{1,3},{2,0},{3,1},{4,6},{5,7},{6,4},{7,5},{8,10},{9,11},{10,... | collective-permute-start | bytes 12296 | tf_op jit(solution)/shard_map/ppermute | solution.py:432
  147.0 28.8 %copy-start = (f32[1,32,16,256]{3,2,1,0:T(8,128)S(1)}, f32[1,32,16,256]{3,2,1,0:T(8,128)}, u32[]{:S(2)}) copy-start(f32[1,32,16,256]{3,2,1,0:T(8,128)} %param.2) | copy-start | bytes 1572868
